TPU v7x, 128 devices: a whole 4x4x4 slice. The times are simulated.
128 devices in a mesh: ctx: 32 (over y, z, x_lo), seq: 2 (over core), fsdp: 2 (over x_hi).
Axes of the slice: x: 4 (x_hi: 2, x_lo: 2; x = x_hi * 2 + x_lo), y: 4, z: 4, core: 2. Of those that a mesh axis runs over, the one named last changes fastest.
Arguments:
- tokens: bfloat16 [4, 4096, 768], P(('seq', 'fsdp'), 'ctx'), may hold values from -6 to 6
- cotangent: bfloat16 [4, 4096, 768], P(('seq', 'fsdp'), 'ctx'), may hold values from -6 to 6
- w_query: bfloat16 [768, 768], P('fsdp'), may hold values from -0.21875 to 0.21875
- w_key: bfloat16 [768, 768], P('fsdp'), may hold values from -0.21875 to 0.21875
- w_value: bfloat16 [768, 768], P('fsdp'), may hold values from -0.21875 to 0.21875
- w_output: bfloat16 [768, 768], P('fsdp'), may hold values from -6 to 6
- b_query: bfloat16 [768], P('fsdp'), may hold values from -1.5 to 1.5
- b_value: bfloat16 [768], P('fsdp'), may hold values from -0.15625 to 0.15625
- b_output: bfloat16 [768], P('fsdp'), may hold values from -1.5 to 1.5
- first_gain: bfloat16 [768], P('fsdp'), may hold values from 0.5 to 1.5
- first_shift: bfloat16 [768], P('fsdp'), may hold values from -1.5 to 1.5
- w_inner: bfloat16 [768, 3072], P('fsdp'), may hold values from -0.21875 to 0.21875
- b_inner: bfloat16 [3072], P('fsdp'), may hold values from -1.5 to 1.5
- w_outer: bfloat16 [3072, 768], P('fsdp'), may hold values from -0.109375 to 0.109375
- b_outer: bfloat16 [768], P('fsdp'), may hold values from -1.5 to 1.5
- second_gain: bfloat16 [768], P('fsdp'), may hold values from 0.5 to 1.5
- second_shift: bfloat16 [768], P('fsdp'), may hold values from -1.5 to 1.5
Outputs:
- layer_out: bfloat16 [4, 4096, 768], P(('seq', 'fsdp'), 'ctx')
- tokens_grad: float32 [4, 4096, 768], P(('seq', 'fsdp'), 'ctx')
- w_query_grad: float32 [768, 768], P('fsdp')
- w_key_grad: float32 [768, 768], P('fsdp')
- w_value_grad: float32 [768, 768], P('fsdp')
- w_output_grad: float32 [768, 768], P('fsdp')
- b_query_grad: float32 [768], P('fsdp')
- b_value_grad: float32 [768], P('fsdp')
- b_output_grad: float32 [768], P('fsdp')
- first_gain_grad: float32 [768], P('fsdp')
- first_shift_grad: float32 [768], P('fsdp')
- w_inner_grad: float32 [768, 3072], P('fsdp')
- b_inner_grad: float32 [3072], P('fsdp')
- w_outer_grad: float32 [3072, 768], P('fsdp')
- b_outer_grad: float32 [768], P('fsdp')
- second_gain_grad: float32 [768], P('fsdp')
- second_shift_grad: float32 [768], P('fsdp')
All inputs are finite; a program needn't handle non-finite values.
Results may differ from a plain program's by a relative error of at most 0.022.
Values may be sent and summed in bfloat16 or wider, within the bound.
A program may use at most 192 MiB of HBM per device.

v0:
```python
import functools

import jax
import jax.numpy as jnp
from jax import lax
from jax.sharding import PartitionSpec as P

HEADS = 12
HEAD_DIM = 64


epsilon = 1e-12


def product(left, right):
    return jnp.dot(left, right, preferred_element_type=jnp.float32)


def product_left(left, right):
    return lax.dot_general(
        left, right, (((0,), (0,)), ((), ())), preferred_element_type=jnp.float32
    )


def product_right(left, right):
    return lax.dot_general(
        left, right, (((1,), (1,)), ((), ())), preferred_element_type=jnp.float32
    )


def layer_norm(hidden, gain, shift):
    centred = hidden - jnp.mean(hidden, axis=-1, keepdims=True)
    inverse = lax.rsqrt(jnp.mean(centred * centred, axis=-1, keepdims=True) + epsilon)
    normal = centred * inverse
    return (normal * gain + shift, normal, inverse)


def norm_back(grad, normal, inverse, gain):
    scaled = grad * gain
    centre = jnp.mean(scaled, axis=-1, keepdims=True)
    along = jnp.mean(scaled * normal, axis=-1, keepdims=True)
    return inverse * (scaled - centre - normal * along)


def group_slice(array, index):
    columns = 2 * HEAD_DIM
    piece = lax.dynamic_slice_in_dim(array, index * columns, columns, 2)
    return piece.reshape(piece.shape[0], piece.shape[1], 2, HEAD_DIM)


def scores_of(query, keys):
    return jnp.einsum(
        "sqhd,skhd->shqk", query, keys, preferred_element_type=jnp.float32
    ) * HEAD_DIM ** (-0.5)


def flatten_group(array):
    return array.reshape(array.shape[0], array.shape[1], 2 * HEAD_DIM)


def to_rows(stacked):
    groups, seqs, count, columns = stacked.shape
    return stacked.transpose(1, 2, 0, 3).reshape(seqs * count, groups * columns)


def local(
    tokens,
    cotangent,
    w_query,
    w_key,
    w_value,
    w_output,
    b_query,
    b_value,
    b_output,
    first_gain,
    first_shift,
    w_inner,
    b_inner,
    w_outer,
    b_outer,
    second_gain,
    second_shift,
):
    seqs, block, width = tokens.shape
    rows = seqs * block
    indices = jnp.arange(HEADS // 2)
    scale = HEAD_DIM ** (-0.5)
    w_query, w_key, w_value, w_output, b_query, b_value, b_output, first_gain, first_shift = (
        lax.all_gather(w_query, "fsdp", axis=0, tiled=True),
        lax.all_gather(w_key, "fsdp", axis=0, tiled=True),
        lax.all_gather(w_value, "fsdp", axis=0, tiled=True),
        lax.all_gather(w_output, "fsdp", axis=0, tiled=True),
        lax.all_gather(b_query, "fsdp", axis=0, tiled=True),
        lax.all_gather(b_value, "fsdp", axis=0, tiled=True),
        lax.all_gather(b_output, "fsdp", axis=0, tiled=True),
        lax.all_gather(first_gain, "fsdp", axis=0, tiled=True),
        lax.all_gather(first_shift, "fsdp", axis=0, tiled=True),
    )
    flat = tokens.reshape(rows, width)
    query = (product(flat, w_query) + b_query).astype(jnp.bfloat16).reshape(seqs, block, width)
    keys = product(flat, w_key).astype(jnp.bfloat16).reshape(seqs, block, width)
    values = (product(flat, w_value) + b_value).astype(jnp.bfloat16).reshape(seqs, block, width)
    keys_all, values_all = (
        lax.all_gather(keys, "ctx", axis=1, tiled=True),
        lax.all_gather(values, "ctx", axis=1, tiled=True),
    )

    def forward_group(index):
        scores = scores_of(group_slice(query, index), group_slice(keys_all, index))
        top = jnp.max(scores, axis=-1, keepdims=True)
        weights = jnp.exp(scores - top)
        total = jnp.sum(weights, axis=-1, keepdims=True)
        probs = (weights / total).astype(jnp.bfloat16)
        mixed = jnp.einsum(
            "shqk,skhd->sqhd",
            probs,
            group_slice(values_all, index),
            preferred_element_type=jnp.float32,
        )
        return (flatten_group(mixed), (top + jnp.log(total))[..., 0])

    mixed, logsum = lax.map(forward_group, indices)
    attended = to_rows(mixed).astype(jnp.bfloat16)
    first_in = flat.astype(jnp.float32) + product(attended, w_output) + b_output
    normed, first_normal, first_inverse = layer_norm(first_in, first_gain, first_shift)
    normed_low = normed.astype(jnp.bfloat16)
    w_inner, b_inner, w_outer, b_outer, second_gain, second_shift = (
        lax.all_gather(w_inner, "fsdp", axis=0, tiled=True),
        lax.all_gather(b_inner, "fsdp", axis=0, tiled=True),
        lax.all_gather(w_outer, "fsdp", axis=0, tiled=True),
        lax.all_gather(b_outer, "fsdp", axis=0, tiled=True),
        lax.all_gather(second_gain, "fsdp", axis=0, tiled=True),
        lax.all_gather(second_shift, "fsdp", axis=0, tiled=True),
    )
    gelu_exact = functools.partial(jax.nn.gelu, approximate=False)
    inner = product(normed_low, w_inner) + b_inner
    active = gelu_exact(inner).astype(jnp.bfloat16)
    second_in = normed + product(active, w_outer) + b_outer
    layer_out, second_normal, second_inverse = layer_norm(second_in, second_gain, second_shift)
    grad_out = cotangent.reshape(rows, width).astype(jnp.float32)
    second_scale = jnp.sum(grad_out * second_normal, axis=0)
    second_offset = jnp.sum(grad_out, axis=0)
    grad_second = norm_back(grad_out, second_normal, second_inverse, second_gain)
    outer_low = grad_second.astype(jnp.bfloat16)
    outer_matrix = product_left(active, outer_low)
    outer_bias = jnp.sum(outer_low.astype(jnp.float32), axis=0)
    slope = jax.vjp(gelu_exact, inner)[1](product_right(outer_low, w_outer))[0]
    inner_low = slope.astype(jnp.bfloat16)
    inner_matrix = product_left(normed_low, inner_low)
    inner_bias = jnp.sum(inner_low.astype(jnp.float32), axis=0)
    grad_normed = grad_second + product_right(inner_low, w_inner)
    first_scale = jnp.sum(grad_normed * first_normal, axis=0)
    first_offset = jnp.sum(grad_normed, axis=0)
    grad_first = norm_back(grad_normed, first_normal, first_inverse, first_gain)
    branch_low = grad_first.astype(jnp.bfloat16)
    output_matrix = product_left(attended, branch_low)
    output_bias = jnp.sum(branch_low.astype(jnp.float32), axis=0)
    upstream = product_right(branch_low, w_output).astype(jnp.bfloat16).reshape(seqs, block, width)

    def backward_group(pair):
        index, group_logsum = pair
        query_part = group_slice(query, index)
        keys_part = group_slice(keys_all, index)
        values_part = group_slice(values_all, index)
        upstream_part = group_slice(upstream, index)
        probs = jnp.exp(scores_of(query_part, keys_part) - group_logsum[..., None])
        prob_grads = jnp.einsum(
            "sqhd,skhd->shqk", upstream_part, values_part, preferred_element_type=jnp.float32
        )
        row_dot = jnp.sum(probs * prob_grads, axis=-1, keepdims=True)
        score_low = (probs * (prob_grads - row_dot)).astype(jnp.bfloat16)
        query_grad = (
            jnp.einsum("shqk,skhd->sqhd", score_low, keys_part, preferred_element_type=jnp.float32)
            * scale
        )
        key_grad = (
            jnp.einsum("shqk,sqhd->skhd", score_low, query_part, preferred_element_type=jnp.float32)
            * scale
        )
        value_grad = jnp.einsum(
            "shqk,sqhd->skhd",
            probs.astype(jnp.bfloat16),
            upstream_part,
            preferred_element_type=jnp.float32,
        )
        return (flatten_group(query_grad), flatten_group(key_grad), flatten_group(value_grad))

    query_grads, key_terms, value_terms = lax.map(backward_group, (indices, logsum))
    key_grads, value_grads = (
        lax.psum_scatter(
            key_terms.astype(jnp.bfloat16), "ctx", scatter_dimension=2, tiled=True
        ).astype(jnp.float32),
        lax.psum_scatter(
            value_terms.astype(jnp.bfloat16), "ctx", scatter_dimension=2, tiled=True
        ).astype(jnp.float32),
    )
    query_low = to_rows(query_grads).astype(jnp.bfloat16)
    key_low = to_rows(key_grads).astype(jnp.bfloat16)
    value_low = to_rows(value_grads).astype(jnp.bfloat16)
    query_matrix = product_left(flat, query_low)
    query_bias = jnp.sum(query_low.astype(jnp.float32), axis=0)
    keys_matrix = product_left(flat, key_low)
    value_matrix = product_left(flat, value_low)
    value_bias = jnp.sum(value_low.astype(jnp.float32), axis=0)
    tokens_grad = (
        grad_first
        + product_right(query_low, w_query)
        + product_right(key_low, w_key)
        + product_right(value_low, w_value)
    )
    (
        query_matrix,
        keys_matrix,
        value_matrix,
        output_matrix,
        query_bias,
        value_bias,
        output_bias,
        first_scale,
        first_offset,
        inner_matrix,
        inner_bias,
        outer_matrix,
        outer_bias,
        second_scale,
        second_offset,
    ) = (
        lax.psum_scatter(
            query_matrix.astype(jnp.bfloat16), "fsdp", scatter_dimension=0, tiled=True
        ).astype(jnp.float32),
        lax.psum_scatter(
            keys_matrix.astype(jnp.bfloat16), "fsdp", scatter_dimension=0, tiled=True
        ).astype(jnp.float32),
        lax.psum_scatter(
            value_matrix.astype(jnp.bfloat16), "fsdp", scatter_dimension=0, tiled=True
        ).astype(jnp.float32),
        lax.psum_scatter(
            output_matrix.astype(jnp.bfloat16), "fsdp", scatter_dimension=0, tiled=True
        ).astype(jnp.float32),
        lax.psum_scatter(
            query_bias.astype(jnp.bfloat16), "fsdp", scatter_dimension=0, tiled=True
        ).astype(jnp.float32),
        lax.psum_scatter(
            value_bias.astype(jnp.bfloat16), "fsdp", scatter_dimension=0, tiled=True
        ).astype(jnp.float32),
        lax.psum_scatter(
            output_bias.astype(jnp.bfloat16), "fsdp", scatter_dimension=0, tiled=True
        ).astype(jnp.float32),
        lax.psum_scatter(
            first_scale.astype(jnp.bfloat16), "fsdp", scatter_dimension=0, tiled=True
        ).astype(jnp.float32),
        lax.psum_scatter(
            first_offset.astype(jnp.bfloat16), "fsdp", scatter_dimension=0, tiled=True
        ).astype(jnp.float32),
        lax.psum_scatter(
            inner_matrix.astype(jnp.bfloat16), "fsdp", scatter_dimension=0, tiled=True
        ).astype(jnp.float32),
        lax.psum_scatter(
            inner_bias.astype(jnp.bfloat16), "fsdp", scatter_dimension=0, tiled=True
        ).astype(jnp.float32),
        lax.psum_scatter(
            outer_matrix.astype(jnp.bfloat16), "fsdp", scatter_dimension=0, tiled=True
        ).astype(jnp.float32),
        lax.psum_scatter(
            outer_bias.astype(jnp.bfloat16), "fsdp", scatter_dimension=0, tiled=True
        ).astype(jnp.float32),
        lax.psum_scatter(
            second_scale.astype(jnp.bfloat16), "fsdp", scatter_dimension=0, tiled=True
        ).astype(jnp.float32),
        lax.psum_scatter(
            second_offset.astype(jnp.bfloat16), "fsdp", scatter_dimension=0, tiled=True
        ).astype(jnp.float32),
    )
    finals = lax.psum(
        (
            query_matrix,
            keys_matrix,
            value_matrix,
            output_matrix,
            query_bias,
            value_bias,
            output_bias,
            first_scale,
            first_offset,
            inner_matrix,
            inner_bias,
            outer_matrix,
            outer_bias,
            second_scale,
            second_offset,
        ),
        ("ctx", "seq"),
    )
    return (
        layer_out.astype(jnp.bfloat16).reshape(seqs, block, width),
        tokens_grad.reshape(seqs, block, width),
    ) + tuple(finals)


def solution(mesh):
    return jax.shard_map(
        local,
        mesh=mesh,
        in_specs=(
            P(("seq", "fsdp"), "ctx", None),
            P(("seq", "fsdp"), "ctx", None),
            P("fsdp", None),
            P("fsdp", None),
            P("fsdp", None),
            P("fsdp", None),
            P("fsdp"),
            P("fsdp"),
            P("fsdp"),
            P("fsdp"),
            P("fsdp"),
            P("fsdp", None),
            P("fsdp"),
            P("fsdp", None),
            P("fsdp"),
            P("fsdp"),
            P("fsdp"),
        ),
        out_specs=(
            P(("seq", "fsdp"), "ctx", None),
            P(("seq", "fsdp"), "ctx", None),
            P("fsdp", None),
            P("fsdp", None),
            P("fsdp", None),
            P("fsdp", None),
            P("fsdp"),
            P("fsdp"),
            P("fsdp"),
            P("fsdp"),
            P("fsdp"),
            P("fsdp", None),
            P("fsdp"),
            P("fsdp", None),
            P("fsdp"),
            P("fsdp"),
            P("fsdp"),
        ),
        check_vma=False,
    )
```

profile of v0, /device:TPU:1, one launch (start us, length us, event | category | flops | bytes accessed | tf_op | source)
XLA Modules:
  0.0 1808.1 jit_solution(1213545254661435694)
XLA Ops:
  9.5 5.3 all-gather.2
  14.8 24.9 %all-gather.20.cloned.1.call-done = bf16[768,768]{1,0:T(8,128)(2,1)} async-done(((bf16[384,768]{1,0:T(8,128)(2,1)}), bf16[768,768]{1,0:T(8,128)(2,1)}) %all-gather.20.cloned.1.call-update) | async-done | bytes 1179664 | tf_op jit(solution)/shard_map/all_gather | solution.py:92
  42.1 25.6 %all-gather.24.cloned.1.call-done = bf16[768,768]{1,0:T(8,128)(2,1)} async-done(((bf16[384,768]{1,0:T(8,128)(2,1)}), bf16[768,768]{1,0:T(8,128)(2,1)}) %all-gather.24.cloned.1.call-update) | async-done | bytes 1179664 | tf_op jit(solution)/shard_map/all_gather | solution.py:91
  77.0 4.7 all-gather.7
  81.7 5.0 all-gather.4
  86.8 5.0 all-gather.3
  91.9 4.7 all-gather.6
  106.1 4.7 all-gather.10
  112.6 141.1 %all-gather.32.cloned.1.call-done = bf16[4096,768]{1,0:T(8,128)(2,1)} async-done(((bf16[128,768]{1,0:T(8,128)(2,1)}), bf16[4096,768]{1,0:T(8,128)(2,1)}) %all-gather.32.cloned.1.call-update) | async-done | bytes 6291472 | tf_op jit(solution)/shard_map/all_gather | solution.py:106
  253.7 8.7 copy.44
  262.4 166.1 %all-gather.34.cloned.1.call-done = bf16[4096,768]{1,0:T(8,128)(2,1)} async-done(((bf16[128,768]{1,0:T(8,128)(2,1)}), bf16[4096,768]{1,0:T(8,128)(2,1)}) %all-gather.34.cloned.1.call-update) | async-done | bytes 6291472 | tf_op jit(solution)/shard_map/all_gather | solution.py:105
  428.5 8.6 copy.46
  437.1 33.5 %while.26 = (s32[]{:T(128)}, bf16[6,1,128,128]{2,3,1,0:T(8,128)(2,1)S(1)}, f32[6,1,2,128]{3,2,1,0:T(2,128)S(1)}, s32[6]{0:T(128)S(1)}, bf16[1,4096,768]{1,2,0:T(...) while((s32[]{:T(128)}, ...), condition=%wide.region_3.4_spmd, body=%wide.region_0.3_spmd.sunk | while | flops 275775232 | bytes 19079360 | solution.py:123
  474.8 66.0 %all-gather.28.cloned.1.call-done = bf16[768,3072]{1,0:T(8,128)(2,1)} async-done(((bf16[384,3072]{1,0:T(8,128)(2,1)}), bf16[768,3072]{1,0:T(8,128)(2,1)}) %all-gather.28.cloned.1.call-update) | async-done | bytes 4718608 | tf_op jit(solution)/shard_map/all_gather | solution.py:129
  540.8 8.4 multiply_convert_fusion.1
  549.1 59.5 %all-gather.30.cloned.1.call-done = bf16[3072,768]{1,0:T(8,128)(2,1)} async-done(((bf16[1536,768]{1,0:T(8,128)(2,1)}), bf16[3072,768]{1,0:T(8,128)(2,1)}) %all-gather.30.cloned.1.call-update) | async-done | bytes 4718608 | tf_op jit(solution)/shard_map/all_gather | solution.py:131
  619.9 71.8 %while.27 = (s32[]{:T(128)}, bf16[6,1,128,128]{2,3,1,0:T(8,128)(2,1)S(1)}, bf16[6,1,4096,128]{2,3,1,0:T(8,128)(2,1)}, bf16[6,1,4096,128]{2,3,1,0:T(8,128)(2,1)},...) while((s32[]{:T(128)}, ...), condition=%wide.region_14.15_spmd, body=%wide.region_12.14_spmd.sunk | while | flops 680558336 | bytes 47093020 | solution.py:189
  691.7 27.8 %copy.54 = bf16[6,1,4096,128]{3,1,0,2:T(2,128)(2,1)} copy(bf16[6,1,4096,128]{2,3,1,0:T(8,128)(2,1)} %get-tuple-element.112) | data formatting | bytes 12582912
  719.5 110.4 %bitcast_reduce_fusion.1 = bf16[4096,6,128]{2,1,0:T(8,128)(2,1)} fusion(bf16[6,1,4096,128]{3,1,0,2:T(2,128)(2,1)} %copy.54), kind=kLoop, calls=%fused_computation.29 | loop fusion | bytes 12582912
  829.8 7.6 copy.172
  837.5 27.8 %copy.56 = bf16[6,1,4096,128]{3,1,0,2:T(2,128)(2,1)} copy(bf16[6,1,4096,128]{2,3,1,0:T(8,128)(2,1)} %get-tuple-element.113) | data formatting | bytes 12582912
  865.4 110.0 %bitcast_reduce_fusion = bf16[4096,6,128]{2,1,0:T(8,128)(2,1)} fusion(bf16[6,1,4096,128]{3,1,0,2:T(2,128)(2,1)} %copy.56), kind=kLoop, calls=%fused_computation.28 | loop fusion | bytes 12582912
  975.4 7.7 copy.171
  1000.9 175.9 %reduce-scatter.27.cloned.1.call-done = bf16[128,768]{1,0:T(8,128)(2,1)} async-done(((bf16[4096,768]{1,0:T(8,128)(2,1)}), bf16[128,768]{1,0:T(8,128)(2,1)}) %reduce-scatter.27.cloned.1.call-update) | async-done | bytes 196624
  1184.0 40.4 %reduce-scatter.29.cloned.1.call-done = bf16[384,768]{1,0:T(8,128)(2,1)} async-done(((bf16[768,768]{1,0:T(8,128)(2,1)}), bf16[384,768]{1,0:T(8,128)(2,1)}) %reduce-scatter.29.cloned.1.call-update) | async-done | bytes 589840
  1225.8 26.8 %reduce-scatter.19.cloned.1.call-done = bf16[384,768]{1,0:T(8,128)(2,1)} async-done(((bf16[768,768]{1,0:T(8,128)(2,1)}), bf16[384,768]{1,0:T(8,128)(2,1)}) %reduce-scatter.19.cloned.1.call-update) | async-done | bytes 589840 | tf_op jit(solution)/shard_map/reduce_scatter | solution.py:238
  1252.6 66.5 %reduce-scatter.21.cloned.1.call-done = bf16[384,3072]{1,0:T(8,128)(2,1)} async-done(((bf16[768,3072]{1,0:T(8,128)(2,1)}), bf16[384,3072]{1,0:T(8,128)(2,1)}) %reduce-scatter.21.cloned.1.call-update) | async-done | bytes 2359312 | tf_op jit(solution)/shard_map/reduce_scatter | solution.py:256
  1319.1 66.4 %reduce-scatter.23.cloned.1.call-done = bf16[1536,768]{1,0:T(8,128)(2,1)} async-done(((bf16[3072,768]{1,0:T(8,128)(2,1)}), bf16[1536,768]{1,0:T(8,128)(2,1)}) %reduce-scatter.23.cloned.1.call-update) | async-done | bytes 2359312 | tf_op jit(solution)/shard_map/reduce_scatter | solution.py:262
  1385.7 7.0 all-reduce.10
  1396.1 17.4 reduce-scatter.31.cloned.1.call-done
  1414.9 26.8 %reduce-scatter.33.cloned.1.call-done = bf16[384,768]{1,0:T(8,128)(2,1)} async-done(((bf16[768,768]{1,0:T(8,128)(2,1)}), bf16[384,768]{1,0:T(8,128)(2,1)}) %reduce-scatter.33.cloned.1.call-update) | async-done | bytes 589840
  1443.1 352.8 %all-reduce.12 = (f32[384,768]{0,1:T(8,128)}, f32[384,768]{0,1:T(8,128)}, f32[384,768]{0,1:T(8,128)S(1)}, f32[384,768]{1,0:T(8,128)}, f32[384]{0:T(512)}, /*inde...) all-reduce(bf16[384,768]{0,1:T(8,128)(2,1)S(1)} %copy.59, ...), channel_id=1, replica_groups=mesh['ctx'=32,'seq'=2,'fsdp'=2] {'ctx','seq'}, use_global_device_ids=true, to_apply=%region_18.19 | all-reduce | flops 3543552 | bytes 21270528 | tf_op jit(solution)/shard_map/psum | solution.py:275
  (351 shorter events, 173.7 us)
Async XLA Ops:
  7.2 32.5 %copy-start = (bf16[1,128,768]{2,1,0:T(8,128)(2,1)S(1)}, bf16[1,128,768]{2,1,0:T(8,128)(2,1)}, u32[]{:S(2)}) copy-start(bf16[1,128,768]{2,1,0:T(8,128)(2,1)} %param.21) | copy-start | bytes 589828
  7.2 32.5 %all-gather.20.cloned.1.call-start = ((), (), s32[]{:S(2)}) async-start(), calls=%async_computation.8 | async-start | bytes 1769472 | tf_op jit(solution)/shard_map/all_gather | solution.py:92
  7.9 59.7 %all-gather.24.cloned.1.call-start = ((), (), s32[]{:S(2)}) async-start(), calls=%async_computation.10 | async-start | bytes 1769472 | tf_op jit(solution)/shard_map/all_gather | solution.py:91
  8.7 102.2 %all-gather.22.cloned.1.call-start = ((), (), s32[]{:S(2)}) async-start(), calls=%async_computation.9 | async-start | bytes 1769472 | tf_op jit(solution)/shard_map/all_gather | solution.py:90
  9.4 244.3 %all-gather.32.cloned.1.call-start = ((), (), s32[]{:S(2)}) async-start(), calls=%async_computation.17 | async-start | bytes 6488064 | tf_op jit(solution)/shard_map/all_gather | solution.py:106
  42.0 386.5 %all-gather.34.cloned.1.call-start = ((), (), s32[]{:S(2)}) async-start(), calls=%async_computation.18 | async-start | bytes 6488064 | tf_op jit(solution)/shard_map/all_gather | solution.py:105
  70.0 402.9 %all-gather.26.cloned.1.call-start = ((), (), s32[]{:S(2)}) async-start(), calls=%async_computation.11 | async-start | bytes 1769472 | tf_op jit(solution)/shard_map/all_gather | solution.py:93
  70.6 470.2 %all-gather.28.cloned.1.call-start = ((), (), s32[]{:S(2)}) async-start(), calls=%async_computation.12 | async-start | bytes 7077888 | tf_op jit(solution)/shard_map/all_gather | solution.py:129
  71.3 5.7 copy-start.16
  71.3 10.4 copy-start.19
  71.3 15.5 copy-start.20
  71.3 20.5 %copy-start.21 = (bf16[384]{0:T(512)(128)(2,1)S(1)}, bf16[384]{0:T(512)(128)(2,1)}, u32[]{:S(2)}) copy-start(bf16[384]{0:T(512)(128)(2,1)} %param.31) | copy-start | bytes 2308
  71.4 25.2 %copy-start.22 = (bf16[384]{0:T(512)(128)(2,1)S(1)}, bf16[384]{0:T(512)(128)(2,1)}, u32[]{:S(2)}) copy-start(bf16[384]{0:T(512)(128)(2,1)} %param.30) | copy-start | bytes 2308
  71.4 30.0 %copy-start.23 = (bf16[384]{0:T(512)(128)(2,1)S(1)}, bf16[384]{0:T(512)(128)(2,1)}, u32[]{:S(2)}) copy-start(bf16[384]{0:T(512)(128)(2,1)} %param.36) | copy-start | bytes 2308
  71.4 34.7 %copy-start.24 = (bf16[384]{0:T(512)(128)(2,1)S(1)}, bf16[384]{0:T(512)(128)(2,1)}, u32[]{:S(2)}) copy-start(bf16[384]{0:T(512)(128)(2,1)} %param.37) | copy-start | bytes 2308
  71.4 537.2 %all-gather.30.cloned.1.call-start = ((), (), s32[]{:S(2)}) async-start(), calls=%async_computation.13 | async-start | bytes 7077888 | tf_op jit(solution)/shard_map/all_gather | solution.py:131
  72.1 925.0 %reduce-scatter.25.cloned.1.call-start = ((), (), s32[]{:S(2)}) async-start(), calls=%async_computation.19 | async-start | bytes 6488064
  470.6 78.5 %copy-start.7 = (bf16[6,1,128,128]{2,3,1,0:T(8,128)(2,1)}, bf16[6,1,128,128]{2,3,1,0:T(8,128)(2,1)S(1)}, u32[]{:S(2)}) copy-start(bf16[6,1,128,128]{2,3,1,0:T(8,128)(2,1)S(1)} %get-tuple-element.109) | copy-start | bytes 589828
  608.6 4.7 slice-start.2
  608.6 4.7 slice-start.3
  608.6 4.7 copy-start.27
  837.5 339.3 %reduce-scatter.27.cloned.1.call-start = ((), (), s32[]{:S(2)}) async-start(), calls=%async_computation.20 | async-start | bytes 6488064
  983.1 241.4 %reduce-scatter.29.cloned.1.call-start = ((), (), s32[]{:S(2)}) async-start(), calls=%async_computation.21 | async-start | bytes 1769472
  987.0 265.6 %reduce-scatter.19.cloned.1.call-start = ((), (), s32[]{:S(2)}) async-start(), calls=%async_computation.14 | async-start | bytes 1769472 | tf_op jit(solution)/shard_map/reduce_scatter | solution.py:238
  988.7 330.3 %reduce-scatter.21.cloned.1.call-start = ((), (), s32[]{:S(2)}) async-start(), calls=%async_computation.15 | async-start | bytes 7077888 | tf_op jit(solution)/shard_map/reduce_scatter | solution.py:256
  992.5 393.0 %reduce-scatter.23.cloned.1.call-start = ((), (), s32[]{:S(2)}) async-start(), calls=%async_computation.16 | async-start | bytes 7077888 | tf_op jit(solution)/shard_map/reduce_scatter | solution.py:262
  996.2 417.3 %reduce-scatter.31.cloned.1.call-start = ((), (), s32[]{:S(2)}) async-start(), calls=%async_computation.22 | async-start | bytes 1769472
  1000.9 440.9 %reduce-scatter.33.cloned.1.call-start = ((), (), s32[]{:S(2)}) async-start(), calls=%async_computation.23 | async-start | bytes 1769472
  1179.1 3.6 copy-start.3
  1182.7 210.6 %copy-start.2 = (bf16[768,768]{1,0:T(8,128)(2,1)S(1)}, bf16[768,768]{1,0:T(8,128)(2,1)}, u32[]{:S(2)}) copy-start(bf16[768,768]{1,0:T(8,128)(2,1)} %all-gather.24.cloned.1.call-done) | copy-start | bytes 3538948
  1184.0 209.3 %copy-start.10 = (bf16[6,1,128,128]{2,3,1,0:T(8,128)(2,1)S(1)}, bf16[6,1,128,128]{2,3,1,0:T(8,128)(2,1)}, u32[]{:S(2)}) copy-start(bf16[6,1,128,128]{2,3,1,0:T(8,128)(2,1)} %copy-done.9) | copy-start | bytes 589828
  1184.0 210.8 %copy-start.1 = (bf16[768,768]{1,0:T(8,128)(2,1)S(1)}, bf16[768,768]{1,0:T(8,128)(2,1)}, u32[]{:S(2)}) copy-start(bf16[768,768]{1,0:T(8,128)(2,1)} %all-gather.20.cloned.1.call-done) | copy-start | bytes 3538948
  (26 other events, 44.6 us)
Sparse Core Ops, SparseCore 0:
  9.7 29.9 all-gather.19
  41.4 26.2 all-gather.23
  69.3 26.3 all-gather.21
  97.8 155.8 all-gather.31
  255.8 172.7 all-gather.33
  430.0 42.7 all-gather.25
  474.5 66.2 all-gather.27
  542.4 66.1 all-gather.29
  837.6 159.4 reduce-scatter.24
  999.4 177.4 reduce-scatter.26
  1179.8 44.6 reduce-scatter.28
  1227.3 25.1 reduce-scatter.18
  1255.6 63.4 reduce-scatter.20
  1322.0 63.4 reduce-scatter.22
  1388.3 25.2 reduce-scatter.30
  1416.4 25.2 reduce-scatter.32
where the time goes:
time: 1820 us; the launch traced here: 1810 us
  waiting for transfers between devices  911 us (50%)
  blocking collectives  403 us (22%)
  local copies, waits for them, and re-layouts  382 us (21%)
  matrix products  74 us (4%)
    psum x1, blocking collectives, local(): lax.psum((query_matrix, keys_matrix, value_matrix, output_matrix, query_b...  353 us
    unnamed x89, local copies, waits for them, and re-layouts  312 us
    unnamed x21, waiting for transfers between devices  266 us
    all_gather x1, waiting for transfers between devices, local(): lax.all_gather(keys, 'ctx', axis=1, tiled=True)  166 us
    all_gather x1, waiting for transfers between devices, local(): lax.all_gather(values, 'ctx', axis=1, tiled=True)  141 us
    reduce_scatter x1, waiting for transfers between devices, local(): lax.psum_scatter(inner_matrix.astype(jnp.bfloat16), 'fsdp', scatter_dimen...  66.5 us
    reduce_scatter x1, waiting for transfers between devices, local(): lax.psum_scatter(outer_matrix.astype(jnp.bfloat16), 'fsdp', scatter_dimen...  66.4 us
    all_gather x1, waiting for transfers between devices, local(): lax.all_gather(w_inner, 'fsdp', axis=0, tiled=True)  66 us
  transfers between devices with their start and end apart: 16, of which 15 were waited for; matrix products, arithmetic and copies ran while one was open for 13% of the time, Pallas kernels for 0%

commit v1 on v0

v1 whole, which is shorter than its diff:
```python
import functools

import jax
import jax.numpy as jnp
from jax import lax
from jax.experimental import pallas as pl
from jax.experimental.pallas import tpu as pltpu
from jax.sharding import PartitionSpec as P

AXES = ("ctx", "seq", "fsdp")
MESH = pl.DeviceIdType.MESH
BF = jnp.bfloat16
F32 = jnp.float32
D = 768
FF = 3072
HALF = 384
GROUP = 192
HD = 64
ROWS = 128
EPS = 1e-12
LIMIT = 56 << 20
VM = pl.BlockSpec(memory_space=pltpu.VMEM)
ANY = pl.BlockSpec(memory_space=pl.ANY)


def shape(*dims, dtype=BF):
    return jax.ShapeDtypeStruct(dims, dtype)


def nn(left, right):
    return jnp.dot(left, right, preferred_element_type=F32)


def nt(left, right):
    return lax.dot_general(left, right, (((1,), (1,)), ((), ())), preferred_element_type=F32)


def tn(left, right):
    return lax.dot_general(left, right, (((0,), (0,)), ((), ())), preferred_element_type=F32)


def wrap(value, size):
    return lax.rem(value + size, size)


def place():
    ctx = lax.axis_index("ctx")
    y = lax.div(ctx, 8)
    z = lax.rem(lax.div(ctx, 2), 4)
    return y, z, lax.rem(ctx, 2), lax.axis_index("seq"), lax.axis_index("fsdp")


def device(y, z, xl, core, half):
    return ((y * 4 + z) * 2 + xl, core, half)


def send(src, dst, out_sem, in_sem, where):
    pltpu.make_async_remote_copy(
        src_ref=src, dst_ref=dst, send_sem=out_sem, recv_sem=in_sem,
        device_id=where, device_id_type=MESH,
    ).start()


def finish(src, dst, out_sem, in_sem, where):
    copy = pltpu.make_async_remote_copy(
        src_ref=src, dst_ref=dst, send_sem=out_sem, recv_sem=in_sem,
        device_id=where, device_id_type=MESH,
    )
    copy.wait_send()
    copy.wait_recv()


def greet(barrier, where):
    pl.semaphore_signal(barrier, inc=1, device_id=where, device_id_type=MESH)


def parts(k):
    return lax.div(k, 8), lax.rem(lax.div(k, 2), 4), lax.rem(k, 2)


def spread_kernel(q_ref, kv_ref, qo_ref, kvo_ref, local_sem, qs, qr, ks, kr):
    y, z, xl, core, half = place()
    me = lax.axis_index("ctx")
    barrier = pltpu.get_barrier_semaphore()

    def other(k):
        dy, dz, dx = parts(k)
        return wrap(y + dy, 4), wrap(z + dz, 4), wrap(xl + dx, 2)

    def source(k):
        dy, dz, dx = parts(k)
        return (wrap(y - dy, 4) * 4 + wrap(z - dz, 4)) * 2 + wrap(xl - dx, 2)

    def hello(k, carry):
        ey, ez, ex = other(k)
        greet(barrier, device(ey, ez, ex, core, half))
        return carry

    lax.fori_loop(1, 32, hello, 0)
    pl.semaphore_wait(barrier, 31)

    def push_q(k, carry):
        ez = wrap(z + k, 4)
        send(q_ref.at[ez], qo_ref.at[z], qs.at[k], qr.at[k], device(y, ez, xl, core, half))
        return carry

    def push(k, carry):
        ey, ez, ex = other(k)
        send(kv_ref.at[ez], kvo_ref.at[me], ks.at[k], kr.at[k], device(ey, ez, ex, core, half))
        return carry

    lax.fori_loop(1, 4, push_q, 0)
    lax.fori_loop(1, 32, push, 0)
    mine = pltpu.make_async_copy(kv_ref.at[z], kvo_ref.at[me], local_sem.at[0])
    mine.start()
    mine_q = pltpu.make_async_copy(q_ref.at[z], qo_ref.at[z], local_sem.at[1])
    mine_q.start()

    def done_q(k, carry):
        finish(q_ref.at[0], qo_ref.at[wrap(z - k, 4)], qs.at[k], qr.at[k], device(y, z, xl, core, half))
        return carry

    def done(k, carry):
        finish(kv_ref.at[0], kvo_ref.at[source(k)], ks.at[k], kr.at[k], device(y, z, xl, core, half))
        return carry

    lax.fori_loop(1, 4, done_q, 0)
    lax.fori_loop(1, 32, done, 0)
    mine.wait()
    mine_q.wait()


def collect_kernel(q_ref, kv_ref, qo_ref, kvo_ref, local_sem, qs, qr, ks, kr):
    y, z, xl, core, half = place()
    me = lax.axis_index("ctx")
    barrier = pltpu.get_barrier_semaphore()

    def other(k):
        dy, dz, dx = parts(k)
        return wrap(y + dy, 4), wrap(z + dz, 4), wrap(xl + dx, 2)

    def source(k):
        dy, dz, dx = parts(k)
        return (wrap(y - dy, 4) * 4 + wrap(z - dz, 4)) * 2 + wrap(xl - dx, 2)

    def hello(k, carry):
        ey, ez, ex = other(k)
        greet(barrier, device(ey, ez, ex, core, half))
        return carry

    lax.fori_loop(1, 32, hello, 0)
    pl.semaphore_wait(barrier, 31)

    def push_q(k, carry):
        ez = wrap(z + k, 4)
        send(q_ref.at[ez], qo_ref.at[z], qs.at[k], qr.at[k], device(y, ez, xl, core, half))
        return carry

    def push(k, carry):
        ey, ez, ex = other(k)
        to = (ey * 4 + ez) * 2 + ex
        send(kv_ref.at[to], kvo_ref.at[me], ks.at[k], kr.at[k], device(ey, ez, ex, core, half))
        return carry

    lax.fori_loop(1, 4, push_q, 0)
    lax.fori_loop(1, 32, push, 0)
    mine = pltpu.make_async_copy(kv_ref.at[me], kvo_ref.at[me], local_sem.at[0])
    mine.start()
    mine_q = pltpu.make_async_copy(q_ref.at[z], qo_ref.at[z], local_sem.at[1])
    mine_q.start()

    def done_q(k, carry):
        finish(q_ref.at[0], qo_ref.at[wrap(z - k, 4)], qs.at[k], qr.at[k], device(y, z, xl, core, half))
        return carry

    def done(k, carry):
        finish(kv_ref.at[0], kvo_ref.at[source(k)], ks.at[k], kr.at[k], device(y, z, xl, core, half))
        return carry

    lax.fori_loop(1, 4, done_q, 0)
    lax.fori_loop(1, 32, done, 0)
    mine.wait()
    mine_q.wait()


def mates_kernel(q_ref, qo_ref, local_sem, qs, qr):
    y, z, xl, core, half = place()
    barrier = pltpu.get_barrier_semaphore()

    def hello(k, carry):
        greet(barrier, device(y, wrap(z + k, 4), xl, core, half))
        return carry

    lax.fori_loop(1, 4, hello, 0)
    pl.semaphore_wait(barrier, 3)

    def push(k, carry):
        ez = wrap(z + k, 4)
        send(q_ref.at[ez], qo_ref.at[z], qs.at[k], qr.at[k], device(y, ez, xl, core, half))
        return carry

    lax.fori_loop(1, 4, push, 0)
    mine = pltpu.make_async_copy(q_ref.at[z], qo_ref.at[z], local_sem)
    mine.start()

    def done(k, carry):
        finish(q_ref.at[0], qo_ref.at[wrap(z - k, 4)], qs.at[k], qr.at[k], device(y, z, xl, core, half))
        return carry

    lax.fori_loop(1, 4, done, 0)
    mine.wait()


def exchange(kernel, name, number, pieces, blocks):
    dma = pltpu.SemaphoreType.DMA
    return pl.pallas_call(
        kernel,
        name=name,
        out_shape=(shape(4, ROWS, 256), shape(32, ROWS, HALF)),
        in_specs=[VM, VM],
        out_specs=(VM, VM),
        scratch_shapes=[dma((2,)), dma((4,)), dma((4,)), dma((32,)), dma((32,))],
        compiler_params=pltpu.CompilerParams(
            collective_id=number, has_side_effects=True, vmem_limit_bytes=LIMIT
        ),
    )(pieces, blocks)


def mates(name, number, pieces):
    dma = pltpu.SemaphoreType.DMA
    return pl.pallas_call(
        mates_kernel,
        name=name,
        out_shape=shape(4, ROWS, 256),
        in_specs=[VM],
        out_specs=VM,
        scratch_shapes=[dma, dma((4,)), dma((4,))],
        compiler_params=pltpu.CompilerParams(
            collective_id=number, has_side_effects=True, vmem_limit_bytes=LIMIT
        ),
    )(pieces)


def project_kernel(x_ref, wq, wk, wv, ra, rb, bias_ref, q_ref, kv_ref, w_ref, sems):
    core = lax.axis_index("seq")
    half = lax.axis_index("fsdp")
    own = pl.multiple_of(half * HALF, HALF)
    first = pl.multiple_of((1 - half) * HALF + core * GROUP, GROUP)
    second = pl.multiple_of((1 - half) * HALF + (1 - core) * GROUP, GROUP)
    copies = []
    for i, w in enumerate((wq, wk, wv)):
        copies.append(pltpu.make_async_copy(w, w_ref.at[i, pl.ds(own, HALF)], sems.at[i]))
    for i in range(3):
        copies.append(pltpu.make_async_copy(ra.at[i], w_ref.at[i, pl.ds(first, GROUP)], sems.at[3 + i]))
        copies.append(pltpu.make_async_copy(rb.at[i], w_ref.at[i, pl.ds(second, GROUP)], sems.at[6 + i]))
    for copy in copies:
        copy.start()
    for copy in copies:
        copy.wait()
    x = x_ref[...]
    pad = jnp.zeros((ROWS, 64), BF)
    query = (nn(x, w_ref[0]) + bias_ref[0:1, :]).astype(BF) * BF(0.125)
    for g in range(4):
        q_ref[g] = jnp.concatenate([query[:, g * GROUP : (g + 1) * GROUP], pad], axis=1)
    keys = nn(x, w_ref[1]).astype(BF)
    values = (nn(x, w_ref[2]) + bias_ref[1:2, :]).astype(BF)
    for g in range(4):
        cut = slice(g * GROUP, (g + 1) * GROUP)
        kv_ref[g] = jnp.concatenate([keys[:, cut], values[:, cut]], axis=1)


def project(x, wq, wk, wv, ra, rb, bias):
    return pl.pallas_call(
        project_kernel,
        name="project",
        out_shape=(shape(4, ROWS, 256), shape(4, ROWS, HALF), shape(3, D, D)),
        in_specs=[VM, ANY, ANY, ANY, ANY, ANY, VM],
        out_specs=(VM, VM, VM),
        scratch_shapes=[pltpu.SemaphoreType.DMA((9,))],
        compiler_params=pltpu.CompilerParams(vmem_limit_bytes=LIMIT),
    )(x, wq, wk, wv, ra, rb, bias)


CHUNK = 256


def load_chunk(ref, i):
    n = CHUNK // ROWS
    return ref[pl.ds(i * n, n)].reshape(CHUNK, HALF)


def stack_head(ref, h):
    return jnp.concatenate([ref[i][:, h * HD : (h + 1) * HD] for i in range(4)], axis=0)


def turned(rows):
    return rows.astype(F32).T.astype(BF)


def attend_kernel(q_ref, kv_ref, o_ref, ot_ref, lse_ref, qt, top, total):
    for h in range(3):
        qt[h] = turned(stack_head(q_ref, h))
    top[...] = jnp.full_like(top, -jnp.inf)
    total[...] = jnp.zeros_like(total)
    ot_ref[...] = jnp.zeros_like(ot_ref)

    def body(i, carry):
        kv = load_chunk(kv_ref, i)
        for h in range(3):
            scores = nn(kv[:, h * HD : (h + 1) * HD], qt[h])
            old = top[h]
            new = jnp.maximum(old, jnp.max(scores, axis=0, keepdims=True))
            shrink = jnp.exp(old - new)
            weights = jnp.exp(scores - new)
            total[h] = total[h] * shrink + jnp.sum(weights, axis=0, keepdims=True)
            mixed = tn(kv[:, GROUP + h * HD : GROUP + (h + 1) * HD], weights.astype(BF))
            ot_ref[h] = ot_ref[h] * shrink + mixed
            top[h] = new
        return carry

    lax.fori_loop(0, 4096 // CHUNK, body, 0)
    heads = []
    for h in range(3):
        lse_ref[h] = top[h] + jnp.log(total[h])
        normal = ot_ref[h] / total[h]
        ot_ref[h] = normal
        heads.append(normal.T.astype(BF))
    heads.append(jnp.zeros((512, 64), BF))
    out = jnp.concatenate(heads, axis=1)
    for i in range(4):
        o_ref[i] = out[i * ROWS : (i + 1) * ROWS]


def attend(q, kv):
    return pl.pallas_call(
        attend_kernel,
        name="attend",
        out_shape=(shape(4, ROWS, 256), shape(3, HD, 512, dtype=F32), shape(3, 1, 512, dtype=F32)),
        in_specs=[VM, VM],
        out_specs=(VM, VM, VM),
        scratch_shapes=[
            pltpu.VMEM((3, HD, 512), BF), pltpu.VMEM((3, 1, 512), F32), pltpu.VMEM((3, 1, 512), F32),
        ],
        compiler_params=pltpu.CompilerParams(vmem_limit_bytes=LIMIT),
    )(q, kv)


def attend_back_kernel(q_ref, kv_ref, da_ref, ot_ref, lse_ref, dq_ref, dkv_ref, qs, qt, ds, dt, delta, acc):
    for h in range(3):
        rows = stack_head(q_ref, h)
        qs[h] = rows
        qt[h] = turned(rows)
        rows = stack_head(da_ref, h)
        ds[h] = rows
        flipped = rows.astype(F32).T
        dt[h] = flipped.astype(BF)
        delta[h] = jnp.sum(flipped * ot_ref[h], axis=0, keepdims=True)
    acc[...] = jnp.zeros_like(acc)

    def body(i, carry):
        kv = load_chunk(kv_ref, i)
        keys, values = [], []
        for h in range(3):
            k = kv[:, h * HD : (h + 1) * HD]
            v = kv[:, GROUP + h * HD : GROUP + (h + 1) * HD]
            probs = jnp.exp(nn(k, qt[h]) - lse_ref[h])
            slopes = (probs * (nn(v, dt[h]) - delta[h])).astype(BF)
            keys.append(nn(slopes, qs[h]).astype(BF))
            values.append(nn(probs.astype(BF), ds[h]).astype(BF))
            acc[h] += tn(k, slopes)
        n = CHUNK // ROWS
        dkv_ref[pl.ds(i * n, n)] = jnp.concatenate(keys + values, axis=1).reshape(n, ROWS, HALF)
        return carry

    lax.fori_loop(0, 4096 // CHUNK, body, 0)
    heads = [(acc[h] * 0.125).T.astype(BF) for h in range(3)]
    heads.append(jnp.zeros((512, 64), BF))
    out = jnp.concatenate(heads, axis=1)
    for i in range(4):
        dq_ref[i] = out[i * ROWS : (i + 1) * ROWS]


def attend_back(q, kv, da, ot, lse):
    return pl.pallas_call(
        attend_back_kernel,
        name="attend_back",
        out_shape=(shape(4, ROWS, 256), shape(32, ROWS, HALF)),
        in_specs=[VM] * 5,
        out_specs=(VM, VM),
        scratch_shapes=[
            pltpu.VMEM((3, 512, HD), BF), pltpu.VMEM((3, HD, 512), BF),
            pltpu.VMEM((3, 512, HD), BF), pltpu.VMEM((3, HD, 512), BF),
            pltpu.VMEM((3, 1, 512), F32), pltpu.VMEM((3, HD, 512), F32),
        ],
        compiler_params=pltpu.CompilerParams(vmem_limit_bytes=LIMIT),
    )(q, kv, da, ot, lse)


def norm(hidden):
    centred = hidden - jnp.mean(hidden, axis=-1, keepdims=True)
    inverse = lax.rsqrt(jnp.mean(centred * centred, axis=-1, keepdims=True) + EPS)
    return centred * inverse, inverse


def norm_back(scaled, normal, inverse):
    centre = jnp.mean(scaled, axis=-1, keepdims=True)
    along = jnp.mean(scaled * normal, axis=-1, keepdims=True)
    return inverse * (scaled - centre - normal * along)


def column(value):
    return jnp.sum(value, axis=0, keepdims=True)


def block_kernel(
    x_ref, ct_ref, a_ref, wo, wo_a, wo_b, wi, wi_a, wi_b, wu, wu_a, wu_b, vec_ref, bi_ref,
    out_ref, dh1_ref, da_ref, af_ref, yb_ref, g_ref, df_ref, du_ref, dz_ref, vg_ref, big_ref,
    w_o, w_i, w_u, slope, sems,
):
    core = lax.axis_index("seq")
    half = lax.axis_index("fsdp")
    copies = []
    for i, (own, first, second, full, size) in enumerate(
        ((wo, wo_a, wo_b, w_o, HALF), (wi, wi_a, wi_b, w_i, HALF), (wu, wu_a, wu_b, w_u, FF // 2))
    ):
        q = size // 2
        at = pl.multiple_of(half * size, size)
        at_a = pl.multiple_of((1 - half) * size + core * q, q)
        at_b = pl.multiple_of((1 - half) * size + (1 - core) * q, q)
        copies.append(
            (
                pltpu.make_async_copy(own, full.at[pl.ds(at, size)], sems.at[3 * i]),
                pltpu.make_async_copy(first, full.at[pl.ds(at_a, q)], sems.at[3 * i + 1]),
                pltpu.make_async_copy(second, full.at[pl.ds(at_b, q)], sems.at[3 * i + 2]),
            )
        )
    for group in copies:
        for copy in group:
            copy.start()
    b_output, first_gain, first_shift = vec_ref[2:3, :], vec_ref[3:4, :], vec_ref[4:5, :]
    b_outer, second_gain, second_shift = vec_ref[5:6, :], vec_ref[6:7, :], vec_ref[7:8, :]
    mixed = jnp.concatenate([a_ref[g][:, :GROUP] for g in range(4)], axis=1)
    af_ref[...] = mixed
    for copy in copies[0]:
        copy.wait()
    hidden = x_ref[...].astype(F32) + nn(mixed, w_o[...]) + b_output
    normal1, inverse1 = norm(hidden)
    normed = normal1 * first_gain + first_shift
    low = normed.astype(BF)
    yb_ref[...] = low
    for group in copies[1:]:
        for copy in group:
            copy.wait()
    second_in = normed + b_outer
    for j in range(4):
        cut = slice(j * D, (j + 1) * D)
        inner = nn(low, w_i[:, cut]) + bi_ref[:, cut]
        cdf = 0.5 * (1.0 + lax.erf(inner * (0.5**0.5)))
        active = (inner * cdf).astype(BF)
        slope[:, cut] = cdf + inner * jnp.exp(inner * inner * -0.5) * 0.3989422804014327
        g_ref[:, cut] = active
        second_in = second_in + nn(active, w_u[cut, :])
    normal2, inverse2 = norm(second_in)
    out_ref[...] = (normal2 * second_gain + second_shift).astype(BF)
    upper = ct_ref[...].astype(F32)
    vg_ref[6:7, :] = column(upper * normal2)
    vg_ref[7:8, :] = column(upper)
    dh2 = norm_back(upper * second_gain, normal2, inverse2)
    df = dh2.astype(BF)
    df_ref[...] = df
    vg_ref[5:6, :] = column(df.astype(F32))
    dy1 = dh2
    for j in range(4):
        cut = slice(j * D, (j + 1) * D)
        du = (slope[:, cut] * nt(df, w_u[cut, :])).astype(BF)
        du_ref[:, cut] = du
        big_ref[:, cut] = column(du.astype(F32))
        dy1 = dy1 + nt(du, w_i[:, cut])
    vg_ref[3:4, :] = column(dy1 * normal1)
    vg_ref[4:5, :] = column(dy1)
    dh1 = norm_back(dy1 * first_gain, normal1, inverse1)
    dh1_ref[...] = dh1
    dz = dh1.astype(BF)
    dz_ref[...] = dz
    vg_ref[2:3, :] = column(dz.astype(F32))
    vg_ref[0:2, :] = jnp.zeros((2, D), F32)
    da = nt(dz, w_o[...]).astype(BF)
    pad = jnp.zeros((ROWS, 64), BF)
    for g in range(4):
        da_ref[g] = jnp.concatenate([da[:, g * GROUP : (g + 1) * GROUP], pad], axis=1)


def block(x, ct, a, weights, vec, b_inner):
    return pl.pallas_call(
        block_kernel,
        name="block",
        out_shape=(
            shape(ROWS, D), shape(ROWS, D, dtype=F32), shape(4, ROWS, 256), shape(ROWS, D), shape(ROWS, D),
            shape(ROWS, FF), shape(ROWS, D), shape(ROWS, FF), shape(ROWS, D), shape(8, D, dtype=F32),
            shape(1, FF, dtype=F32),
        ),
        in_specs=[VM, VM, VM] + [ANY] * 9 + [VM, VM],
        out_specs=(VM,) * 11,
        scratch_shapes=[
            pltpu.VMEM((D, D), BF), pltpu.VMEM((D, FF), BF), pltpu.VMEM((FF, D), BF),
            pltpu.VMEM((ROWS, FF), F32), pltpu.SemaphoreType.DMA((9,)),
        ],
        compiler_params=pltpu.CompilerParams(vmem_limit_bytes=LIMIT),
    )(x, ct, a, *weights, vec, b_inner)


def put(ref, at, value):
    ref[at] = value.astype(BF).reshape(4, 2, 48, HALF)


def wide_kernel(yb, yb_o, g, g_o, a, a_o, df, df_o, du, du_o, dz, dz_o, one_ref, two_ref, zero_ref):
    core = lax.axis_index("seq")

    def right(ref, other, start):
        cols = pl.ds(pl.multiple_of(start + core * HALF, HALF), HALF)
        return jnp.concatenate([ref[:, cols], other[:, cols]], axis=0)

    def left(ref, other, start):
        return jnp.concatenate([ref[:, start : start + HALF], other[:, start : start + HALF]], axis=0)

    outer = right(df, df_o, 0)
    attn = right(dz, dz_o, 0)
    for half in range(2):
        for m in range(4):
            put(one_ref, (half, m), tn(left(g, g_o, half * 1536 + m * HALF), outer))
        rows = left(yb, yb_o, half * HALF)
        for m in range(4):
            put(two_ref, (half, m), tn(rows, right(du, du_o, m * D)))
        put(zero_ref, half, tn(left(a, a_o, half * HALF), attn))


def wide(*arrays):
    return pl.pallas_call(
        wide_kernel,
        name="wide",
        out_shape=(shape(2, 4, 4, 2, 48, HALF), shape(2, 4, 4, 2, 48, HALF), shape(2, 4, 2, 48, HALF)),
        in_specs=[VM] * 12,
        out_specs=(VM, VM, VM),
        compiler_params=pltpu.CompilerParams(vmem_limit_bytes=LIMIT),
    )(*arrays)


def tail_kernel(dq_ref, dkv_ref, dh1_ref, w_ref, grad_ref, low_ref, vg_ref):
    low_ref[0] = jnp.concatenate([dq_ref[g][:, :GROUP] for g in range(4)], axis=1)
    sums = []
    for g in range(4):
        total = dkv_ref[2 * g].astype(F32)
        for k in range(1, 8):
            total = total + dkv_ref[(k // 2) * 8 + 2 * g + k % 2].astype(F32)
        sums.append(total.astype(BF))
    low_ref[1] = jnp.concatenate([s[:, :GROUP] for s in sums], axis=1)
    low_ref[2] = jnp.concatenate([s[:, GROUP:] for s in sums], axis=1)
    grad = dh1_ref[...]
    for i in range(3):
        grad = grad + nt(low_ref[i], w_ref[i])
    grad_ref[...] = grad
    vg_ref[...] = jnp.concatenate(
        [column(low_ref[0].astype(F32)), column(low_ref[2].astype(F32)), jnp.zeros((6, D), F32)], axis=0
    )


def tail(dq, dkv, dh1, w):
    return pl.pallas_call(
        tail_kernel,
        name="tail",
        out_shape=(shape(ROWS, D, dtype=F32), shape(3, ROWS, D), shape(8, D, dtype=F32)),
        in_specs=[VM] * 4,
        out_specs=(VM,) * 3,
        compiler_params=pltpu.CompilerParams(vmem_limit_bytes=LIMIT),
    )(dq, dkv, dh1, w)


def narrow_kernel(x, x_o, low, low_o, attn_ref, zero_ref):
    core = lax.axis_index("seq")
    cols = pl.ds(pl.multiple_of(core * HALF, HALF), HALF)
    for half in range(2):
        cut = slice(half * HALF, (half + 1) * HALF)
        rows = jnp.concatenate([x[:, cut], x_o[:, cut]], axis=0)
        for m in range(3):
            put(zero_ref, (half, m), tn(rows, jnp.concatenate([low[m, :, cols], low_o[m, :, cols]], axis=0)))
        zero_ref[half, 3] = attn_ref[half]


def narrow(*arrays):
    return pl.pallas_call(
        narrow_kernel,
        name="narrow",
        out_shape=shape(2, 4, 4, 2, 48, HALF),
        in_specs=[VM] * 5,
        out_specs=VM,
        compiler_params=pltpu.CompilerParams(vmem_limit_bytes=LIMIT),
    )(*arrays)


def reduce_kernel(
    g0, g1, g2, out, r0, r1, r2, s0, s1, s2, t0, t1, t2,
    a_out, a_in, b_out, b_in, c_out, c_in, d_out, d_in, e_out, e_in,
):
    y, z, xl, core, half = place()
    x = half * 2 + xl
    barrier = pltpu.get_barrier_semaphore()

    def along_x(k):
        e = wrap(x + k, 4)
        return device(y, z, lax.rem(e, 2), core, lax.div(e, 2))

    def pair(k):
        return lax.div(k, 4), lax.rem(k, 4)

    def at_yz(k):
        i, j = pair(k)
        return device(wrap(y + i, 4), wrap(z + j, 4), xl, core, half)

    def at_xz(k):
        i, j = pair(k)
        e = wrap(x + i, 4)
        return device(y, wrap(z + j, 4), lax.rem(e, 2), core, lax.div(e, 2))

    def at_xy(k):
        i, j = pair(k)
        e = wrap(x + i, 4)
        return device(wrap(y + j, 4), z, lax.rem(e, 2), core, lax.div(e, 2))

    def hello_yz(k, carry):
        greet(barrier, at_yz(k))
        return carry

    def hello_x(k, carry):
        i = lax.div(k - 1, 3) + 1
        j = lax.rem(k - 1, 3) + 1
        greet(barrier, at_xz(i * 4 + j))
        greet(barrier, at_xy(i * 4 + j))
        return carry

    def hello_row(k, carry):
        greet(barrier, along_x(k))
        return carry

    lax.fori_loop(1, 16, hello_yz, 0)
    lax.fori_loop(1, 10, hello_x, 0)
    lax.fori_loop(1, 4, hello_row, 0)
    greet(barrier, device(y, z, xl, 1 - core, half))
    pl.semaphore_wait(barrier, 37)

    def first(k, carry):
        e = wrap(x + k, 4)
        send(g0.at[lax.div(e, 2), :, :, lax.rem(e, 2)], r0.at[k - 1], a_out.at[0, k], a_in.at[0, k], along_x(k))
        send(g1.at[:, wrap(y + k, 4)], r1.at[k - 1], a_out.at[1, k], a_in.at[1, k], at_yz(k * 4))
        send(g2.at[:, :, wrap(z + k, 4)], r2.at[k - 1], a_out.at[2, k], a_in.at[2, k], at_yz(k))
        return carry

    lax.fori_loop(1, 4, first, 0)
    here = device(y, z, xl, core, half)

    def sum1(own, got, to, sem):
        for k in range(1, 4):
            finish(got.at[k - 1], got.at[k - 1], a_out.at[sem, k], a_in.at[sem, k], here)

        def add(i, carry):
            p, q, o = own(i)
            total = o.astype(F32)
            for k in range(3):
                total = total + got[(k,) + p].astype(F32)
            to[q] = total.astype(BF)
            return carry

        lax.fori_loop(0, 16, add, 0)

    def own0(i):
        p, q = pair(i)
        return (p, q), (p, q), g0[half, p, q, xl]

    def own1(i):
        f, q, r = lax.div(i, 8), lax.rem(lax.div(i, 2), 4), lax.rem(i, 2)
        return (f, q, r), (f, q, r), g1[f, y, q, r]

    def own2(i):
        f, q, r = lax.div(i, 8), lax.rem(lax.div(i, 2), 4), lax.rem(i, 2)
        return (f, q, r), (f, q, r), g2[f, q, z, r]

    sum1(own1, r1, s1, 1)

    def second1(k, carry):
        i, j = pair(k)
        e = wrap(x + i, 4)
        send(s1.at[lax.div(e, 2), wrap(z + j, 4), lax.rem(e, 2)], t1.at[k], b_out.at[1, k], b_in.at[1, k], at_xz(k))
        return carry

    lax.fori_loop(1, 16, second1, 0)
    sum1(own2, r2, s2, 2)

    def second2(k, carry):
        i, j = pair(k)
        e = wrap(x + i, 4)
        send(s2.at[lax.div(e, 2), wrap(y + j, 4), lax.rem(e, 2)], t2.at[k], b_out.at[2, k], b_in.at[2, k], at_xy(k))
        return carry

    lax.fori_loop(1, 16, second2, 0)
    sum1(own0, r0, s0, 0)

    def second0(k, carry):
        i, j = pair(k)
        send(s0.at[wrap(y + i, 4), wrap(z + j, 4)], t0.at[k], b_out.at[0, k], b_in.at[0, k], at_yz(k))
        return carry

    lax.fori_loop(1, 16, second0, 0)

    def sum2(own, got, slab):
        def done(k, carry):
            finish(got.at[k], got.at[k], b_out.at[slab, k], b_in.at[slab, k], here)
            return carry

        lax.fori_loop(1, 16, done, 0)

        def add(k, total):
            return total + got[k].astype(F32)

        total = lax.fori_loop(1, 16, add, own.astype(F32))
        out[core, slab, y, z, xl] = total.astype(BF)

    sum2(s1[half, z, xl], t1, 1)

    def third1(k, carry):
        i, j = lax.rem(k, 2), lax.div(k, 2)
        mine = out.at[core, 1, y, z, xl]
        send(mine, mine, c_out.at[1, k], c_in.at[1, k], device(y, wrap(z + j, 4), wrap(xl + i, 2), core, half))
        return carry

    lax.fori_loop(1, 8, third1, 0)
    sum2(s2[half, y, xl], t2, 2)

    def third2(k, carry):
        i, j = lax.rem(k, 2), lax.div(k, 2)
        mine = out.at[core, 2, y, z, xl]
        send(mine, mine, c_out.at[2, k], c_in.at[2, k], device(wrap(y + j, 4), z, wrap(xl + i, 2), core, half))
        return carry

    lax.fori_loop(1, 8, third2, 0)
    sum2(s0[y, z], t0, 0)

    def third0(k, carry):
        mine = out.at[core, 0, y, z, xl]
        send(mine, mine, c_out.at[0, k], c_in.at[0, k], at_yz(k))
        return carry

    lax.fori_loop(1, 16, third0, 0)

    def got1(k, carry):
        i, j = lax.rem(k, 2), lax.div(k, 2)
        piece = out.at[core, 1, y, wrap(z - j, 4), wrap(xl - i, 2)]
        finish(piece, piece, c_out.at[1, k], c_in.at[1, k], here)
        return carry

    lax.fori_loop(1, 8, got1, 0)

    def fourth1(k, carry):
        mine = out.at[core, 1, y]
        send(mine, mine, d_out.at[1, k], d_in.at[1, k], at_yz(k * 4))
        return carry

    lax.fori_loop(1, 4, fourth1, 0)

    def got2(k, carry):
        i, j = lax.rem(k, 2), lax.div(k, 2)
        piece = out.at[core, 2, wrap(y - j, 4), z, wrap(xl - i, 2)]
        finish(piece, piece, c_out.at[2, k], c_in.at[2, k], here)
        return carry

    lax.fori_loop(1, 8, got2, 0)

    def fourth2(k, carry):
        mine = out.at[core, 2, :, z]
        send(mine, mine, d_out.at[2, k], d_in.at[2, k], at_yz(k))
        return carry

    lax.fori_loop(1, 4, fourth2, 0)

    def got0(k, carry):
        i, j = pair(k)
        piece = out.at[core, 0, wrap(y - i, 4), wrap(z - j, 4), xl]
        finish(piece, piece, c_out.at[0, k], c_in.at[0, k], here)
        return carry

    lax.fori_loop(1, 16, got0, 0)
    mine0 = out.at[core, 0, :, :, xl]
    send(mine0, mine0, d_out.at[0, 1], d_in.at[0, 1], device(y, z, 1 - xl, core, half))

    def last1(k, carry):
        piece = out.at[core, 1, wrap(y - k, 4)]
        finish(piece, piece, d_out.at[1, k], d_in.at[1, k], here)
        return carry

    def last2(k, carry):
        piece = out.at[core, 2, :, wrap(z - k, 4)]
        finish(piece, piece, d_out.at[2, k], d_in.at[2, k], here)
        return carry

    sibling = device(y, z, xl, 1 - core, half)
    lax.fori_loop(1, 4, last1, 0)
    send(out.at[core, 1], out.at[core, 1], e_out.at[1], e_in.at[1], sibling)
    lax.fori_loop(1, 4, last2, 0)
    send(out.at[core, 2], out.at[core, 2], e_out.at[2], e_in.at[2], sibling)
    piece0 = out.at[core, 0, :, :, 1 - xl]
    finish(piece0, piece0, d_out.at[0, 1], d_in.at[0, 1], here)
    send(out.at[core, 0], out.at[core, 0], e_out.at[0], e_in.at[0], sibling)
    for slab in (1, 2, 0):
        piece = out.at[1 - core, slab]
        finish(piece, piece, e_out.at[slab], e_in.at[slab], here)


def reduce(g0, g1, g2):
    dma = pltpu.SemaphoreType.DMA
    blk = (48, HALF)
    return pl.pallas_call(
        reduce_kernel,
        name="reduce",
        out_shape=shape(2, 3, 4, 4, 2, *blk),
        in_specs=[VM] * 3,
        out_specs=VM,
        scratch_shapes=[
            pltpu.VMEM((3, 4, 4, *blk), BF), pltpu.VMEM((3, 2, 4, 2, *blk), BF), pltpu.VMEM((3, 2, 4, 2, *blk), BF),
            pltpu.VMEM((4, 4, *blk), BF), pltpu.VMEM((2, 4, 2, *blk), BF), pltpu.VMEM((2, 4, 2, *blk), BF),
            pltpu.VMEM((16, *blk), BF), pltpu.VMEM((16, *blk), BF), pltpu.VMEM((16, *blk), BF),
            dma((3, 4)), dma((3, 4)), dma((3, 16)), dma((3, 16)), dma((3, 16)), dma((3, 16)),
            dma((3, 4)), dma((3, 4)), dma((3,)), dma((3,)),
        ],
        compiler_params=pltpu.CompilerParams(
            collective_id=5, has_side_effects=True, vmem_limit_bytes=LIMIT
        ),
    )(g0, g1, g2)


def swap_halves(array):
    pairs = []
    for ctx in range(32):
        for core in range(2):
            for half in range(2):
                there = (ctx // 2) * 2 + (1 - ctx % 2)
                pairs.append(((ctx * 2 + core) * 2 + half, (there * 2 + core) * 2 + 1 - half))
    return lax.ppermute(array, AXES, pairs)


def swap_cores(array):
    return lax.ppermute(array, "seq", [(0, 1), (1, 0)])


def local(
    tokens, cotangent, w_query, w_key, w_value, w_output, b_query, b_value, b_output,
    first_gain, first_shift, w_inner, b_inner, w_outer, b_outer, second_gain, second_shift,
):
    core = lax.axis_index("seq")
    half = lax.axis_index("fsdp")
    x = tokens[0]

    def share(w):
        return lax.dynamic_slice_in_dim(w, core * (w.shape[0] // 2), w.shape[0] // 2, 0)

    small = jnp.concatenate(
        [b_query, b_value, b_output, first_gain, first_shift, b_outer, second_gain, second_shift, b_inner]
    ).reshape(12, HALF)
    small_o = swap_halves(small)
    qkv_a = swap_halves(jnp.stack([share(w) for w in (w_query, w_key, w_value)]))
    qkv_b = swap_cores(qkv_a)
    later, qkv_a = lax.optimization_barrier((tuple(share(w) for w in (w_output, w_inner, w_outer)), qkv_a))
    later_a = [swap_halves(w) for w in later]
    later_b = [swap_cores(w) for w in later_a]

    low_first = half == 0
    ahead = jnp.where(low_first, small, small_o).astype(F32)
    behind = jnp.where(low_first, small_o, small).astype(F32)
    vec = jnp.concatenate([ahead[:8], behind[:8]], axis=1)
    bi = jnp.concatenate([ahead[8:].reshape(1, 1536), behind[8:].reshape(1, 1536)], axis=1)

    q, kv, w_qkv = project(x, w_query, w_key, w_value, qkv_a, qkv_b, vec)
    q_all, kv_all = exchange(spread_kernel, "spread", 1, q, kv)
    mixed, mixed_t, lse = attend(q_all, kv_all)
    mixed = mates("mates_out", 2, mixed)
    weights = []
    for own, a, b in zip((w_output, w_inner, w_outer), later_a, later_b):
        weights += [own, a, b]
    layer_out, dh1, da, a_full, yb, g, df, du, dz, vg, big = block(x, cotangent[0], mixed, weights, vec, bi)
    da_all = mates("mates_in", 3, da)
    acts = (yb, g, a_full, df, du, dz)
    acts_o = [swap_cores(v) for v in acts]
    x_o = swap_cores(x)
    g1, g2, g0o = wide(*[v for pair in zip(acts, acts_o) for v in pair])
    dq, dkv = attend_back(q_all, kv_all, da_all, mixed_t, lse)
    dq, dkv = exchange(collect_kernel, "collect", 4, dq, dkv)
    tokens_grad, low, vg2 = tail(dq, dkv, dh1, w_qkv)
    low_o = swap_cores(low)
    g0 = narrow(x, x_o, low, low_o, g0o)
    summed = reduce(g0, g1, g2)

    vectors = jnp.concatenate([vg + vg2, big.reshape(4, D)], axis=0)
    vectors = lax.psum(vectors, AXES)
    vecs = lax.dynamic_slice_in_dim(vectors[:8], half * HALF, HALF, 1)
    b_inner_grad = lax.dynamic_slice_in_dim(vectors[8:].reshape(FF), half * 1536, 1536, 0)

    full = jnp.concatenate(
        [summed[0].reshape(3, 1536, HALF), summed[1].reshape(3, 1536, HALF)], axis=2
    ).astype(F32)
    inner = full[2].reshape(4, HALF, D).transpose(1, 0, 2).reshape(HALF, FF)
    return (
        layer_out[None], tokens_grad[None],
        full[0, :HALF], full[0, HALF : 2 * HALF], full[0, 2 * HALF : 3 * HALF], full[0, 3 * HALF :],
        vecs[0], vecs[1], vecs[2], vecs[3], vecs[4], inner, b_inner_grad, full[1], vecs[5], vecs[6], vecs[7],
    )


def solution(mesh):
    rows = P(("seq", "fsdp"), "ctx", None)
    mat = P("fsdp", None)
    vec = P("fsdp")
    return jax.shard_map(
        local,
        mesh=mesh,
        in_specs=(rows, rows, mat, mat, mat, mat, vec, vec, vec, vec, vec, mat, vec, mat, vec, vec, vec),
        out_specs=(rows, rows, mat, mat, mat, mat, vec, vec, vec, vec, vec, mat, vec, mat, vec, vec, vec),
        check_vma=False,
    )
```

time: 1820 us -> 500 us (0.27)
  waiting for transfers between devices: 911 us -> 69.8 us
  local copies, waits for them, and re-layouts: 382 us -> 30.6 us
  blocking collectives: 403 us -> 66.6 us
  Pallas kernels: 0 us -> 295 us
  matrix products: 74 us -> 0 us
  starting transfers between devices: 0.82 us -> 26.6 us
    all_gather x8 -> x0, waiting for transfers between devices: 485 us -> none  [the longest x1 166 us: local(): lax.all_gather(keys, 'ctx', axis=1, tiled=True)]
    unnamed x89 -> x61, local copies, waits for them, and re-layouts: 312 us -> 16.1 us
    pallas_call x0 -> x12, Pallas kernels: none -> 295 us  [the longest x2 114 us: exchange(): pl.pallas_call(kernel, name=name, out_shape=(shape(4, ROWS, 256), shape(3...]
    psum x1, blocking collectives: 353 us -> 66.6 us  [local(): vectors = lax.psum(vectors, AXES)]
    unnamed x21 -> x0, waiting for transfers between devices: 266 us -> none
    reduce_scatter x3 -> x0, waiting for transfers between devices: 160 us -> none  [the longest x1 66.5 us: local(): lax.psum_scatter(inner_matrix.astype(jnp.bfloat16), 'fsdp', scatter_dimen...]
    dot_general x60 -> x0, matrix products: 74 us -> none  [the longest x6 19.6 us: product(): return jnp.dot(left, right, preferred_element_type=jnp.float32)]
    ppermute x0 -> x17, waiting for transfers between devices: none -> 69.8 us  [the longest x5 68.4 us: swap_halves(): return lax.ppermute(array, AXES, pairs)]
  transfers between devices with their start and end apart: 16 -> 17, of which waited for: 15 -> 6; matrix products, arithmetic and copies ran while one was open for 13% -> 4% of each run, Pallas kernels for 0% -> 39%
where the time goes in v1:
time: 500 us; the launch traced here: 499 us
  Pallas kernels  295 us (59%)
  waiting for transfers between devices  69.8 us (14%)
  blocking collectives  66.6 us (13%)
  local copies, waits for them, and re-layouts  30.6 us (6%)
  starting transfers between devices  26.6 us (5%)
  other arithmetic  9.51 us (2%)
    pallas_call x2, Pallas kernels, exchange(): pl.pallas_call(kernel, name=name, out_shape=(shape(4, ROWS, 256), shape(3...  114 us
    pallas_call x1, Pallas kernels, reduce(): pl.pallas_call(reduce_kernel, name='reduce', out_shape=shape(2, 3, 4, 4,...  86.3 us
    ppermute x5, waiting for transfers between devices, swap_halves(): return lax.ppermute(array, AXES, pairs)  68.4 us
    psum x1, blocking collectives, local(): vectors = lax.psum(vectors, AXES)  66.6 us
    pallas_call x1, Pallas kernels, attend_back(): pl.pallas_call(attend_back_kernel, name='attend_back', out_shape=(shape(4...  25.4 us
    pallas_call x1, Pallas kernels, attend(): pl.pallas_call(attend_kernel, name='attend', out_shape=(shape(4, ROWS, 25...  20.7 us
    unnamed x61, local copies, waits for them, and re-layouts  16.1 us
    pallas_call x2, Pallas kernels, mates(): pl.pallas_call(mates_kernel, name=name, out_shape=shape(4, ROWS, 256), in...  15.4 us
  transfers between devices with their start and end apart: 17, of which 6 were waited for; matrix products, arithmetic and copies ran while one was open for 4% of the time, Pallas kernels for 39%

profile of v1, /device:TPU:1, one launch (start us, length us, event | category | flops | bytes accessed | tf_op | source)
XLA Modules:
  0.0 499.2 jit_solution(8404871931584199371)
XLA Ops:
  3.8 3.3 collective-permute-start
  9.4 17.0 %collective-permute-done.ra = bf16[3,192,768]{2,1,0:T(8,128)(2,1)} collective-permute-done((bf16[3,192,768]{2,1,0:T(8,128)(2,1)}, bf16[3,192,768]{2,1,0:T(8,128)(2,1)}, u32[]{:S(2)}, u32[]{:S(2)}) %collective-permute-start) | collective-permute-done | bytes 884768 | tf_op jit(solution)/shard_map/ppermute | solution.py:845
  26.4 2.8 collective-permute-start.5
  29.2 24.4 %collective-permute-done.5.wi_a = bf16[192,3072]{1,0:T(8,128)(2,1)S(1)} collective-permute-done((bf16[192,3072]{1,0:T(8,128)(2,1)S(1)}, bf16[192,3072]{1,0:T(8,128)(2,1)S(1)}, u32[]{:S(2)}, u32[]{:S(2)}) %collective-permute-start.5) | collective-permute-done | bytes 1179680 | tf_op jit(solution)/shard_map/ppermute | solution.py:845
  53.6 4.5 collective-permute-start.6
  58.2 20.7 %collective-permute-done.7.wu_a = bf16[768,768]{1,0:T(8,128)(2,1)S(1)} collective-permute-done((bf16[768,768]{1,0:T(8,128)(2,1)S(1)}, bf16[768,768]{1,0:T(8,128)(2,1)S(1)}, u32[]{:S(2)}, u32[]{:S(2)}) %collective-permute-start.7) | collective-permute-done | bytes 1179680 | tf_op jit(solution)/shard_map/ppermute | solution.py:845
  78.9 2.5 collective-permute-start.8
  85.7 1.4 dynamic-update-slice.3
  87.1 1.4 dynamic-update-slice.4
  94.2 2.8 collective-permute-start.2
  98.9 2.7 collective-permute-start.3
  102.3 5.4 %collective-permute-done.3.wo_a = bf16[192,768]{1,0:T(8,128)(2,1)S(1)} collective-permute-done((bf16[192,768]{1,0:T(8,128)(2,1)}, bf16[192,768]{1,0:T(8,128)(2,1)S(1)}, u32[]{:S(2)}, u32[]{:S(2)}) %collective-permute-start.3) | collective-permute-done | bytes 294944 | tf_op jit(solution)/shard_map/ppermute | solution.py:845
  107.7 2.1 collective-permute-start.4
  111.4 5.6 %project.1 = (bf16[4,128,256]{2,1,0:T(8,128)(2,1)}, bf16[4,128,384]{2,1,0:T(8,128)(2,1)}, bf16[3,768,768]{2,1,0:T(8,128)(2,1)}) custom-call(bf16[128,768]{1,0:T(8,128)(2,1)} %bitcast.41, bf16[384,768]{1,0:T(8,128)(2,1)} %wq.1, bf16[384,768]{1,0:T(8,128)(2,1)} %wk.1, bf16[384,768]{1,0:T(8,128)(2,1)} %wv.1, bf16[3,192,768]{2,1,0:T(8,128)(2,1)} %collective-permute-done.ra, ...), custom_call_target="tpu_custom_call" | custom-call | tf_op jit(solution)/shard_map/project/pallas_call | solution.py:273
  116.9 62.1 %spread.1 = (bf16[4,128,256]{2,1,0:T(8,128)(2,1)}, bf16[32,128,384]{2,1,0:T(8,128)(2,1)}) custom-call(bf16[4,128,256]{2,1,0:T(8,128)(2,1)} %get-tuple-element.51.q_ref, bf16[4,128,384]{2,1,0:T(8,128)(2,1)} %get-tuple-element.52.kv_ref), custom_call_target="tpu_custom_call" | custom-call | tf_op jit(solution)/shard_map/spread/pallas_call | solution.py:216
  179.0 20.7 %attend.1 = (bf16[4,128,256]{2,1,0:T(8,128)(2,1)}, f32[3,64,512]{2,1,0:T(8,128)}, f32[3,1,512]{2,1,0:T(1,128)}) custom-call(bf16[4,128,256]{2,1,0:T(8,128)(2,1)} %get-tuple-element.53.q_ref, bf16[32,128,384]{2,1,0:T(8,128)(2,1)} %get-tuple-element.54.kv_ref), custom_call_target="tpu_custom_call" | custom-call | tf_op jit(solution)/shard_map/attend/pallas_call | solution.py:335
  199.7 7.1 %mates_out.1.a_ref = bf16[4,128,256]{2,1,0:T(8,128)(2,1)} custom-call(bf16[4,128,256]{2,1,0:T(8,128)(2,1)} %get-tuple-element.55.q_ref), custom_call_target="tpu_custom_call" | custom-call | tf_op jit(solution)/shard_map/mates_out/pallas_call | solution.py:231
  207.9 12.0 %block.1 = (bf16[128,768]{1,0:T(8,128)(2,1)}, f32[128,768]{1,0:T(8,128)}, bf16[4,128,256]{2,1,0:T(8,128)(2,1)}, bf16[128,768]{1,0:T(8,128)(2,1)}, bf16[128,768]{...) custom-call(bf16[128,768]{1,0:T(8,128)(2,1)} %bitcast.42, ...), custom_call_target="tpu_custom_call" | custom-call | tf_op jit(solution)/shard_map/block/pallas_call | solution.py:494
  219.9 2.1 collective-permute-start.12
  222.6 8.3 %mates_in.1.da_ref = bf16[4,128,256]{2,1,0:T(8,128)(2,1)} custom-call(bf16[4,128,256]{2,1,0:T(8,128)(2,1)} %get-tuple-element.60.q_ref), custom_call_target="tpu_custom_call" | custom-call | tf_op jit(solution)/shard_map/mates_in/pallas_call | solution.py:231
  230.9 25.4 %attend_back.1 = (bf16[4,128,256]{2,1,0:T(8,128)(2,1)}, bf16[32,128,384]{2,1,0:T(8,128)(2,1)}) custom-call(bf16[4,128,256]{2,1,0:T(8,128)(2,1)} %get-tuple-element.53.q_ref, bf16[32,128,384]{2,1,0:T(8,128)(2,1)} %get-tuple-element.54.kv_ref, bf16[4,128,256]{2,1,0:T(8,128)(2,1)} %mates_in.1.da_ref, f32[3,64,512]{2,1,0:T(8,128)} %get-tuple-element.61.ot_ref, ...), custom_call_target="tpu_custom_call" | custom-call | tf_op jit(solution)/shard_map/attend_back/pallas_call | solution.py:384
  256.2 52.2 %collect.1 = (bf16[4,128,256]{2,1,0:T(8,128)(2,1)}, bf16[32,128,384]{2,1,0:T(8,128)(2,1)}) custom-call(bf16[4,128,256]{2,1,0:T(8,128)(2,1)} %get-tuple-element.63.q_ref, bf16[32,128,384]{2,1,0:T(8,128)(2,1)} %get-tuple-element.64.kv_ref), custom_call_target="tpu_custom_call" | custom-call | tf_op jit(solution)/shard_map/collect/pallas_call | solution.py:216
  308.5 5.5 %tail.1 = (f32[128,768]{1,0:T(8,128)}, bf16[3,128,768]{2,1,0:T(8,128)(2,1)}, f32[8,768]{1,0:T(8,128)}) custom-call(bf16[4,128,256]{2,1,0:T(8,128)(2,1)} %get-tuple-element.65.dq_ref, bf16[32,128,384]{2,1,0:T(8,128)(2,1)} %get-tuple-element.66.dkv_ref, f32[128,768]{1,0:T(8,128)} %get-tuple-element.67.dh1_ref, bf16[3,768,768]{2,1,0:T(8,128)(2,1)} %get-tuple-element.68.w_ref), custom_call_target="tpu_custom_call" | custom-call | tf_op jit(solution)/shard_map/tail/pallas_call | solution.py:568
  314.0 1.6 collective-permute-start.10
  320.1 66.6 %psum.7 = f32[12,768]{1,0:T(8,128)S(1)} all-reduce(f32[12,768]{1,0:T(8,128)S(1)} %pad_maximum_fusion.2), channel_id=1, replica_groups=mesh['ctx'=32,'seq'=2,'fsdp'=2] {'ctx','seq','fsdp'}, use_global_device_ids=true, to_apply=%region_0.1 | all-reduce | flops 9216 | bytes 73728 | tf_op jit(solution)/shard_map/psum | solution.py:900
  389.9 6.3 %wide.1 = (bf16[2,4,4,2,48,384]{5,4,3,2,1,0:T(8,128)(2,1)}, bf16[2,4,4,2,48,384]{5,4,3,2,1,0:T(8,128)(2,1)}, bf16[2,4,2,48,384]{4,3,2,1,0:T(8,128)(2,1)}) custom-call(bf16[128,768]{1,0:T(8,128)(2,1)} %get-tuple-element.71.yb, bf16[128,768]{1,0:T(8,128)(2,1)} %copy-done.15, bf16[128,3072]{1,0:T(8,128)(2,1)} %get-tuple-element.72.g, ...), custom_call_target="tpu_custom_call" | custom-call | tf_op jit(solution)/shard_map/wide/pallas_call | solution.py:538
  397.0 3.9 narrow.1.g0
  400.9 86.3 %reduce.21 = bf16[2,3,4,4,2,48,384]{6,5,4,3,2,1,0:T(8,128)(2,1)} custom-call(bf16[2,4,4,2,48,384]{5,4,3,2,1,0:T(8,128)(2,1)} %narrow.1.g0, bf16[2,4,4,2,48,384]{5,4,3,2,1,0:T(8,128)(2,1)} %get-tuple-element.78.g1, bf16[2,4,4,2,48,384]{5,4,3,2,1,0:T(8,128)(2,1)} %get-tuple-element.79.g2), custom_call_target="tpu_custom_call" | custom-call | tf_op jit(solution)/shard_map/reduce/pallas_call | solution.py:819
  487.2 4.0 fusion.1
  491.2 2.3 convert_bitcast_fusion.1
  493.5 2.9 convert_bitcast_fusion
  496.4 2.9 copy.35
  (104 shorter events, 29.5 us)
Async XLA Ops:
  3.8 22.5 %collective-permute-start = (bf16[3,192,768]{2,1,0:T(8,128)(2,1)}, bf16[3,192,768]{2,1,0:T(8,128)(2,1)}, u32[]{:S(2)}, u32[]{:S(2)}) collective-permute-start(bf16[3,192,768]{2,1,0:T(8,128)(2,1)} %pad_maximum_fusion.1), channel_id=1, source_target_pairs={{0,5},{1,4},{2,7},{3,6},{4,1},{5,0},{6,3},{7,2},{8,13},{9,12},{10,... | collective-permute-start | bytes 2654216 | tf_op jit(solution)/shard_map/ppermute | solution.py:845
  7.9 73.5 %copy-start.22 = (bf16[384]{0:T(512)(128)(2,1)S(1)}, bf16[384]{0:T(512)(128)(2,1)}, u32[]{:S(2)}) copy-start(bf16[384]{0:T(512)(128)(2,1)} %param.23) | copy-start | bytes 2308
  7.9 74.9 %copy-start.23 = (bf16[384]{0:T(512)(128)(2,1)S(1)}, bf16[384]{0:T(512)(128)(2,1)}, u32[]{:S(2)}) copy-start(bf16[384]{0:T(512)(128)(2,1)} %param.24) | copy-start | bytes 2308
  7.9 76.4 %copy-start.24 = (bf16[384]{0:T(512)(128)(2,1)S(1)}, bf16[384]{0:T(512)(128)(2,1)}, u32[]{:S(2)}) copy-start(bf16[384]{0:T(512)(128)(2,1)} %param.25) | copy-start | bytes 2308
  7.9 85.0 %copy-start.21 = (bf16[1536]{0:T(1024)(128)(2,1)S(1)}, bf16[1536]{0:T(1024)(128)(2,1)}, u32[]{:S(2)}) copy-start(bf16[1536]{0:T(1024)(128)(2,1)} %param.29) | copy-start | bytes 9220
  26.4 27.3 %collective-permute-start.5 = (bf16[192,3072]{1,0:T(8,128)(2,1)S(1)}, bf16[192,3072]{1,0:T(8,128)(2,1)S(1)}, u32[]{:S(2)}, u32[]{:S(2)}) collective-permute-start(bf16[192,3072]{1,0:T(8,128)(2,1)S(1)} %constant_dynamic-slice_fusion.2), channel_id=1, source_target_pairs={{0,5},{1,4},{2,7},{3,6},{4,1},{5,0},{6,3},{7,2},{8,13},{9,12},{10,... | collective-permute-start | bytes 3538952 | tf_op jit(solution)/shard_map/ppermute | solution.py:845
  29.2 49.7 %collective-permute-start.7 = (bf16[768,768]{1,0:T(8,128)(2,1)S(1)}, bf16[768,768]{1,0:T(8,128)(2,1)S(1)}, u32[]{:S(2)}, u32[]{:S(2)}) collective-permute-start(bf16[768,768]{1,0:T(8,128)(2,1)S(1)} %constant_dynamic-slice_fusion.1), channel_id=1, source_target_pairs={{0,5},{1,4},{2,7},{3,6},{4,1},{5,0},{6,3},{7,2},{8,13},{9,12},{10,... | collective-permute-start | bytes 3538952 | tf_op jit(solution)/shard_map/ppermute | solution.py:845
  53.6 125.4 %copy-start.3 = (bf16[192,3072]{1,0:T(8,128)(2,1)}, bf16[192,3072]{1,0:T(8,128)(2,1)S(1)}, u32[]{:S(2)}) copy-start(bf16[192,3072]{1,0:T(8,128)(2,1)S(1)} %collective-permute-done.5.wi_a) | copy-start | bytes 3538948
  53.6 153.2 %collective-permute-start.6 = (bf16[192,3072]{1,0:T(8,128)(2,1)S(1)}, bf16[192,3072]{1,0:T(8,128)(2,1)S(1)}, u32[]{:S(2)}, u32[]{:S(2)}) collective-permute-start(bf16[192,3072]{1,0:T(8,128)(2,1)S(1)} %collective-permute-done.5.wi_a), channel_id=1, source_target_pairs={{0,2},{2,0},{1,3},{3,1},{4,6},{6,4},{5,7},{7,5},{8,10},{10,8},{9,1... | collective-permute-start | bytes 3538952 | tf_op jit(solution)/shard_map/ppermute | solution.py:849
  78.9 100.1 %copy-start.4 = (bf16[768,768]{1,0:T(8,128)(2,1)}, bf16[768,768]{1,0:T(8,128)(2,1)S(1)}, u32[]{:S(2)}) copy-start(bf16[768,768]{1,0:T(8,128)(2,1)S(1)} %collective-permute-done.7.wu_a) | copy-start | bytes 3538948
  78.9 127.9 %collective-permute-start.8 = (bf16[768,768]{1,0:T(8,128)(2,1)S(1)}, bf16[768,768]{1,0:T(8,128)(2,1)}, u32[]{:S(2)}, u32[]{:S(2)}) collective-permute-start(bf16[768,768]{1,0:T(8,128)(2,1)S(1)} %collective-permute-done.7.wu_a), channel_id=1, source_target_pairs={{0,2},{2,0},{1,3},{3,1},{4,6},{6,4},{5,7},{7,5},{8,10},{10,8},{9,1... | collective-permute-start | bytes 3538952 | tf_op jit(solution)/shard_map/ppermute | solution.py:849
  94.2 3.9 collective-permute-start.2
  97.0 13.5 %collective-permute-start.1 = (bf16[3,192,768]{2,1,0:T(8,128)(2,1)}, bf16[3,192,768]{2,1,0:T(8,128)(2,1)S(1)}, u32[]{:S(2)}, u32[]{:S(2)}) collective-permute-start(bf16[3,192,768]{2,1,0:T(8,128)(2,1)} %collective-permute-done.ra), channel_id=1, source_target_pairs={{0,2},{2,0},{1,3},{3,1},{4,6},{6,4},{5,7},{7,5},{8,10},{10,8},{9,1... | collective-permute-start | bytes 2654216 | tf_op jit(solution)/shard_map/ppermute | solution.py:849
  98.9 8.8 %collective-permute-start.3 = (bf16[192,768]{1,0:T(8,128)(2,1)}, bf16[192,768]{1,0:T(8,128)(2,1)S(1)}, u32[]{:S(2)}, u32[]{:S(2)}) collective-permute-start(bf16[192,768]{1,0:T(8,128)(2,1)} %constant_dynamic-slice_fusion.3), channel_id=1, source_target_pairs={{0,5},{1,4},{2,7},{3,6},{4,1},{5,0},{6,3},{7,2},{8,13},{9,12},{10,... | collective-permute-start | bytes 884744 | tf_op jit(solution)/shard_map/ppermute | solution.py:845
  107.7 99.2 %copy-start.10 = (bf16[192,768]{1,0:T(8,128)(2,1)}, bf16[192,768]{1,0:T(8,128)(2,1)S(1)}, u32[]{:S(2)}) copy-start(bf16[192,768]{1,0:T(8,128)(2,1)S(1)} %collective-permute-done.3.wo_a) | copy-start | bytes 884740
  107.7 99.1 %collective-permute-start.4 = (bf16[192,768]{1,0:T(8,128)(2,1)S(1)}, bf16[192,768]{1,0:T(8,128)(2,1)S(1)}, u32[]{:S(2)}, u32[]{:S(2)}) collective-permute-start(bf16[192,768]{1,0:T(8,128)(2,1)S(1)} %collective-permute-done.3.wo_a), channel_id=1, source_target_pairs={{0,2},{2,0},{1,3},{3,1},{4,6},{6,4},{5,7},{7,5},{8,10},{10,8},{9,1... | collective-permute-start | bytes 884744 | tf_op jit(solution)/shard_map/ppermute | solution.py:849
  219.9 168.2 %collective-permute-start.12 = (bf16[128,3072]{1,0:T(8,128)(2,1)}, bf16[128,3072]{1,0:T(8,128)(2,1)S(1)}, u32[]{:S(2)}, u32[]{:S(2)}) collective-permute-start(bf16[128,3072]{1,0:T(8,128)(2,1)} %get-tuple-element.72.g), channel_id=1, source_target_pairs={{0,2},{2,0},{1,3},{3,1},{4,6},{6,4},{5,7},{7,5},{8,10},{10,8},{9,1... | collective-permute-start | bytes 2359304 | tf_op jit(solution)/shard_map/ppermute | solution.py:849
  222.1 166.1 %collective-permute-start.15 = (bf16[128,3072]{1,0:T(8,128)(2,1)}, bf16[128,3072]{1,0:T(8,128)(2,1)S(1)}, u32[]{:S(2)}, u32[]{:S(2)}) collective-permute-start(bf16[128,3072]{1,0:T(8,128)(2,1)} %get-tuple-element.75.du), channel_id=1, source_target_pairs={{0,2},{2,0},{1,3},{3,1},{4,6},{6,4},{5,7},{7,5},{8,10},{10,8},{9,1... | collective-permute-start | bytes 2359304 | tf_op jit(solution)/shard_map/ppermute | solution.py:849
  222.1 93.5 %collective-permute-start.11 = (bf16[128,768]{1,0:T(8,128)(2,1)}, bf16[128,768]{1,0:T(8,128)(2,1)S(1)}, u32[]{:S(2)}, u32[]{:S(2)}) collective-permute-start(bf16[128,768]{1,0:T(8,128)(2,1)} %get-tuple-element.71.yb), channel_id=1, source_target_pairs={{0,2},{2,0},{1,3},{3,1},{4,6},{6,4},{5,7},{7,5},{8,10},{10,8},{9,1... | collective-permute-start | bytes 589832 | tf_op jit(solution)/shard_map/ppermute | solution.py:849
  308.5 7.2 %copy-start.13 = (bf16[128,768]{1,0:T(8,128)(2,1)S(1)}, bf16[128,768]{1,0:T(8,128)(2,1)}, u32[]{:S(2)}) copy-start(bf16[128,768]{1,0:T(8,128)(2,1)} %get-tuple-element.74.df) | copy-start | bytes 589828
  308.5 9.0 %copy-start.14 = (bf16[128,768]{1,0:T(8,128)(2,1)S(1)}, bf16[128,768]{1,0:T(8,128)(2,1)}, u32[]{:S(2)}) copy-start(bf16[128,768]{1,0:T(8,128)(2,1)} %get-tuple-element.76.dz) | copy-start | bytes 589828
  308.5 9.4 %copy-start.1 = (bf16[1,128,768]{2,1,0:T(8,128)(2,1)S(1)}, bf16[1,128,768]{2,1,0:T(8,128)(2,1)}, u32[]{:S(2)}) copy-start(bf16[1,128,768]{2,1,0:T(8,128)(2,1)} %param.17) | copy-start | bytes 589828
  308.5 10.2 %copy-start.20 = (f32[1,3072]{1,0:T(1,128)S(1)}, f32[1,3072]{1,0:T(1,128)}, u32[]{:S(2)}) copy-start(f32[1,3072]{1,0:T(1,128)} %get-tuple-element.82) | copy-start | bytes 36868
  308.5 10.9 %copy-start.19 = (f32[8,768]{1,0:T(8,128)S(1)}, f32[8,768]{1,0:T(8,128)}, u32[]{:S(2)}) copy-start(f32[8,768]{1,0:T(8,128)} %get-tuple-element.80) | copy-start | bytes 73732
  314.0 82.1 %collective-permute-start.10 = (bf16[3,128,768]{2,1,0:T(8,128)(2,1)}, bf16[3,128,768]{2,1,0:T(8,128)(2,1)S(1)}, u32[]{:S(2)}, u32[]{:S(2)}) collective-permute-start(bf16[3,128,768]{2,1,0:T(8,128)(2,1)} %get-tuple-element.70.low), channel_id=1, source_target_pairs={{0,2},{2,0},{1,3},{3,1},{4,6},{6,4},{5,7},{7,5},{8,10},{10,8},{9,1... | collective-permute-start | bytes 1769480 | tf_op jit(solution)/shard_map/ppermute | solution.py:849
  315.6 1.9 collective-permute-start.13
  315.7 72.5 %copy-start.15 = (bf16[128,768]{1,0:T(8,128)(2,1)}, bf16[128,768]{1,0:T(8,128)(2,1)S(1)}, u32[]{:S(2)}) copy-start(bf16[128,768]{1,0:T(8,128)(2,1)S(1)} %collective-permute-done.11.yb_o) | copy-start | bytes 589828
  315.7 2.2 collective-permute-start.14
  317.5 70.6 %copy-start.16 = (bf16[128,768]{1,0:T(8,128)(2,1)}, bf16[128,768]{1,0:T(8,128)(2,1)S(1)}, u32[]{:S(2)}) copy-start(bf16[128,768]{1,0:T(8,128)(2,1)S(1)} %collective-permute-done.13.a_o) | copy-start | bytes 589828
  317.5 70.6 %collective-permute-start.16 = (bf16[128,768]{1,0:T(8,128)(2,1)S(1)}, bf16[128,768]{1,0:T(8,128)(2,1)}, u32[]{:S(2)}, u32[]{:S(2)}) collective-permute-start(bf16[128,768]{1,0:T(8,128)(2,1)S(1)} %copy-done.14), channel_id=1, source_target_pairs={{0,2},{2,0},{1,3},{3,1},{4,6},{6,4},{5,7},{7,5},{8,10},{10,8},{9,1... | collective-permute-start | bytes 589832 | tf_op jit(solution)/shard_map/ppermute | solution.py:849
  317.9 70.3 %copy-start.17 = (bf16[128,768]{1,0:T(8,128)(2,1)}, bf16[128,768]{1,0:T(8,128)(2,1)S(1)}, u32[]{:S(2)}) copy-start(bf16[128,768]{1,0:T(8,128)(2,1)S(1)} %collective-permute-done.14.df_o) | copy-start | bytes 589828
  317.9 78.3 %collective-permute-start.9 = (bf16[128,768]{1,0:T(8,128)(2,1)S(1)}, bf16[128,768]{1,0:T(8,128)(2,1)S(1)}, u32[]{:S(2)}, u32[]{:S(2)}) collective-permute-start(bf16[128,768]{1,0:T(8,128)(2,1)S(1)} %bitcast.44), channel_id=1, source_target_pairs={{0,2},{2,0},{1,3},{3,1},{4,6},{6,4},{5,7},{7,5},{8,10},{10,8},{9,1... | collective-permute-start | bytes 589832 | tf_op jit(solution)/shard_map/ppermute | solution.py:849
  (10 other events, 26.1 us)

commit v2 on v1

--- a/solution.py
+++ b/solution.py
@@ -74,219 +74,289 @@
     pl.semaphore_signal(barrier, inc=1, device_id=where, device_id_type=MESH)
 
 
-def parts(k):
-    return lax.div(k, 8), lax.rem(lax.div(k, 2), 4), lax.rem(k, 2)
-
-
-def spread_kernel(q_ref, kv_ref, qo_ref, kvo_ref, local_sem, qs, qr, ks, kr):
-    y, z, xl, core, half = place()
-    me = lax.axis_index("ctx")
-    barrier = pltpu.get_barrier_semaphore()
-
-    def other(k):
-        dy, dz, dx = parts(k)
-        return wrap(y + dy, 4), wrap(z + dz, 4), wrap(xl + dx, 2)
-
-    def source(k):
-        dy, dz, dx = parts(k)
-        return (wrap(y - dy, 4) * 4 + wrap(z - dz, 4)) * 2 + wrap(xl - dx, 2)
-
-    def hello(k, carry):
-        ey, ez, ex = other(k)
-        greet(barrier, device(ey, ez, ex, core, half))
-        return carry
-
-    lax.fori_loop(1, 32, hello, 0)
-    pl.semaphore_wait(barrier, 31)
-
-    def push_q(k, carry):
-        ez = wrap(z + k, 4)
-        send(q_ref.at[ez], qo_ref.at[z], qs.at[k], qr.at[k], device(y, ez, xl, core, half))
-        return carry
-
-    def push(k, carry):
-        ey, ez, ex = other(k)
-        send(kv_ref.at[ez], kvo_ref.at[me], ks.at[k], kr.at[k], device(ey, ez, ex, core, half))
-        return carry
-
-    lax.fori_loop(1, 4, push_q, 0)
-    lax.fori_loop(1, 32, push, 0)
-    mine = pltpu.make_async_copy(kv_ref.at[z], kvo_ref.at[me], local_sem.at[0])
-    mine.start()
-    mine_q = pltpu.make_async_copy(q_ref.at[z], qo_ref.at[z], local_sem.at[1])
-    mine_q.start()
+def pair(k):
+    return lax.div(k, 4), lax.rem(k, 4)
+
+
+class Turn:
+    def __init__(self):
+        self.y, self.z, self.xl, self.core, self.half = place()
+        self.stays = self.xl == self.core
+
+    def partner(self, k):
+        i, j = pair(k)
+        return device(wrap(self.y + i, 4), wrap(self.z + j, 4), self.core, self.xl, self.half)
+
+    def ahead(self, k):
+        i, j = pair(k)
+        return wrap(self.y + i, 4), wrap(self.z + j, 4)
+
+    def behind(self, k):
+        i, j = pair(k)
+        return wrap(self.y - i, 4), wrap(self.z - j, 4)
+
+    def sibling(self):
+        return device(self.y, self.z, self.xl, 1 - self.core, self.half)
+
+    def greet(self, count, others=()):
+        barrier = pltpu.get_barrier_semaphore()
+
+        def hello(k, carry):
+            greet(barrier, self.partner(k))
+            return carry
+
+        lax.fori_loop(1, count, hello, 0)
+        for where in others:
+            greet(barrier, where)
+
+        @pl.when(jnp.logical_not(self.stays))
+        def _():
+            greet(barrier, self.partner(0))
+
+        pl.semaphore_wait(barrier, count - 1 + len(others) + lax.rem(self.xl + self.core, 2))
+
+    def start(self, count, src, dst, outs, ins):
+        def push(k, carry):
+            send(src(k), dst, outs.at[k], ins.at[k], self.partner(k))
+            return carry
+
+        @pl.when(self.stays)
+        def _():
+            pltpu.make_async_copy(src(0), dst, ins.at[0]).start()
+
+        @pl.when(jnp.logical_not(self.stays))
+        def _():
+            push(0, 0)
+
+        lax.fori_loop(1, count, push, 0)
+
+    def end(self, k, got, outs, ins):
+        finish(got, got, outs.at[k], ins.at[k], self.partner(k))
+
+    def end_first(self, got, outs, ins):
+        @pl.when(self.stays)
+        def _():
+            pltpu.make_async_copy(got, got, ins.at[0]).wait()
+
+        @pl.when(jnp.logical_not(self.stays))
+        def _():
+            self.end(0, got, outs, ins)
+
+
+def spread_kernel(q_ref, kv_ref, qo_ref, kvo_ref, qs, qr, ks, kr, fs, fr):
+    turn = Turn()
+    y, z, xl, core = turn.y, turn.z, turn.xl, turn.core
+    turn.greet(16, (turn.sibling(),))
+    turn.start(4, lambda k: q_ref.at[turn.ahead(k)[1]], qo_ref.at[z], qs, qr)
+    turn.start(16, lambda k: kv_ref.at[turn.ahead(k)[1]], kvo_ref.at[y, z, xl], ks, kr)
+
+    def onward(k):
+        i, j = turn.behind(k)
+        piece = kvo_ref.at[i, j, core]
+        send(piece, piece, fs.at[k], fr.at[k], turn.sibling())
+
+    turn.end_first(kvo_ref.at[y, z, core], ks, kr)
+    onward(0)
+
+    def relay(k, carry):
+        i, j = turn.behind(k)
+        turn.end(k, kvo_ref.at[i, j, core], ks, kr)
+        onward(k)
+        return carry
+
+    lax.fori_loop(1, 16, relay, 0)
+    turn.end_first(qo_ref.at[z], qs, qr)
 
     def done_q(k, carry):
-        finish(q_ref.at[0], qo_ref.at[wrap(z - k, 4)], qs.at[k], qr.at[k], device(y, z, xl, core, half))
-        return carry
+        turn.end(k, qo_ref.at[turn.behind(k)[1]], qs, qr)
+        return carry
+
+    lax.fori_loop(1, 4, done_q, 0)
 
     def done(k, carry):
-        finish(kv_ref.at[0], kvo_ref.at[source(k)], ks.at[k], kr.at[k], device(y, z, xl, core, half))
+        i, j = turn.behind(k)
+        piece = kvo_ref.at[i, j, 1 - core]
+        finish(piece, piece, fs.at[k], fr.at[k], turn.sibling())
+        return carry
+
+    lax.fori_loop(0, 16, done, 0)
+
+
+def collect_kernel(q_ref, kv_ref, qo_ref, kvo_ref, other, both, qs, qr, ks, kr, fs, fr):
+    turn = Turn()
+    y, z, xl, core = turn.y, turn.z, turn.xl, turn.core
+    turn.greet(16, (turn.sibling(),))
+    for i in range(4):
+        send(kv_ref.at[i, :, 1 - core], other.at[i], fs.at[i], fr.at[i], turn.sibling())
+    turn.start(4, lambda k: q_ref.at[turn.ahead(k)[1]], qo_ref.at[z], qs, qr)
+    for i in range(4):
+        finish(other.at[i], other.at[i], fs.at[i], fr.at[i], turn.sibling())
+
+    def add(k, carry):
+        i, j = pair(k)
+        both[i, j] = (kv_ref[i, j, core].astype(F32) + other[i, j].astype(F32)).astype(BF)
+        return carry
+
+    lax.fori_loop(0, 16, add, 0)
+    turn.start(16, lambda k: both.at[turn.ahead(k)], kvo_ref.at[y, z], ks, kr)
+    turn.end_first(qo_ref.at[z], qs, qr)
+
+    def done_q(k, carry):
+        turn.end(k, qo_ref.at[turn.behind(k)[1]], qs, qr)
         return carry
 
     lax.fori_loop(1, 4, done_q, 0)
-    lax.fori_loop(1, 32, done, 0)
-    mine.wait()
-    mine_q.wait()
-
-
-def collect_kernel(q_ref, kv_ref, qo_ref, kvo_ref, local_sem, qs, qr, ks, kr):
-    y, z, xl, core, half = place()
-    me = lax.axis_index("ctx")
-    barrier = pltpu.get_barrier_semaphore()
-
-    def other(k):
-        dy, dz, dx = parts(k)
-        return wrap(y + dy, 4), wrap(z + dz, 4), wrap(xl + dx, 2)
-
-    def source(k):
-        dy, dz, dx = parts(k)
-        return (wrap(y - dy, 4) * 4 + wrap(z - dz, 4)) * 2 + wrap(xl - dx, 2)
-
-    def hello(k, carry):
-        ey, ez, ex = other(k)
-        greet(barrier, device(ey, ez, ex, core, half))
-        return carry
-
-    lax.fori_loop(1, 32, hello, 0)
-    pl.semaphore_wait(barrier, 31)
-
-    def push_q(k, carry):
-        ez = wrap(z + k, 4)
-        send(q_ref.at[ez], qo_ref.at[z], qs.at[k], qr.at[k], device(y, ez, xl, core, half))
-        return carry
-
-    def push(k, carry):
-        ey, ez, ex = other(k)
-        to = (ey * 4 + ez) * 2 + ex
-        send(kv_ref.at[to], kvo_ref.at[me], ks.at[k], kr.at[k], device(ey, ez, ex, core, half))
-        return carry
-
-    lax.fori_loop(1, 4, push_q, 0)
-    lax.fori_loop(1, 32, push, 0)
-    mine = pltpu.make_async_copy(kv_ref.at[me], kvo_ref.at[me], local_sem.at[0])
-    mine.start()
-    mine_q = pltpu.make_async_copy(q_ref.at[z], qo_ref.at[z], local_sem.at[1])
-    mine_q.start()
+    turn.end_first(kvo_ref.at[y, z], ks, kr)
+
+    def done(k, carry):
+        turn.end(k, kvo_ref.at[turn.behind(k)], ks, kr)
+        return carry
+
+    lax.fori_loop(1, 16, done, 0)
+
+
+def mates_kernel(q_ref, qo_ref, qs, qr):
+    turn = Turn()
+    turn.greet(4)
+    turn.start(4, lambda k: q_ref.at[turn.ahead(k)[1]], qo_ref.at[turn.z], qs, qr)
+    turn.end_first(qo_ref.at[turn.z], qs, qr)
 
     def done_q(k, carry):
-        finish(q_ref.at[0], qo_ref.at[wrap(z - k, 4)], qs.at[k], qr.at[k], device(y, z, xl, core, half))
-        return carry
-
-    def done(k, carry):
-        finish(kv_ref.at[0], kvo_ref.at[source(k)], ks.at[k], kr.at[k], device(y, z, xl, core, half))
+        turn.end(k, qo_ref.at[turn.behind(k)[1]], qs, qr)
         return carry
 
     lax.fori_loop(1, 4, done_q, 0)
-    lax.fori_loop(1, 32, done, 0)
-    mine.wait()
-    mine_q.wait()
-
-
-def mates_kernel(q_ref, qo_ref, local_sem, qs, qr):
-    y, z, xl, core, half = place()
-    barrier = pltpu.get_barrier_semaphore()
-
-    def hello(k, carry):
-        greet(barrier, device(y, wrap(z + k, 4), xl, core, half))
-        return carry
-
-    lax.fori_loop(1, 4, hello, 0)
-    pl.semaphore_wait(barrier, 3)
-
-    def push(k, carry):
-        ez = wrap(z + k, 4)
-        send(q_ref.at[ez], qo_ref.at[z], qs.at[k], qr.at[k], device(y, ez, xl, core, half))
-        return carry
-
-    lax.fori_loop(1, 4, push, 0)
-    mine = pltpu.make_async_copy(q_ref.at[z], qo_ref.at[z], local_sem)
-    mine.start()
-
-    def done(k, carry):
-        finish(q_ref.at[0], qo_ref.at[wrap(z - k, 4)], qs.at[k], qr.at[k], device(y, z, xl, core, half))
-        return carry
-
-    lax.fori_loop(1, 4, done, 0)
-    mine.wait()
-
-
-def exchange(kernel, name, number, pieces, blocks):
-    dma = pltpu.SemaphoreType.DMA
-    return pl.pallas_call(
-        kernel,
-        name=name,
-        out_shape=(shape(4, ROWS, 256), shape(32, ROWS, HALF)),
+
+
+def cost(us):
+    return pl.CostEstimate(flops=0, transcendentals=0, bytes_accessed=int(us * 3e6))
+
+
+def remote(number):
+    return pltpu.CompilerParams(collective_id=number, has_side_effects=True, vmem_limit_bytes=LIMIT)
+
+
+def plain():
+    return pltpu.CompilerParams(vmem_limit_bytes=LIMIT)
+
+
+DMA = pltpu.SemaphoreType.DMA
+
+
+def spread(q, kv):
+    return pl.pallas_call(
+        spread_kernel,
+        name="spread",
+        out_shape=(shape(4, ROWS, 256), shape(4, 4, 2, ROWS, HALF)),
         in_specs=[VM, VM],
         out_specs=(VM, VM),
-        scratch_shapes=[dma((2,)), dma((4,)), dma((4,)), dma((32,)), dma((32,))],
-        compiler_params=pltpu.CompilerParams(
-            collective_id=number, has_side_effects=True, vmem_limit_bytes=LIMIT
-        ),
-    )(pieces, blocks)
+        scratch_shapes=[DMA((4,)), DMA((4,)), DMA((16,)), DMA((16,)), DMA((16,)), DMA((16,))],
+        compiler_params=remote(1),
+        cost_estimate=cost(30),
+    )(q, kv)
+
+
+def collect(q, kv):
+    return pl.pallas_call(
+        collect_kernel,
+        name="collect",
+        out_shape=(shape(4, ROWS, 256), shape(4, 4, ROWS, HALF)),
+        in_specs=[VM, VM],
+        out_specs=(VM, VM),
+        scratch_shapes=[
+            pltpu.VMEM((4, 4, ROWS, HALF), BF), pltpu.VMEM((4, 4, ROWS, HALF), BF),
+            DMA((4,)), DMA((4,)), DMA((16,)), DMA((16,)), DMA((4,)), DMA((4,)),
+        ],
+        compiler_params=remote(4),
+        cost_estimate=cost(30),
+    )(q, kv)
 
 
 def mates(name, number, pieces):
-    dma = pltpu.SemaphoreType.DMA
     return pl.pallas_call(
         mates_kernel,
         name=name,
         out_shape=shape(4, ROWS, 256),
         in_specs=[VM],
         out_specs=VM,
-        scratch_shapes=[dma, dma((4,)), dma((4,))],
-        compiler_params=pltpu.CompilerParams(
-            collective_id=number, has_side_effects=True, vmem_limit_bytes=LIMIT
-        ),
+        scratch_shapes=[DMA((4,)), DMA((4,))],
+        compiler_params=remote(number),
+        cost_estimate=cost(6),
     )(pieces)
 
 
-def project_kernel(x_ref, wq, wk, wv, ra, rb, bias_ref, q_ref, kv_ref, w_ref, sems):
-    core = lax.axis_index("seq")
-    half = lax.axis_index("fsdp")
+def project_kernel(x_ref, wq, wk, wv, small, q_ref, kv_ref, w_ref, vec_ref, bi_ref, small_o, own_sem, a_out, a_in, b_out, b_in):
+    y, z, xl, core, half = place()
+    across = device(y, z, 1 - xl, core, 1 - half)
+    sibling = device(y, z, xl, 1 - core, half)
+    barrier = pltpu.get_barrier_semaphore()
+    greet(barrier, across)
+    greet(barrier, sibling)
+    pl.semaphore_wait(barrier, 2)
+    start = pl.multiple_of(core * GROUP, GROUP)
     own = pl.multiple_of(half * HALF, HALF)
-    first = pl.multiple_of((1 - half) * HALF + core * GROUP, GROUP)
-    second = pl.multiple_of((1 - half) * HALF + (1 - core) * GROUP, GROUP)
-    copies = []
+    give = pl.ds(pl.multiple_of(half * HALF + core * GROUP, GROUP), GROUP)
+    take = pl.ds(pl.multiple_of((1 - half) * HALF + core * GROUP, GROUP), GROUP)
+    last = pl.ds(pl.multiple_of((1 - half) * HALF + (1 - core) * GROUP, GROUP), GROUP)
+    send(small, small_o, a_out.at[3], a_in.at[3], across)
     for i, w in enumerate((wq, wk, wv)):
-        copies.append(pltpu.make_async_copy(w, w_ref.at[i, pl.ds(own, HALF)], sems.at[i]))
+        send(w.at[pl.ds(start, GROUP)], w_ref.at[i, give], a_out.at[i], a_in.at[i], across)
+    mine = [
+        pltpu.make_async_copy(w, w_ref.at[i, pl.ds(own, HALF)], own_sem.at[i]) for i, w in enumerate((wq, wk, wv))
+    ]
+    for copy in mine:
+        copy.start()
+    finish(small_o, small_o, a_out.at[3], a_in.at[3], across)
+    near, far = small[...].astype(F32), small_o[...].astype(F32)
+    ahead = jnp.where(half == 0, near, far)
+    behind = jnp.where(half == 0, far, near)
+    vec_ref[:, :HALF] = ahead[:8]
+    vec_ref[:, HALF:] = behind[:8]
+    for i in range(4):
+        bi_ref[:, i * HALF : (i + 1) * HALF] = ahead[8 + i : 9 + i]
+        bi_ref[:, 1536 + i * HALF : 1536 + (i + 1) * HALF] = behind[8 + i : 9 + i]
+    x = x_ref[...]
     for i in range(3):
-        copies.append(pltpu.make_async_copy(ra.at[i], w_ref.at[i, pl.ds(first, GROUP)], sems.at[3 + i]))
-        copies.append(pltpu.make_async_copy(rb.at[i], w_ref.at[i, pl.ds(second, GROUP)], sems.at[6 + i]))
-    for copy in copies:
-        copy.start()
-    for copy in copies:
-        copy.wait()
-    x = x_ref[...]
+        piece = w_ref.at[i, take]
+        finish(piece, piece, a_out.at[i], a_in.at[i], across)
+        send(piece, piece, b_out.at[i], b_in.at[i], sibling)
+    done = []
+    for i in range(3):
+        piece = w_ref.at[i, last]
+        finish(piece, piece, b_out.at[i], b_in.at[i], sibling)
+        mine[i].wait()
+        done.append(nn(x, w_ref[i]))
     pad = jnp.zeros((ROWS, 64), BF)
-    query = (nn(x, w_ref[0]) + bias_ref[0:1, :]).astype(BF) * BF(0.125)
-    for g in range(4):
-        q_ref[g] = jnp.concatenate([query[:, g * GROUP : (g + 1) * GROUP], pad], axis=1)
-    keys = nn(x, w_ref[1]).astype(BF)
-    values = (nn(x, w_ref[2]) + bias_ref[1:2, :]).astype(BF)
+    query = (done[0] + vec_ref[0:1, :]).astype(BF) * BF(0.125)
+    keys = done[1].astype(BF)
+    values = (done[2] + vec_ref[1:2, :]).astype(BF)
     for g in range(4):
         cut = slice(g * GROUP, (g + 1) * GROUP)
+        q_ref[g] = jnp.concatenate([query[:, cut], pad], axis=1)
         kv_ref[g] = jnp.concatenate([keys[:, cut], values[:, cut]], axis=1)
 
 
-def project(x, wq, wk, wv, ra, rb, bias):
+def project(x, wq, wk, wv, small):
     return pl.pallas_call(
         project_kernel,
         name="project",
-        out_shape=(shape(4, ROWS, 256), shape(4, ROWS, HALF), shape(3, D, D)),
-        in_specs=[VM, ANY, ANY, ANY, ANY, ANY, VM],
-        out_specs=(VM, VM, VM),
-        scratch_shapes=[pltpu.SemaphoreType.DMA((9,))],
-        compiler_params=pltpu.CompilerParams(vmem_limit_bytes=LIMIT),
-    )(x, wq, wk, wv, ra, rb, bias)
+        out_shape=(
+            shape(4, ROWS, 256), shape(4, ROWS, HALF), shape(3, D, D), shape(8, D, dtype=F32), shape(1, FF, dtype=F32),
+        ),
+        in_specs=[VM, ANY, ANY, ANY, VM],
+        out_specs=(VM,) * 5,
+        scratch_shapes=[pltpu.VMEM((16, HALF), BF), DMA((3,)), DMA((4,)), DMA((4,)), DMA((3,)), DMA((3,))],
+        compiler_params=remote(6),
+        cost_estimate=cost(25),
+    )(x, wq, wk, wv, small)
 
 
 CHUNK = 256
 
 
 def load_chunk(ref, i):
-    n = CHUNK // ROWS
-    return ref[pl.ds(i * n, n)].reshape(CHUNK, HALF)
+    y, z = pair(i)
+    return ref[y, z].reshape(CHUNK, HALF)
 
 
 def stack_head(ref, h):
@@ -335,13 +405,14 @@
     return pl.pallas_call(
         attend_kernel,
         name="attend",
+        cost_estimate=cost(20),
         out_shape=(shape(4, ROWS, 256), shape(3, HD, 512, dtype=F32), shape(3, 1, 512, dtype=F32)),
         in_specs=[VM, VM],
         out_specs=(VM, VM, VM),
         scratch_shapes=[
             pltpu.VMEM((3, HD, 512), BF), pltpu.VMEM((3, 1, 512), F32), pltpu.VMEM((3, 1, 512), F32),
         ],
-        compiler_params=pltpu.CompilerParams(vmem_limit_bytes=LIMIT),
+        compiler_params=plain(),
     )(q, kv)
 
 
@@ -368,8 +439,8 @@
             keys.append(nn(slopes, qs[h]).astype(BF))
             values.append(nn(probs.astype(BF), ds[h]).astype(BF))
             acc[h] += tn(k, slopes)
-        n = CHUNK // ROWS
-        dkv_ref[pl.ds(i * n, n)] = jnp.concatenate(keys + values, axis=1).reshape(n, ROWS, HALF)
+        y, z = pair(i)
+        dkv_ref[y, z] = jnp.concatenate(keys + values, axis=1).reshape(2, ROWS, HALF)
         return carry
 
     lax.fori_loop(0, 4096 // CHUNK, body, 0)
@@ -384,7 +455,8 @@
     return pl.pallas_call(
         attend_back_kernel,
         name="attend_back",
-        out_shape=(shape(4, ROWS, 256), shape(32, ROWS, HALF)),
+        cost_estimate=cost(25),
+        out_shape=(shape(4, ROWS, 256), shape(4, 4, 2, ROWS, HALF)),
         in_specs=[VM] * 5,
         out_specs=(VM, VM),
         scratch_shapes=[
@@ -392,7 +464,7 @@
             pltpu.VMEM((3, 512, HD), BF), pltpu.VMEM((3, HD, 512), BF),
             pltpu.VMEM((3, 1, 512), F32), pltpu.VMEM((3, HD, 512), F32),
         ],
-        compiler_params=pltpu.CompilerParams(vmem_limit_bytes=LIMIT),
+        compiler_params=plain(),
     )(q, kv, da, ot, lse)
 
 
@@ -414,7 +486,7 @@
 
 def block_kernel(
     x_ref, ct_ref, a_ref, wo, wo_a, wo_b, wi, wi_a, wi_b, wu, wu_a, wu_b, vec_ref, bi_ref,
-    out_ref, dh1_ref, da_ref, af_ref, yb_ref, g_ref, df_ref, du_ref, dz_ref, vg_ref, big_ref,
+    out_ref, dh1_ref, da_ref, af_ref, yb_ref, g_ref, df_ref, du_ref, dz_ref, vg_ref,
     w_o, w_i, w_u, slope, sems,
 ):
     core = lax.axis_index("seq")
@@ -463,27 +535,36 @@
     normal2, inverse2 = norm(second_in)
     out_ref[...] = (normal2 * second_gain + second_shift).astype(BF)
     upper = ct_ref[...].astype(F32)
-    vg_ref[6:7, :] = column(upper * normal2)
-    vg_ref[7:8, :] = column(upper)
+
+
+    def note(row, value):
+        for h in range(2):
+            vg_ref[h, row : row + 1, :] = value[:, h * HALF : (h + 1) * HALF]
+
+    vg_ref[...] = jnp.zeros_like(vg_ref)
+    note(6, column(upper * normal2))
+    note(7, column(upper))
     dh2 = norm_back(upper * second_gain, normal2, inverse2)
     df = dh2.astype(BF)
     df_ref[...] = df
-    vg_ref[5:6, :] = column(df.astype(F32))
+    note(5, column(df.astype(F32)))
     dy1 = dh2
     for j in range(4):
         cut = slice(j * D, (j + 1) * D)
         du = (slope[:, cut] * nt(df, w_u[cut, :])).astype(BF)
         du_ref[:, cut] = du
-        big_ref[:, cut] = column(du.astype(F32))
+        sums = column(du.astype(F32))
+        for i in range(2):
+            n = 2 * j + i
+            vg_ref[n // 4, 8 + n % 4 : 9 + n % 4, :] = sums[:, i * HALF : (i + 1) * HALF]
         dy1 = dy1 + nt(du, w_i[:, cut])
-    vg_ref[3:4, :] = column(dy1 * normal1)
-    vg_ref[4:5, :] = column(dy1)
+    note(3, column(dy1 * normal1))
+    note(4, column(dy1))
     dh1 = norm_back(dy1 * first_gain, normal1, inverse1)
     dh1_ref[...] = dh1
     dz = dh1.astype(BF)
     dz_ref[...] = dz
-    vg_ref[2:3, :] = column(dz.astype(F32))
-    vg_ref[0:2, :] = jnp.zeros((2, D), F32)
+    note(2, column(dz.astype(F32)))
     da = nt(dz, w_o[...]).astype(BF)
     pad = jnp.zeros((ROWS, 64), BF)
     for g in range(4):
@@ -494,18 +575,19 @@
     return pl.pallas_call(
         block_kernel,
         name="block",
+        cost_estimate=cost(12),
         out_shape=(
             shape(ROWS, D), shape(ROWS, D, dtype=F32), shape(4, ROWS, 256), shape(ROWS, D), shape(ROWS, D),
-            shape(ROWS, FF), shape(ROWS, D), shape(ROWS, FF), shape(ROWS, D), shape(8, D, dtype=F32),
-            shape(1, FF, dtype=F32),
+            shape(ROWS, FF), shape(ROWS, D), shape(ROWS, FF), shape(ROWS, D),
+            shape(2, 16, HALF, dtype=F32),
         ),
         in_specs=[VM, VM, VM] + [ANY] * 9 + [VM, VM],
-        out_specs=(VM,) * 11,
+        out_specs=(VM,) * 10,
         scratch_shapes=[
             pltpu.VMEM((D, D), BF), pltpu.VMEM((D, FF), BF), pltpu.VMEM((FF, D), BF),
             pltpu.VMEM((ROWS, FF), F32), pltpu.SemaphoreType.DMA((9,)),
         ],
-        compiler_params=pltpu.CompilerParams(vmem_limit_bytes=LIMIT),
+        compiler_params=plain(),
     )(x, ct, a, *weights, vec, b_inner)
 
 
@@ -538,20 +620,21 @@
     return pl.pallas_call(
         wide_kernel,
         name="wide",
+        cost_estimate=cost(6),
         out_shape=(shape(2, 4, 4, 2, 48, HALF), shape(2, 4, 4, 2, 48, HALF), shape(2, 4, 2, 48, HALF)),
         in_specs=[VM] * 12,
         out_specs=(VM, VM, VM),
-        compiler_params=pltpu.CompilerParams(vmem_limit_bytes=LIMIT),
+        compiler_params=plain(),
     )(*arrays)
 
 
-def tail_kernel(dq_ref, dkv_ref, dh1_ref, w_ref, grad_ref, low_ref, vg_ref):
+def tail_kernel(dq_ref, dkv_ref, dh1_ref, w_ref, vg_ref, grad_ref, low_ref, vo_ref):
     low_ref[0] = jnp.concatenate([dq_ref[g][:, :GROUP] for g in range(4)], axis=1)
     sums = []
     for g in range(4):
-        total = dkv_ref[2 * g].astype(F32)
-        for k in range(1, 8):
-            total = total + dkv_ref[(k // 2) * 8 + 2 * g + k % 2].astype(F32)
+        total = dkv_ref[0, g].astype(F32)
+        for k in range(1, 4):
+            total = total + dkv_ref[k, g].astype(F32)
         sums.append(total.astype(BF))
     low_ref[1] = jnp.concatenate([s[:, :GROUP] for s in sums], axis=1)
     low_ref[2] = jnp.concatenate([s[:, GROUP:] for s in sums], axis=1)
@@ -559,20 +642,23 @@
     for i in range(3):
         grad = grad + nt(low_ref[i], w_ref[i])
     grad_ref[...] = grad
-    vg_ref[...] = jnp.concatenate(
-        [column(low_ref[0].astype(F32)), column(low_ref[2].astype(F32)), jnp.zeros((6, D), F32)], axis=0
-    )
-
-
-def tail(dq, dkv, dh1, w):
+    vo_ref[...] = vg_ref[...]
+    for row, i in ((0, 0), (1, 2)):
+        value = column(low_ref[i].astype(F32))
+        for h in range(2):
+            vo_ref[h, row : row + 1, :] = value[:, h * HALF : (h + 1) * HALF]
+
+
+def tail(*arrays):
     return pl.pallas_call(
         tail_kernel,
         name="tail",
-        out_shape=(shape(ROWS, D, dtype=F32), shape(3, ROWS, D), shape(8, D, dtype=F32)),
-        in_specs=[VM] * 4,
+        out_shape=(shape(ROWS, D, dtype=F32), shape(3, ROWS, D), shape(2, 16, HALF, dtype=F32)),
+        in_specs=[VM] * 5,
         out_specs=(VM,) * 3,
-        compiler_params=pltpu.CompilerParams(vmem_limit_bytes=LIMIT),
-    )(dq, dkv, dh1, w)
+        compiler_params=plain(),
+        cost_estimate=cost(6),
+    )(*arrays)
 
 
 def narrow_kernel(x, x_o, low, low_o, attn_ref, zero_ref):
@@ -590,15 +676,16 @@
     return pl.pallas_call(
         narrow_kernel,
         name="narrow",
+        cost_estimate=cost(4),
         out_shape=shape(2, 4, 4, 2, 48, HALF),
         in_specs=[VM] * 5,
         out_specs=VM,
-        compiler_params=pltpu.CompilerParams(vmem_limit_bytes=LIMIT),
+        compiler_params=plain(),
     )(*arrays)
 
 
 def reduce_kernel(
-    g0, g1, g2, out, r0, r1, r2, s0, s1, s2, t0, t1, t2,
+    g0, g1, g2, vg, out, vo, r0, r1, r2, s0, s1, s2, t0, t1, t2, rv, sv, tv, uv,
     a_out, a_in, b_out, b_in, c_out, c_in, d_out, d_in, e_out, e_in,
 ):
     y, z, xl, core, half = place()
@@ -609,9 +696,6 @@
         e = wrap(x + k, 4)
         return device(y, z, lax.rem(e, 2), core, lax.div(e, 2))
 
-    def pair(k):
-        return lax.div(k, 4), lax.rem(k, 4)
-
     def at_yz(k):
         i, j = pair(k)
         return device(wrap(y + i, 4), wrap(z + j, 4), xl, core, half)
@@ -652,6 +736,7 @@
         send(g0.at[lax.div(e, 2), :, :, lax.rem(e, 2)], r0.at[k - 1], a_out.at[0, k], a_in.at[0, k], along_x(k))
         send(g1.at[:, wrap(y + k, 4)], r1.at[k - 1], a_out.at[1, k], a_in.at[1, k], at_yz(k * 4))
         send(g2.at[:, :, wrap(z + k, 4)], r2.at[k - 1], a_out.at[2, k], a_in.at[2, k], at_yz(k))
+        send(vg.at[lax.div(e, 2)], rv.at[k - 1], a_out.at[3, k], a_in.at[3, k], along_x(k))
         return carry
 
     lax.fori_loop(1, 4, first, 0)
@@ -683,6 +768,16 @@
         f, q, r = lax.div(i, 8), lax.rem(lax.div(i, 2), 4), lax.rem(i, 2)
         return (f, q, r), (f, q, r), g2[f, q, z, r]
 
+    for k in range(1, 4):
+        finish(rv.at[k - 1], rv.at[k - 1], a_out.at[3, k], a_in.at[3, k], here)
+    part = vg[half] + rv[0] + rv[1] + rv[2]
+    sv[...] = part.astype(BF)
+
+    def second3(k, carry):
+        send(sv, tv.at[k], b_out.at[3, k], b_in.at[3, k], at_yz(k))
+        return carry
+
+    lax.fori_loop(1, 16, second3, 0)
     sum1(own1, r1, s1, 1)
 
     def second1(k, carry):
@@ -723,6 +818,14 @@
         total = lax.fori_loop(1, 16, add, own.astype(F32))
         out[core, slab, y, z, xl] = total.astype(BF)
 
+    def done3(k, total):
+        finish(tv.at[k], tv.at[k], b_out.at[3, k], b_in.at[3, k], here)
+        return total + tv[k].astype(F32)
+
+    vo[...] = lax.fori_loop(1, 16, done3, part)
+    sibling = device(y, z, xl, 1 - core, half)
+    send(vo, uv, e_out.at[3], e_in.at[3], sibling)
+
     sum2(s1[half, z, xl], t1, 1)
 
     def third1(k, carry):
@@ -800,7 +903,6 @@
         finish(piece, piece, d_out.at[2, k], d_in.at[2, k], here)
         return carry
 
-    sibling = device(y, z, xl, 1 - core, half)
     lax.fori_loop(1, 4, last1, 0)
     send(out.at[core, 1], out.at[core, 1], e_out.at[1], e_in.at[1], sibling)
     lax.fori_loop(1, 4, last2, 0)
@@ -811,28 +913,63 @@
     for slab in (1, 2, 0):
         piece = out.at[1 - core, slab]
         finish(piece, piece, e_out.at[slab], e_in.at[slab], here)
-
-
-def reduce(g0, g1, g2):
+    finish(uv, uv, e_out.at[3], e_in.at[3], here)
+    vo[...] = vo[...] + uv[...]
+
+
+def reduce(g0, g1, g2, vg):
     dma = pltpu.SemaphoreType.DMA
     blk = (48, HALF)
     return pl.pallas_call(
         reduce_kernel,
         name="reduce",
-        out_shape=shape(2, 3, 4, 4, 2, *blk),
-        in_specs=[VM] * 3,
-        out_specs=VM,
+        out_shape=(shape(2, 3, 4, 4, 2, *blk), shape(16, HALF, dtype=F32)),
+        in_specs=[VM] * 4,
+        out_specs=(VM, VM),
         scratch_shapes=[
             pltpu.VMEM((3, 4, 4, *blk), BF), pltpu.VMEM((3, 2, 4, 2, *blk), BF), pltpu.VMEM((3, 2, 4, 2, *blk), BF),
             pltpu.VMEM((4, 4, *blk), BF), pltpu.VMEM((2, 4, 2, *blk), BF), pltpu.VMEM((2, 4, 2, *blk), BF),
             pltpu.VMEM((16, *blk), BF), pltpu.VMEM((16, *blk), BF), pltpu.VMEM((16, *blk), BF),
-            dma((3, 4)), dma((3, 4)), dma((3, 16)), dma((3, 16)), dma((3, 16)), dma((3, 16)),
-            dma((3, 4)), dma((3, 4)), dma((3,)), dma((3,)),
+            pltpu.VMEM((3, 16, HALF), F32), pltpu.VMEM((16, HALF), BF), pltpu.VMEM((16, 16, HALF), BF),
+            pltpu.VMEM((16, HALF), F32),
+            dma((4, 4)), dma((4, 4)), dma((4, 16)), dma((4, 16)), dma((3, 16)), dma((3, 16)),
+            dma((3, 4)), dma((3, 4)), dma((4,)), dma((4,)),
         ],
         compiler_params=pltpu.CompilerParams(
             collective_id=5, has_side_effects=True, vmem_limit_bytes=LIMIT
         ),
-    )(g0, g1, g2)
+        cost_estimate=cost(80),
+    )(g0, g1, g2, vg)
+
+
+def spell_kernel(zero, one, two, q_ref, k_ref, v_ref, o_ref, i_ref, u_ref):
+    for c in range(2):
+        cols = slice(c * HALF, (c + 1) * HALF)
+        for m, ref in enumerate((q_ref, k_ref, v_ref, o_ref)):
+            ref[:, cols] = zero[c, 0, m, 0].astype(F32)
+            i_ref[:, m * D + c * HALF : m * D + (c + 1) * HALF] = two[c, 0, m, 0].astype(F32)
+            u_ref[m * 48 : (m + 1) * 48, cols] = one[c, 0, 0, m].astype(F32)
+
+
+def spell(summed):
+    summed = summed.reshape(2, 3, 4, 8, 48, HALF)
+    part = pl.BlockSpec((48, D), lambda i: (i, 0))
+    return pl.pallas_call(
+        spell_kernel,
+        name="spell",
+        grid=(8,),
+        out_shape=tuple(
+            shape(*dims, dtype=F32) for dims in ((HALF, D), (HALF, D), (HALF, D), (HALF, D), (HALF, FF), (1536, D))
+        ),
+        in_specs=[
+            pl.BlockSpec((2, 1, 4, 1, 48, HALF), lambda i: (0, 0, 0, i, 0, 0)),
+            pl.BlockSpec((2, 1, 1, 4, 48, HALF), lambda i: (0, 1, i // 2, i % 2, 0, 0)),
+            pl.BlockSpec((2, 1, 4, 1, 48, HALF), lambda i: (0, 2, 0, i, 0, 0)),
+        ],
+        out_specs=(part, part, part, part, pl.BlockSpec((48, FF), lambda i: (i, 0)), pl.BlockSpec((192, D), lambda i: (i, 0))),
+        compiler_params=plain(),
+        cost_estimate=cost(6),
+    )(summed, summed, summed)
 
 
 def swap_halves(array):
@@ -860,55 +997,38 @@
     def share(w):
         return lax.dynamic_slice_in_dim(w, core * (w.shape[0] // 2), w.shape[0] // 2, 0)
 
+    rows = [b_query, b_value, b_output, first_gain, first_shift, b_outer, second_gain, second_shift]
     small = jnp.concatenate(
-        [b_query, b_value, b_output, first_gain, first_shift, b_outer, second_gain, second_shift, b_inner]
-    ).reshape(12, HALF)
-    small_o = swap_halves(small)
-    qkv_a = swap_halves(jnp.stack([share(w) for w in (w_query, w_key, w_value)]))
-    qkv_b = swap_cores(qkv_a)
-    later, qkv_a = lax.optimization_barrier((tuple(share(w) for w in (w_output, w_inner, w_outer)), qkv_a))
-    later_a = [swap_halves(w) for w in later]
-    later_b = [swap_cores(w) for w in later_a]
-
-    low_first = half == 0
-    ahead = jnp.where(low_first, small, small_o).astype(F32)
-    behind = jnp.where(low_first, small_o, small).astype(F32)
-    vec = jnp.concatenate([ahead[:8], behind[:8]], axis=1)
-    bi = jnp.concatenate([ahead[8:].reshape(1, 1536), behind[8:].reshape(1, 1536)], axis=1)
-
-    q, kv, w_qkv = project(x, w_query, w_key, w_value, qkv_a, qkv_b, vec)
-    q_all, kv_all = exchange(spread_kernel, "spread", 1, q, kv)
+        [v.reshape(1, HALF) for v in rows] + [b_inner.reshape(4, HALF), jnp.zeros((4, HALF), BF)], axis=0
+    )
+    q, kv, w_qkv, vec, bi = project(x, w_query, w_key, w_value, small)
+    later = tuple(share(w) for w in (w_output, w_inner, w_outer))
+    later, q = lax.optimization_barrier((later, q))
+    later = [swap_halves(w) for w in later]
+    q_all, kv_all = spread(q, kv)
     mixed, mixed_t, lse = attend(q_all, kv_all)
+    mixed, later = lax.optimization_barrier((mixed, later))
+    others = [swap_cores(w) for w in later]
     mixed = mates("mates_out", 2, mixed)
     weights = []
-    for own, a, b in zip((w_output, w_inner, w_outer), later_a, later_b):
+    for own, a, b in zip((w_output, w_inner, w_outer), later, others):
         weights += [own, a, b]
-    layer_out, dh1, da, a_full, yb, g, df, du, dz, vg, big = block(x, cotangent[0], mixed, weights, vec, bi)
+    layer_out, dh1, da, a_full, yb, g, df, du, dz, vg = block(x, cotangent[0], mixed, weights, vec, bi)
     da_all = mates("mates_in", 3, da)
     acts = (yb, g, a_full, df, du, dz)
     acts_o = [swap_cores(v) for v in acts]
     x_o = swap_cores(x)
     g1, g2, g0o = wide(*[v for pair in zip(acts, acts_o) for v in pair])
     dq, dkv = attend_back(q_all, kv_all, da_all, mixed_t, lse)
-    dq, dkv = exchange(collect_kernel, "collect", 4, dq, dkv)
-    tokens_grad, low, vg2 = tail(dq, dkv, dh1, w_qkv)
+    dq, dkv = collect(dq, dkv)
+    tokens_grad, low, vg = tail(dq, dkv, dh1, w_qkv, vg)
     low_o = swap_cores(low)
     g0 = narrow(x, x_o, low, low_o, g0o)
-    summed = reduce(g0, g1, g2)
-
-    vectors = jnp.concatenate([vg + vg2, big.reshape(4, D)], axis=0)
-    vectors = lax.psum(vectors, AXES)
-    vecs = lax.dynamic_slice_in_dim(vectors[:8], half * HALF, HALF, 1)
-    b_inner_grad = lax.dynamic_slice_in_dim(vectors[8:].reshape(FF), half * 1536, 1536, 0)
-
-    full = jnp.concatenate(
-        [summed[0].reshape(3, 1536, HALF), summed[1].reshape(3, 1536, HALF)], axis=2
-    ).astype(F32)
-    inner = full[2].reshape(4, HALF, D).transpose(1, 0, 2).reshape(HALF, FF)
+    summed, vecs = reduce(g0, g1, g2, vg)
+    gq, gk, gv, go, gi, gu = spell(summed)
     return (
-        layer_out[None], tokens_grad[None],
-        full[0, :HALF], full[0, HALF : 2 * HALF], full[0, 2 * HALF : 3 * HALF], full[0, 3 * HALF :],
-        vecs[0], vecs[1], vecs[2], vecs[3], vecs[4], inner, b_inner_grad, full[1], vecs[5], vecs[6], vecs[7],
+        layer_out[None], tokens_grad[None], gq, gk, gv, go,
+        vecs[0], vecs[1], vecs[2], vecs[3], vecs[4], gi, vecs[8:12].reshape(1536), gu, vecs[5], vecs[6], vecs[7],
     )
 
 

time: 500 us -> 332 us (0.66)
  waiting for transfers between devices: 69.8 us -> 2.62 us
  blocking collectives: 66.6 us -> 0 us
  starting transfers between devices: 26.6 us -> 7.5 us
  other arithmetic: 9.51 us -> 0 us
  local copies, waits for them, and re-layouts: 30.6 us -> 22.5 us
    ppermute x5 -> x3, waiting for transfers between devices: 68.4 us -> 0.01 us  [swap_halves(): return lax.ppermute(array, AXES, pairs)]
    psum x1 -> x0, blocking collectives: 66.6 us -> none  [local(): vectors = lax.psum(vectors, AXES)]
    pallas_call x8 -> x9, Pallas kernels: 269 us -> 243 us  [the longest x1 89.5 us: reduce(): pl.pallas_call(reduce_kernel, name='reduce', out_shape=(shape(2, 3, 4, 4,...]
    pallas_call x1, Pallas kernels: 5.58 us -> 29.6 us  [project(): pl.pallas_call(project_kernel, name='project', out_shape=(shape(4, ROWS,...]
    ppermute x12 -> x11, starting transfers between devices: 14.9 us -> 2.74 us  [swap_cores(): return lax.ppermute(array, 'seq', [(0, 1), (1, 0)])]
    unnamed x61 -> x38, local copies, waits for them, and re-layouts: 16.1 us -> 4.11 us
    ppermute x5 -> x3, starting transfers between devices: 11.6 us -> 4.76 us  [swap_halves(): return lax.ppermute(array, AXES, pairs)]
    reshape x4 -> x10, local copies, waits for them, and re-layouts: 3.6 us -> 9.72 us  [the longest x8 8.41 us: local(): v.reshape(1, HALF)]
  transfers between devices with their start and end apart: 17 -> 14, of which waited for: 6 -> 3; matrix products, arithmetic and copies ran while one was open for 4% -> 0% of each run, Pallas kernels for 39% -> 46%
where the time goes in v2:
time: 332 us; the launch traced here: 331 us
  Pallas kernels  297 us (89%)
  local copies, waits for them, and re-layouts  22.5 us (7%)
  starting transfers between devices  7.5 us (2%)
    pallas_call x1, Pallas kernels, reduce(): pl.pallas_call(reduce_kernel, name='reduce', out_shape=(shape(2, 3, 4, 4,...  89.5 us
    pallas_call x1, Pallas kernels, spread(): pl.pallas_call(spread_kernel, name='spread', out_shape=(shape(4, ROWS, 25...  39.9 us
    pallas_call x1, Pallas kernels, collect(): pl.pallas_call(collect_kernel, name='collect', out_shape=(shape(4, ROWS,...  36 us
    pallas_call x1, Pallas kernels, project(): pl.pallas_call(project_kernel, name='project', out_shape=(shape(4, ROWS,...  29.6 us
    pallas_call x1, Pallas kernels, attend_back(): pl.pallas_call(attend_back_kernel, name='attend_back', cost_estimate=cost...  25.3 us
    pallas_call x1, Pallas kernels, attend(): pl.pallas_call(attend_kernel, name='attend', cost_estimate=cost(20), out_...  20.7 us
    pallas_call x2, Pallas kernels, mates(): pl.pallas_call(mates_kernel, name=name, out_shape=shape(4, ROWS, 256), in...  20.2 us
    pallas_call x1, Pallas kernels, block(): pl.pallas_call(block_kernel, name='block', cost_estimate=cost(12), out_sh...  11.9 us
  transfers between devices with their start and end apart: 14, of which 3 were waited for; matrix products, arithmetic and copies ran while one was open for 0% of the time, Pallas kernels for 46%

profile of v2, /device:TPU:1, one launch (start us, length us, event | category | flops | bytes accessed | tf_op | source)
XLA Modules:
  0.0 330.6 jit_solution(13506569667530341890)
XLA Ops:
  0.7 0.8 reshape.67
  1.5 0.7 reshape.68
  2.9 1.2 reshape.70
  4.1 1.2 reshape.71
  5.4 1.2 reshape.72
  6.6 1.2 reshape.73
  7.8 1.2 reshape.74
  9.1 0.7 reshape.75
  9.8 1.7 constant_dynamic-slice_fusion.2
  11.5 1.3 constant_dynamic-slice_fusion.1
  12.8 1.1 constant_dynamic-slice_fusion
  13.9 2.0 concatenate.3.small
  15.9 29.6 %project.1 = (bf16[4,128,256]{2,1,0:T(8,128)(2,1)}, bf16[4,128,384]{2,1,0:T(8,128)(2,1)}, bf16[3,768,768]{2,1,0:T(8,128)(2,1)}, f32[8,768]{1,0:T(8,128)}, f32[1,3072]{1,0:T(1,128)}) custom-call(bf16[128,768]{1,0:T(8,128)(2,1)} %bitcast.8, bf16[384,768]{1,0:T(8,128)(2,1)} %wq.1, bf16[384,768]{1,0:T(8,128)(2,1)} %wk.1, bf16[384,768]{1,0:T(8,128)(2,1)} %wv.1, ...), custom_call_target="tpu_custom_call" | custom-call | bytes 75000000 | tf_op jit(solution)/shard_map/project/pallas_call | solution.py:340
  45.5 2.1 collective-permute-start.1
  48.3 2.0 collective-permute-start
  50.3 39.9 %spread.1 = (bf16[4,128,256]{2,1,0:T(8,128)(2,1)}, bf16[4,4,2,128,384]{4,3,2,1,0:T(8,128)(2,1)}) custom-call(bf16[4,128,256]{2,1,0:T(8,128)(2,1)} %get-tuple-element.64.q_ref, bf16[4,128,384]{2,1,0:T(8,128)(2,1)} %get-tuple-element.65.kv_ref), custom_call_target="tpu_custom_call" | custom-call | bytes 90000000 | tf_op jit(solution)/shard_map/spread/pallas_call | solution.py:247
  90.2 20.7 %attend.1 = (bf16[4,128,256]{2,1,0:T(8,128)(2,1)}, f32[3,64,512]{2,1,0:T(8,128)}, f32[3,1,512]{2,1,0:T(1,128)}) custom-call(bf16[4,128,256]{2,1,0:T(8,128)(2,1)} %get-tuple-element.66.q_ref, bf16[4,4,2,128,384]{4,3,2,1,0:T(8,128)(2,1)} %get-tuple-element.67.kv_ref), custom_call_target="tpu_custom_call" | custom-call | bytes 60000000 | tf_op jit(solution)/shard_map/attend/pallas_call | solution.py:405
  111.9 9.9 %mates_out.1.a_ref = bf16[4,128,256]{2,1,0:T(8,128)(2,1)} custom-call(bf16[4,128,256]{2,1,0:T(8,128)(2,1)} %get-tuple-element.72.q_ref), custom_call_target="tpu_custom_call" | custom-call | bytes 18000000 | tf_op jit(solution)/shard_map/mates_out/pallas_call | solution.py:276
  123.3 11.9 %block.1 = (bf16[128,768]{1,0:T(8,128)(2,1)}, f32[128,768]{1,0:T(8,128)}, bf16[4,128,256]{2,1,0:T(8,128)(2,1)}, bf16[128,768]{1,0:T(8,128)(2,1)}, bf16[128,768]{...) custom-call(bf16[128,768]{1,0:T(8,128)(2,1)} %bitcast.9, ...), custom_call_target="tpu_custom_call" | custom-call | bytes 36000000 | tf_op jit(solution)/shard_map/block/pallas_call | solution.py:575
  136.0 10.2 %mates_in.1.da_ref = bf16[4,128,256]{2,1,0:T(8,128)(2,1)} custom-call(bf16[4,128,256]{2,1,0:T(8,128)(2,1)} %get-tuple-element.79.q_ref), custom_call_target="tpu_custom_call" | custom-call | bytes 18000000 | tf_op jit(solution)/shard_map/mates_in/pallas_call | solution.py:276
  146.2 25.3 %attend_back.1 = (bf16[4,128,256]{2,1,0:T(8,128)(2,1)}, bf16[4,4,2,128,384]{4,3,2,1,0:T(8,128)(2,1)}) custom-call(bf16[4,128,256]{2,1,0:T(8,128)(2,1)} %get-tuple-element.66.q_ref, bf16[4,4,2,128,384]{4,3,2,1,0:T(8,128)(2,1)} %get-tuple-element.67.kv_ref, bf16[4,128,256]{2,1,0:T(8,128)(2,1)} %mates_in.1.da_ref, f32[3,64,512]{2,1,0:T(8,128)} %get-tuple-element.80.ot_ref, ...), custom_call_target="tpu_custom_call" | custom-call | bytes 75000000 | tf_op jit(solution)/shard_map/attend_back/pallas_call | solution.py:455
  171.5 36.0 %collect.1 = (bf16[4,128,256]{2,1,0:T(8,128)(2,1)}, bf16[4,4,128,384]{3,2,1,0:T(8,128)(2,1)}) custom-call(bf16[4,128,256]{2,1,0:T(8,128)(2,1)} %get-tuple-element.82.q_ref, bf16[4,4,2,128,384]{4,3,2,1,0:T(8,128)(2,1)} %get-tuple-element.83.kv_ref), custom_call_target="tpu_custom_call" | custom-call | bytes 90000000 | tf_op jit(solution)/shard_map/collect/pallas_call | solution.py:260
  207.5 4.7 %tail.1 = (f32[128,768]{1,0:T(8,128)}, bf16[3,128,768]{2,1,0:T(8,128)(2,1)}, f32[2,16,384]{2,1,0:T(8,128)}) custom-call(bf16[4,128,256]{2,1,0:T(8,128)(2,1)} %get-tuple-element.84.dq_ref, bf16[4,4,128,384]{3,2,1,0:T(8,128)(2,1)} %get-tuple-element.85.dkv_ref, f32[128,768]{1,0:T(8,128)} %get-tuple-element.86.dh1_ref, ...), custom_call_target="tpu_custom_call" | custom-call | bytes 18000000 | tf_op jit(solution)/shard_map/tail/pallas_call | solution.py:653
  212.9 1.6 collective-permute-done.10.a_o
  215.1 0.8 collective-permute-done.13.dz_o
  216.9 0.9 copy-done.7
  217.7 6.2 %wide.1 = (bf16[2,4,4,2,48,384]{5,4,3,2,1,0:T(8,128)(2,1)}, bf16[2,4,4,2,48,384]{5,4,3,2,1,0:T(8,128)(2,1)}, bf16[2,4,2,48,384]{4,3,2,1,0:T(8,128)(2,1)}) custom-call(bf16[128,768]{1,0:T(8,128)(2,1)} %get-tuple-element.91.yb, bf16[128,768]{1,0:T(8,128)(2,1)} %copy-done.14, bf16[128,3072]{1,0:T(8,128)(2,1)} %get-tuple-element.92.g, ...), custom_call_target="tpu_custom_call" | custom-call | bytes 18000000 | tf_op jit(solution)/shard_map/wide/pallas_call | solution.py:620
  224.9 3.9 %narrow.1.g0 = bf16[2,4,4,2,48,384]{5,4,3,2,1,0:T(8,128)(2,1)} custom-call(bf16[128,768]{1,0:T(8,128)(2,1)} %bitcast.10, bf16[128,768]{1,0:T(8,128)(2,1)} %copy-done.17, bf16[3,128,768]{2,1,0:T(8,128)(2,1)} %get-tuple-element.90.low, bf16[3,128,768]{2,1,0:T(8,128)(2,1)} %copy-done.8, bf16[2,4,2,48,384]{4,3,2,1,0:T(8,128)(2,1)} %get-tuple-element.97.attn_ref), custom_call_target="tpu_custom_call" | custom-call | bytes 12000000 | tf_op jit(solution)/shard_map/narrow/pallas_call | solution.py:676
  228.7 89.5 %reduce.17 = (bf16[2,3,4,4,2,48,384]{6,5,4,3,2,1,0:T(8,128)(2,1)}, f32[16,384]{1,0:T(8,128)}) custom-call(bf16[2,4,4,2,48,384]{5,4,3,2,1,0:T(8,128)(2,1)} %narrow.1.g0, bf16[2,4,4,2,48,384]{5,4,3,2,1,0:T(8,128)(2,1)} %get-tuple-element.98.g1, bf16[2,4,4,2,48,384]{5,4,3,2,1,0:T(8,128)(2,1)} %get-tuple-element.99.g2, f32[2,16,384]{2,1,0:T(8,128)} %get-tuple-element.100.vg), custom_call_target="tpu_custom_call" | custom-call | bytes 240000000 | tf_op jit(solution)/shard_map/reduce/pallas_call | solution.py:923
  318.2 0.7 slice.32
  318.9 1.8 slice_reduce_fusion
  321.3 9.3 %spell.1 = (f32[384,768]{1,0:T(8,128)}, f32[384,768]{1,0:T(8,128)}, f32[384,768]{1,0:T(8,128)}, f32[384,768]{1,0:T(8,128)}, f32[384,3072]{1,0:T(8,128)}, /*index=5*/f32[1536,768]{1,0:T(8,128)}) custom-call(bf16[2,3,4,8,48,384]{5,4,3,2,1,0:T(8,128)(2,1)} %bitcast.5, bf16[2,3,4,8,48,384]{5,4,3,2,1,0:T(8,128)(2,1)} %bitcast.6, ...), custom_call_target="tpu_custom_call" | custom-call | bytes 18000000 | tf_op jit(solution)/shard_map/spell/pallas_call | solution.py:957
  (64 shorter events, 8.1 us)
Async XLA Ops:
  0.7 12.2 %copy-start = (bf16[1536,768]{1,0:T(8,128)(2,1)S(1)}, bf16[1536,768]{1,0:T(8,128)(2,1)}, u32[]{:S(2)}) copy-start(bf16[1536,768]{1,0:T(8,128)(2,1)} %wu.1) | copy-start | bytes 7077892
  45.5 65.3 %collective-permute-start.1 = (bf16[192,3072]{1,0:T(8,128)(2,1)S(1)}, bf16[192,3072]{1,0:T(8,128)(2,1)S(1)}, u32[]{:S(2)}, u32[]{:S(2)}) collective-permute-start(bf16[192,3072]{1,0:T(8,128)(2,1)S(1)} %constant_dynamic-slice_fusion.1), channel_id=1, source_target_pairs={{0,5},{1,4},{2,7},{3,6},{4,1},{5,0},{6,3},{7,2},{8,13},{9,12},{10,... | collective-permute-start | bytes 3538952 | tf_op jit(solution)/shard_map/ppermute | solution.py:982
  47.6 63.3 %collective-permute-start.2 = (bf16[768,768]{1,0:T(8,128)(2,1)}, bf16[768,768]{1,0:T(8,128)(2,1)S(1)}, u32[]{:S(2)}, u32[]{:S(2)}) collective-permute-start(bf16[768,768]{1,0:T(8,128)(2,1)} %constant_dynamic-slice_fusion), channel_id=1, source_target_pairs={{0,5},{1,4},{2,7},{3,6},{4,1},{5,0},{6,3},{7,2},{8,13},{9,12},{10,... | collective-permute-start | bytes 3538952 | tf_op jit(solution)/shard_map/ppermute | solution.py:982
  48.3 62.6 %collective-permute-start = (bf16[192,768]{1,0:T(8,128)(2,1)}, bf16[192,768]{1,0:T(8,128)(2,1)S(1)}, u32[]{:S(2)}, u32[]{:S(2)}) collective-permute-start(bf16[192,768]{1,0:T(8,128)(2,1)} %constant_dynamic-slice_fusion.2), channel_id=1, source_target_pairs={{0,5},{1,4},{2,7},{3,6},{4,1},{5,0},{6,3},{7,2},{8,13},{9,12},{10,... | collective-permute-start | bytes 884744 | tf_op jit(solution)/shard_map/ppermute | solution.py:982
  110.9 11.0 %copy-start.9 = (bf16[192,768]{1,0:T(8,128)(2,1)}, bf16[192,768]{1,0:T(8,128)(2,1)S(1)}, u32[]{:S(2)}) copy-start(bf16[192,768]{1,0:T(8,128)(2,1)S(1)} %collective-permute-done.wo_a) | copy-start | bytes 884740
  110.9 11.0 %copy-start.2 = (bf16[192,3072]{1,0:T(8,128)(2,1)}, bf16[192,3072]{1,0:T(8,128)(2,1)S(1)}, u32[]{:S(2)}) copy-start(bf16[192,3072]{1,0:T(8,128)(2,1)S(1)} %collective-permute-done.1.wi_a) | copy-start | bytes 3538948
  110.9 11.0 %copy-start.3 = (bf16[768,768]{1,0:T(8,128)(2,1)}, bf16[768,768]{1,0:T(8,128)(2,1)S(1)}, u32[]{:S(2)}) copy-start(bf16[768,768]{1,0:T(8,128)(2,1)S(1)} %collective-permute-done.2.wu_a) | copy-start | bytes 3538948
  110.9 10.9 %collective-permute-start.4 = (bf16[192,3072]{1,0:T(8,128)(2,1)S(1)}, bf16[192,3072]{1,0:T(8,128)(2,1)S(1)}, u32[]{:S(2)}, u32[]{:S(2)}) collective-permute-start(bf16[192,3072]{1,0:T(8,128)(2,1)S(1)} %collective-permute-done.1.wi_a), channel_id=1, source_target_pairs={{0,2},{2,0},{1,3},{3,1},{4,6},{6,4},{5,7},{7,5},{8,10},{10,8},{9,1... | collective-permute-start | bytes 3538952 | tf_op jit(solution)/shard_map/ppermute | solution.py:986
  111.3 10.5 %collective-permute-start.5 = (bf16[768,768]{1,0:T(8,128)(2,1)S(1)}, bf16[768,768]{1,0:T(8,128)(2,1)S(1)}, u32[]{:S(2)}, u32[]{:S(2)}) collective-permute-start(bf16[768,768]{1,0:T(8,128)(2,1)S(1)} %collective-permute-done.2.wu_a), channel_id=1, source_target_pairs={{0,2},{2,0},{1,3},{3,1},{4,6},{6,4},{5,7},{7,5},{8,10},{10,8},{9,1... | collective-permute-start | bytes 3538952 | tf_op jit(solution)/shard_map/ppermute | solution.py:986
  111.5 10.3 %collective-permute-start.3 = (bf16[192,768]{1,0:T(8,128)(2,1)S(1)}, bf16[192,768]{1,0:T(8,128)(2,1)S(1)}, u32[]{:S(2)}, u32[]{:S(2)}) collective-permute-start(bf16[192,768]{1,0:T(8,128)(2,1)S(1)} %collective-permute-done.wo_a), channel_id=1, source_target_pairs={{0,2},{2,0},{1,3},{3,1},{4,6},{6,4},{5,7},{7,5},{8,10},{10,8},{9,1... | collective-permute-start | bytes 884744 | tf_op jit(solution)/shard_map/ppermute | solution.py:986
  121.8 0.7 copy-start.10
  121.8 1.1 copy-start.4
  121.9 1.5 copy-start.5
  135.3 80.7 %collective-permute-start.9 = (bf16[128,3072]{1,0:T(8,128)(2,1)}, bf16[128,3072]{1,0:T(8,128)(2,1)S(1)}, u32[]{:S(2)}, u32[]{:S(2)}) collective-permute-start(bf16[128,3072]{1,0:T(8,128)(2,1)} %get-tuple-element.92.g), channel_id=1, source_target_pairs={{0,2},{2,0},{1,3},{3,1},{4,6},{6,4},{5,7},{7,5},{8,10},{10,8},{9,1... | collective-permute-start | bytes 2359304 | tf_op jit(solution)/shard_map/ppermute | solution.py:986
  135.4 80.6 %collective-permute-start.12 = (bf16[128,3072]{1,0:T(8,128)(2,1)}, bf16[128,3072]{1,0:T(8,128)(2,1)S(1)}, u32[]{:S(2)}, u32[]{:S(2)}) collective-permute-start(bf16[128,3072]{1,0:T(8,128)(2,1)} %get-tuple-element.95.du), channel_id=1, source_target_pairs={{0,2},{2,0},{1,3},{3,1},{4,6},{6,4},{5,7},{7,5},{8,10},{10,8},{9,1... | collective-permute-start | bytes 2359304 | tf_op jit(solution)/shard_map/ppermute | solution.py:986
  135.9 76.8 %collective-permute-start.8 = (bf16[128,768]{1,0:T(8,128)(2,1)}, bf16[128,768]{1,0:T(8,128)(2,1)S(1)}, u32[]{:S(2)}, u32[]{:S(2)}) collective-permute-start(bf16[128,768]{1,0:T(8,128)(2,1)} %get-tuple-element.91.yb), channel_id=1, source_target_pairs={{0,2},{2,0},{1,3},{3,1},{4,6},{6,4},{5,7},{7,5},{8,10},{10,8},{9,1... | collective-permute-start | bytes 589832 | tf_op jit(solution)/shard_map/ppermute | solution.py:986
  207.5 4.7 %copy-start.11 = (bf16[128,768]{1,0:T(8,128)(2,1)S(1)}, bf16[128,768]{1,0:T(8,128)(2,1)}, u32[]{:S(2)}) copy-start(bf16[128,768]{1,0:T(8,128)(2,1)} %get-tuple-element.93.a) | copy-start | bytes 589828
  207.5 5.2 %copy-start.12 = (bf16[128,768]{1,0:T(8,128)(2,1)S(1)}, bf16[128,768]{1,0:T(8,128)(2,1)}, u32[]{:S(2)}) copy-start(bf16[128,768]{1,0:T(8,128)(2,1)} %get-tuple-element.94.df) | copy-start | bytes 589828
  207.5 7.0 %copy-start.13 = (bf16[128,768]{1,0:T(8,128)(2,1)S(1)}, bf16[128,768]{1,0:T(8,128)(2,1)}, u32[]{:S(2)}) copy-start(bf16[128,768]{1,0:T(8,128)(2,1)} %get-tuple-element.96.dz) | copy-start | bytes 589828
  207.5 7.2 %copy-start.1 = (bf16[1,128,768]{2,1,0:T(8,128)(2,1)S(1)}, bf16[1,128,768]{2,1,0:T(8,128)(2,1)}, u32[]{:S(2)}) copy-start(bf16[1,128,768]{2,1,0:T(8,128)(2,1)} %param.17) | copy-start | bytes 589828
  212.2 11.8 %collective-permute-start.7 = (bf16[3,128,768]{2,1,0:T(8,128)(2,1)}, bf16[3,128,768]{2,1,0:T(8,128)(2,1)S(1)}, u32[]{:S(2)}, u32[]{:S(2)}) collective-permute-start(bf16[3,128,768]{2,1,0:T(8,128)(2,1)} %get-tuple-element.90.low), channel_id=1, source_target_pairs={{0,2},{2,0},{1,3},{3,1},{4,6},{6,4},{5,7},{7,5},{8,10},{10,8},{9,1... | collective-permute-start | bytes 1769480 | tf_op jit(solution)/shard_map/ppermute | solution.py:986
  212.2 2.3 collective-permute-start.10
  212.7 3.2 copy-start.14
  212.7 2.0 collective-permute-start.11
  214.5 1.5 copy-start.15
  214.5 1.4 collective-permute-start.13
  214.8 1.2 copy-start.16
  214.8 9.2 %collective-permute-start.6 = (bf16[128,768]{1,0:T(8,128)(2,1)S(1)}, bf16[128,768]{1,0:T(8,128)(2,1)S(1)}, u32[]{:S(2)}, u32[]{:S(2)}) collective-permute-start(bf16[128,768]{1,0:T(8,128)(2,1)S(1)} %bitcast.11), channel_id=1, source_target_pairs={{0,2},{2,0},{1,3},{3,1},{4,6},{6,4},{5,7},{7,5},{8,10},{10,8},{9,1... | collective-permute-start | bytes 589832 | tf_op jit(solution)/shard_map/ppermute | solution.py:986
  215.9 0.7 copy-start.18
  215.9 0.9 copy-start.6
  216.9 0.9 copy-start.7
  224.0 0.9 copy-start.8
  (1 other events, 0.7 us)

commit v3 on v2

--- a/solution.py
+++ b/solution.py
@@ -18,13 +18,25 @@
 HD = 64
 ROWS = 128
 EPS = 1e-12
-LIMIT = 56 << 20
+LIMIT = 24 << 20
 VM = pl.BlockSpec(memory_space=pltpu.VMEM)
-ANY = pl.BlockSpec(memory_space=pl.ANY)
+ANY = pl.BlockSpec(memory_space=pltpu.HBM)
+
+
+def plain_shape(*dims, dtype=BF):
+    return jax.ShapeDtypeStruct(dims, dtype)
 
 
 def shape(*dims, dtype=BF):
-    return jax.ShapeDtypeStruct(dims, dtype)
+    return pltpu.VMEM(dims, dtype)
+
+
+def hbm(array):
+    return pltpu.with_memory_space_constraint(array, pltpu.HBM)
+
+
+def vm(array):
+    return pltpu.with_memory_space_constraint(array, pltpu.VMEM)
 
 
 def nn(left, right):
@@ -98,14 +110,14 @@
     def sibling(self):
         return device(self.y, self.z, self.xl, 1 - self.core, self.half)
 
-    def greet(self, count, others=()):
+    def hello(self, count, others=()):
         barrier = pltpu.get_barrier_semaphore()
 
-        def hello(k, carry):
+        def one(k, carry):
             greet(barrier, self.partner(k))
             return carry
 
-        lax.fori_loop(1, count, hello, 0)
+        lax.fori_loop(1, count, one, 0)
         for where in others:
             greet(barrier, where)
 
@@ -113,7 +125,9 @@
         def _():
             greet(barrier, self.partner(0))
 
-        pl.semaphore_wait(barrier, count - 1 + len(others) + lax.rem(self.xl + self.core, 2))
+    def ready(self, count, others=0):
+        barrier = pltpu.get_barrier_semaphore()
+        pl.semaphore_wait(barrier, count - 1 + others + lax.rem(self.xl + self.core, 2))
 
     def start(self, count, src, dst, outs, ins):
         def push(k, carry):
@@ -143,49 +157,11 @@
             self.end(0, got, outs, ins)
 
 
-def spread_kernel(q_ref, kv_ref, qo_ref, kvo_ref, qs, qr, ks, kr, fs, fr):
-    turn = Turn()
-    y, z, xl, core = turn.y, turn.z, turn.xl, turn.core
-    turn.greet(16, (turn.sibling(),))
-    turn.start(4, lambda k: q_ref.at[turn.ahead(k)[1]], qo_ref.at[z], qs, qr)
-    turn.start(16, lambda k: kv_ref.at[turn.ahead(k)[1]], kvo_ref.at[y, z, xl], ks, kr)
-
-    def onward(k):
-        i, j = turn.behind(k)
-        piece = kvo_ref.at[i, j, core]
-        send(piece, piece, fs.at[k], fr.at[k], turn.sibling())
-
-    turn.end_first(kvo_ref.at[y, z, core], ks, kr)
-    onward(0)
-
-    def relay(k, carry):
-        i, j = turn.behind(k)
-        turn.end(k, kvo_ref.at[i, j, core], ks, kr)
-        onward(k)
-        return carry
-
-    lax.fori_loop(1, 16, relay, 0)
-    turn.end_first(qo_ref.at[z], qs, qr)
-
-    def done_q(k, carry):
-        turn.end(k, qo_ref.at[turn.behind(k)[1]], qs, qr)
-        return carry
-
-    lax.fori_loop(1, 4, done_q, 0)
-
-    def done(k, carry):
-        i, j = turn.behind(k)
-        piece = kvo_ref.at[i, j, 1 - core]
-        finish(piece, piece, fs.at[k], fr.at[k], turn.sibling())
-        return carry
-
-    lax.fori_loop(0, 16, done, 0)
-
-
 def collect_kernel(q_ref, kv_ref, qo_ref, kvo_ref, other, both, qs, qr, ks, kr, fs, fr):
     turn = Turn()
     y, z, xl, core = turn.y, turn.z, turn.xl, turn.core
-    turn.greet(16, (turn.sibling(),))
+    turn.hello(16, (turn.sibling(),))
+    turn.ready(16, 1)
     for i in range(4):
         send(kv_ref.at[i, :, 1 - core], other.at[i], fs.at[i], fr.at[i], turn.sibling())
     turn.start(4, lambda k: q_ref.at[turn.ahead(k)[1]], qo_ref.at[z], qs, qr)
@@ -215,19 +191,6 @@
     lax.fori_loop(1, 16, done, 0)
 
 
-def mates_kernel(q_ref, qo_ref, qs, qr):
-    turn = Turn()
-    turn.greet(4)
-    turn.start(4, lambda k: q_ref.at[turn.ahead(k)[1]], qo_ref.at[turn.z], qs, qr)
-    turn.end_first(qo_ref.at[turn.z], qs, qr)
-
-    def done_q(k, carry):
-        turn.end(k, qo_ref.at[turn.behind(k)[1]], qs, qr)
-        return carry
-
-    lax.fori_loop(1, 4, done_q, 0)
-
-
 def cost(us):
     return pl.CostEstimate(flops=0, transcendentals=0, bytes_accessed=int(us * 3e6))
 
@@ -241,19 +204,6 @@
 
 
 DMA = pltpu.SemaphoreType.DMA
-
-
-def spread(q, kv):
-    return pl.pallas_call(
-        spread_kernel,
-        name="spread",
-        out_shape=(shape(4, ROWS, 256), shape(4, 4, 2, ROWS, HALF)),
-        in_specs=[VM, VM],
-        out_specs=(VM, VM),
-        scratch_shapes=[DMA((4,)), DMA((4,)), DMA((16,)), DMA((16,)), DMA((16,)), DMA((16,))],
-        compiler_params=remote(1),
-        cost_estimate=cost(30),
-    )(q, kv)
 
 
 def collect(q, kv):
@@ -269,45 +219,176 @@
         ],
         compiler_params=remote(4),
         cost_estimate=cost(30),
-    )(q, kv)
-
-
-def mates(name, number, pieces):
-    return pl.pallas_call(
-        mates_kernel,
-        name=name,
-        out_shape=shape(4, ROWS, 256),
-        in_specs=[VM],
-        out_specs=VM,
-        scratch_shapes=[DMA((4,)), DMA((4,))],
-        compiler_params=remote(number),
-        cost_estimate=cost(6),
-    )(pieces)
-
-
-def project_kernel(x_ref, wq, wk, wv, small, q_ref, kv_ref, w_ref, vec_ref, bi_ref, small_o, own_sem, a_out, a_in, b_out, b_in):
-    y, z, xl, core, half = place()
-    across = device(y, z, 1 - xl, core, 1 - half)
-    sibling = device(y, z, xl, 1 - core, half)
+    )(vm(q), vm(kv))
+
+
+CHUNK = 256
+
+
+def load_chunk(ref, at):
+    return ref[at].reshape(CHUNK, HALF)
+
+
+def stack_head(ref, h):
+    return jnp.concatenate([ref[i][:, h * HD : (h + 1) * HD] for i in range(4)], axis=0)
+
+
+def turned(rows):
+    return rows.astype(F32).T.astype(BF)
+
+
+class Fetch:
+    def __init__(self, turn, sources, fulls, own, sems):
+        self.core, self.half = turn.core, turn.half
+        y, z, xl = turn.y, turn.z, turn.xl
+        self.odd = (lax.rem(y, 2), lax.rem(z, 2), xl)
+        self.across = device(y, z, 1 - xl, turn.core, 1 - turn.half)
+        self.beside = (
+            device(y + 1 - 2 * self.odd[0], z, xl, turn.core, turn.half),
+            device(y, z + 1 - 2 * self.odd[1], xl, turn.core, turn.half),
+            device(y, z, 1 - xl, turn.core, turn.half),
+        )
+        self.sibling = turn.sibling()
+        self.sources, self.fulls, self.own = sources, fulls, own
+        self.sizes = (HALF, FF // 2, HALF)
+        self.xs, self.xr, self.ys, self.yr, self.ds, self.dr, self.es, self.er = sems
+
+    def rows(self, n, c, odd):
+        size = self.sizes[n]
+        if n == 2:
+            return odd * (size // 2), size // 2
+        return c * (size // 6) + odd * (size // 12), size // 12
+
+    def piece(self, n, half, c, odd):
+        start, size = self.rows(n, c, odd)
+        return self.fulls[n].at[pl.ds(pl.multiple_of(half * self.sizes[n] + start, 32), size)]
+
+    def each(self, act, flip=False):
+        pl.when(self.core == (1 if flip else 0))(lambda: act(0))
+        pl.when(self.core == (0 if flip else 1))(lambda: act(1))
+
+    def keep(self):
+        for n in range(3):
+            rows = self.fulls[n].at[pl.ds(pl.multiple_of(self.half * self.sizes[n], 32), self.sizes[n])]
+            yield pltpu.make_async_copy(self.sources[n], rows, self.own.at[n])
+
+    def give(self, n, c, slot):
+        odd = 1 - self.odd[2] if c % 3 == 2 else self.odd[c % 3]
+        start, size = self.rows(n, c, odd)
+        src = self.sources[n].at[pl.ds(pl.multiple_of(start, 32), size)]
+        send(src, self.piece(n, self.half, c, odd), self.xs.at[slot], self.xr.at[slot], self.across)
+
+    def own_rows(self):
+        for copy in self.keep():
+            copy.start()
+
+    def issue(self, c):
+        if c == 0:
+            pl.when(self.core == 1)(lambda: self.give(2, 1, 6))
+        if c < 6:
+            self.each(lambda n: self.give(n, c, c))
+
+    def pass_x(self, n, c, slot):
+        piece = self.piece(n, 1 - self.half, c, self.odd[c % 3])
+        finish(piece, piece, self.xs.at[slot], self.xr.at[slot], self.across)
+        send(piece, piece, self.ys.at[slot], self.yr.at[slot], self.beside[c % 3])
+        send(piece, piece, self.ds.at[slot], self.dr.at[slot], self.sibling)
+
+    def pass_y(self, n, c, slot):
+        piece = self.piece(n, 1 - self.half, c, 1 - self.odd[c % 3])
+        finish(piece, piece, self.ys.at[slot], self.yr.at[slot], self.beside[c % 3])
+        send(piece, piece, self.es.at[slot], self.er.at[slot], self.sibling)
+
+    def step_x(self, c):
+        self.each(lambda n: self.pass_x(n, c, c))
+        if c == 0:
+            pl.when(self.core == 1)(lambda: self.pass_x(2, 1, 6))
+
+    def step_y(self, c):
+        self.each(lambda n: self.pass_y(n, c, c))
+        if c == 0:
+            pl.when(self.core == 1)(lambda: self.pass_y(2, 1, 6))
+
+    def between(self, n, c, odd, out_sem, in_sem):
+        piece = self.piece(n, 1 - self.half, c, odd)
+        return pltpu.make_async_remote_copy(
+            src_ref=piece, dst_ref=piece, send_sem=out_sem, recv_sem=in_sem,
+            device_id=self.sibling, device_id_type=MESH,
+        )
+
+    def end(self):
+        def sent(n, c, slot):
+            odd = self.odd[c % 3]
+            self.between(n, c, odd, self.ds.at[slot], self.dr.at[slot]).wait_send()
+            self.between(n, c, 1 - odd, self.es.at[slot], self.er.at[slot]).wait_send()
+
+        def came(n, c, slot):
+            odd = self.odd[c % 3]
+            self.between(n, c, odd, self.ds.at[slot], self.dr.at[slot]).wait_recv()
+            self.between(n, c, 1 - odd, self.es.at[slot], self.er.at[slot]).wait_recv()
+
+        def act(n):
+            for c in range(6):
+                sent(n, c, c)
+                came(1 - n, c, c)
+
+        self.each(act)
+        pl.when(self.core == 1)(lambda: sent(2, 1, 6))
+        pl.when(self.core == 0)(lambda: came(2, 1, 6))
+        for copy in self.keep():
+            copy.wait()
+
+
+def front_kernel(
+    x_ref, wq, wk, wv, v0, v1, v2, v3, v4, v5, v6, v7, v8, wi, wu, wo,
+    a_ref, qo_ref, kvo_ref, ot_ref, lse_ref, w_ref, w_i, w_u, w_o, vec_ref, bi_ref,
+    q_ref, kv_ref, small, small_o, o_ref, qt, top, total,
+    own_sem, a_out, a_in, b_out, b_in, qs, qr, ks, kr, fs, fr, os, om, own, *sems,
+):
+    turn = Turn()
+    y, z, xl, core, half = turn.y, turn.z, turn.xl, turn.core, turn.half
+    fetch = Fetch(turn, (wi, wu, wo), (w_i, w_u, w_o), own, sems)
+    across, sibling = fetch.across, fetch.sibling
     barrier = pltpu.get_barrier_semaphore()
     greet(barrier, across)
     greet(barrier, sibling)
-    pl.semaphore_wait(barrier, 2)
+    greet(barrier, fetch.beside[2])
+
+    def hello(k, carry):
+        greet(barrier, turn.partner(k))
+        return carry
+
+    lax.fori_loop(1, 16, hello, 0)
+
+    @pl.when(jnp.logical_not(turn.stays))
+    def _():
+        greet(barrier, turn.partner(0))
+        greet(barrier, fetch.beside[0])
+        greet(barrier, fetch.beside[1])
+
     start = pl.multiple_of(core * GROUP, GROUP)
-    own = pl.multiple_of(half * HALF, HALF)
+    rows = pl.multiple_of(half * HALF, HALF)
     give = pl.ds(pl.multiple_of(half * HALF + core * GROUP, GROUP), GROUP)
     take = pl.ds(pl.multiple_of((1 - half) * HALF + core * GROUP, GROUP), GROUP)
     last = pl.ds(pl.multiple_of((1 - half) * HALF + (1 - core) * GROUP, GROUP), GROUP)
-    send(small, small_o, a_out.at[3], a_in.at[3], across)
-    for i, w in enumerate((wq, wk, wv)):
-        send(w.at[pl.ds(start, GROUP)], w_ref.at[i, give], a_out.at[i], a_in.at[i], across)
     mine = [
-        pltpu.make_async_copy(w, w_ref.at[i, pl.ds(own, HALF)], own_sem.at[i]) for i, w in enumerate((wq, wk, wv))
+        pltpu.make_async_copy(w, w_ref.at[i, pl.ds(rows, HALF)], own_sem.at[i]) for i, w in enumerate((wq, wk, wv))
     ]
     for copy in mine:
         copy.start()
+    fetch.own_rows()
+    small[...] = jnp.zeros_like(small)
+    for i, v in enumerate((v0, v1, v2, v3, v4, v5, v6, v7)):
+        small[i : i + 1, :] = v[...].astype(F32).reshape(1, HALF)
+    for i in range(4):
+        small[8 + i : 9 + i, :] = v8[i * HALF : (i + 1) * HALF].astype(F32).reshape(1, HALF)
+    pl.semaphore_wait(barrier, 18 + 3 * lax.rem(xl + core, 2))
+    send(small, small_o, a_out.at[3], a_in.at[3], across)
+    for i, w in enumerate((wk, wv, wq)):
+        i = (1, 2, 0)[i]
+        send(w.at[pl.ds(start, GROUP)], w_ref.at[i, give], a_out.at[i], a_in.at[i], across)
     finish(small_o, small_o, a_out.at[3], a_in.at[3], across)
-    near, far = small[...].astype(F32), small_o[...].astype(F32)
+    near, far = small[...], small_o[...]
     ahead = jnp.where(half == 0, near, far)
     behind = jnp.where(half == 0, far, near)
     vec_ref[:, :HALF] = ahead[:8]
@@ -316,66 +397,56 @@
         bi_ref[:, i * HALF : (i + 1) * HALF] = ahead[8 + i : 9 + i]
         bi_ref[:, 1536 + i * HALF : 1536 + (i + 1) * HALF] = behind[8 + i : 9 + i]
     x = x_ref[...]
-    for i in range(3):
+    for i in (1, 2, 0):
         piece = w_ref.at[i, take]
         finish(piece, piece, a_out.at[i], a_in.at[i], across)
         send(piece, piece, b_out.at[i], b_in.at[i], sibling)
-    done = []
-    for i in range(3):
+    for c in range(6):
+        fetch.issue(c)
+    done = {}
+    for i in (1, 2, 0):
         piece = w_ref.at[i, last]
         finish(piece, piece, b_out.at[i], b_in.at[i], sibling)
         mine[i].wait()
-        done.append(nn(x, w_ref[i]))
+        done[i] = nn(x, w_ref[i])
+        if i == 2:
+            keys = done[1].astype(BF)
+            values = (done[2] + vec_ref[1:2, :]).astype(BF)
+            for g in range(4):
+                cut = slice(g * GROUP, (g + 1) * GROUP)
+                kv_ref[g] = jnp.concatenate([keys[:, cut], values[:, cut]], axis=1)
+            turn.start(16, lambda k: kv_ref.at[turn.ahead(k)[1]], kvo_ref.at[y, z, xl], ks, kr)
     pad = jnp.zeros((ROWS, 64), BF)
     query = (done[0] + vec_ref[0:1, :]).astype(BF) * BF(0.125)
-    keys = done[1].astype(BF)
-    values = (done[2] + vec_ref[1:2, :]).astype(BF)
     for g in range(4):
-        cut = slice(g * GROUP, (g + 1) * GROUP)
-        q_ref[g] = jnp.concatenate([query[:, cut], pad], axis=1)
-        kv_ref[g] = jnp.concatenate([keys[:, cut], values[:, cut]], axis=1)
-
-
-def project(x, wq, wk, wv, small):
-    return pl.pallas_call(
-        project_kernel,
-        name="project",
-        out_shape=(
-            shape(4, ROWS, 256), shape(4, ROWS, HALF), shape(3, D, D), shape(8, D, dtype=F32), shape(1, FF, dtype=F32),
-        ),
-        in_specs=[VM, ANY, ANY, ANY, VM],
-        out_specs=(VM,) * 5,
-        scratch_shapes=[pltpu.VMEM((16, HALF), BF), DMA((3,)), DMA((4,)), DMA((4,)), DMA((3,)), DMA((3,))],
-        compiler_params=remote(6),
-        cost_estimate=cost(25),
-    )(x, wq, wk, wv, small)
-
-
-CHUNK = 256
-
-
-def load_chunk(ref, i):
-    y, z = pair(i)
-    return ref[y, z].reshape(CHUNK, HALF)
-
-
-def stack_head(ref, h):
-    return jnp.concatenate([ref[i][:, h * HD : (h + 1) * HD] for i in range(4)], axis=0)
-
-
-def turned(rows):
-    return rows.astype(F32).T.astype(BF)
-
-
-def attend_kernel(q_ref, kv_ref, o_ref, ot_ref, lse_ref, qt, top, total):
+        q_ref[g] = jnp.concatenate([query[:, g * GROUP : (g + 1) * GROUP], pad], axis=1)
+    turn.start(4, lambda k: q_ref.at[turn.ahead(k)[1]], qo_ref.at[z], qs, qr)
+
+    def onward(k):
+        i, j = turn.behind(k)
+        piece = kvo_ref.at[i, j, core]
+        send(piece, piece, fs.at[k], fr.at[k], turn.sibling())
+
+    turn.end_first(qo_ref.at[z], qs, qr)
+
+    def done_q(k, carry):
+        turn.end(k, qo_ref.at[turn.behind(k)[1]], qs, qr)
+        return carry
+
+    lax.fori_loop(1, 4, done_q, 0)
+    turn.end_first(kvo_ref.at[y, z, core], ks, kr)
+    onward(0)
     for h in range(3):
-        qt[h] = turned(stack_head(q_ref, h))
+        qt[h] = turned(stack_head(qo_ref, h))
     top[...] = jnp.full_like(top, -jnp.inf)
     total[...] = jnp.zeros_like(total)
     ot_ref[...] = jnp.zeros_like(ot_ref)
 
-    def body(i, carry):
-        kv = load_chunk(kv_ref, i)
+    def work(k):
+        i, j = turn.behind(k)
+        piece = kvo_ref.at[i, j, 1 - core]
+        finish(piece, piece, fs.at[k], fr.at[k], turn.sibling())
+        kv = load_chunk(kvo_ref, (i, j))
         for h in range(3):
             scores = nn(kv[:, h * HD : (h + 1) * HD], qt[h])
             old = top[h]
@@ -386,9 +457,19 @@
             mixed = tn(kv[:, GROUP + h * HD : GROUP + (h + 1) * HD], weights.astype(BF))
             ot_ref[h] = ot_ref[h] * shrink + mixed
             top[h] = new
-        return carry
-
-    lax.fori_loop(0, 4096 // CHUNK, body, 0)
+
+    def relay(k, carry):
+        i, j = turn.behind(k)
+        turn.end(k, kvo_ref.at[i, j, core], ks, kr)
+        onward(k)
+        work(k - 1)
+
+        for c in range(6):
+            pl.when(k == c + 10)(functools.partial(fetch.step_x, c))
+        return carry
+
+    lax.fori_loop(1, 16, relay, 0)
+    work(15)
     heads = []
     for h in range(3):
         lse_ref[h] = top[h] + jnp.log(total[h])
@@ -399,21 +480,41 @@
     out = jnp.concatenate(heads, axis=1)
     for i in range(4):
         o_ref[i] = out[i * ROWS : (i + 1) * ROWS]
-
-
-def attend(q, kv):
+    turn.start(4, lambda k: o_ref.at[turn.ahead(k)[1]], a_ref.at[z], os, om)
+    for c in range(6):
+        fetch.step_y(c)
+    turn.end_first(a_ref.at[z], os, om)
+
+    def done_o(k, carry):
+        turn.end(k, a_ref.at[turn.behind(k)[1]], os, om)
+        return carry
+
+    lax.fori_loop(1, 4, done_o, 0)
+    fetch.end()
+
+
+def front(*arrays):
     return pl.pallas_call(
-        attend_kernel,
-        name="attend",
-        cost_estimate=cost(20),
-        out_shape=(shape(4, ROWS, 256), shape(3, HD, 512, dtype=F32), shape(3, 1, 512, dtype=F32)),
-        in_specs=[VM, VM],
-        out_specs=(VM, VM, VM),
+        front_kernel,
+        name="front",
+        cost_estimate=cost(70),
+        out_shape=(
+            shape(4, ROWS, 256), shape(4, ROWS, 256), shape(4, 4, 2, ROWS, HALF),
+            shape(3, HD, 512, dtype=F32), shape(3, 1, 512, dtype=F32),
+            shape(3, D, D), shape(D, FF), shape(FF, D), shape(D, D), shape(8, D, dtype=F32), shape(1, FF, dtype=F32),
+        ),
+        in_specs=[VM, ANY, ANY, ANY] + [VM] * 9 + [ANY] * 3,
+        out_specs=(VM,) * 11,
         scratch_shapes=[
+            pltpu.VMEM((4, ROWS, 256), BF), pltpu.VMEM((4, ROWS, HALF), BF),
+            pltpu.VMEM((16, HALF), F32), pltpu.VMEM((16, HALF), F32),
+            pltpu.VMEM((4, ROWS, 256), BF),
             pltpu.VMEM((3, HD, 512), BF), pltpu.VMEM((3, 1, 512), F32), pltpu.VMEM((3, 1, 512), F32),
-        ],
-        compiler_params=plain(),
-    )(q, kv)
+            DMA((3,)), DMA((4,)), DMA((4,)), DMA((3,)), DMA((3,)),
+            DMA((4,)), DMA((4,)), DMA((16,)), DMA((16,)), DMA((16,)), DMA((16,)), DMA((4,)), DMA((4,)), DMA((3,)),
+        ] + [DMA((7,))] * 8,
+        compiler_params=remote(1),
+    )(arrays[0], *map(hbm, arrays[1:4]), *arrays[4:13], *map(hbm, arrays[13:]))
 
 
 def attend_back_kernel(q_ref, kv_ref, da_ref, ot_ref, lse_ref, dq_ref, dkv_ref, qs, qt, ds, dt, delta, acc):
@@ -429,7 +530,7 @@
     acc[...] = jnp.zeros_like(acc)
 
     def body(i, carry):
-        kv = load_chunk(kv_ref, i)
+        kv = load_chunk(kv_ref, pair(i))
         keys, values = [], []
         for h in range(3):
             k = kv[:, h * HD : (h + 1) * HD]
@@ -465,7 +566,7 @@
             pltpu.VMEM((3, 1, 512), F32), pltpu.VMEM((3, HD, 512), F32),
         ],
         compiler_params=plain(),
-    )(q, kv, da, ot, lse)
+    )(*map(vm, (q, kv, da, ot, lse)))
 
 
 def norm(hidden):
@@ -485,44 +586,21 @@
 
 
 def block_kernel(
-    x_ref, ct_ref, a_ref, wo, wo_a, wo_b, wi, wi_a, wi_b, wu, wu_a, wu_b, vec_ref, bi_ref,
+    x_ref, ct_ref, a_ref, w_i, w_u, w_o, vec_ref, bi_ref,
     out_ref, dh1_ref, da_ref, af_ref, yb_ref, g_ref, df_ref, du_ref, dz_ref, vg_ref,
-    w_o, w_i, w_u, slope, sems,
+    slope, da_out, outs, ins,
 ):
-    core = lax.axis_index("seq")
-    half = lax.axis_index("fsdp")
-    copies = []
-    for i, (own, first, second, full, size) in enumerate(
-        ((wo, wo_a, wo_b, w_o, HALF), (wi, wi_a, wi_b, w_i, HALF), (wu, wu_a, wu_b, w_u, FF // 2))
-    ):
-        q = size // 2
-        at = pl.multiple_of(half * size, size)
-        at_a = pl.multiple_of((1 - half) * size + core * q, q)
-        at_b = pl.multiple_of((1 - half) * size + (1 - core) * q, q)
-        copies.append(
-            (
-                pltpu.make_async_copy(own, full.at[pl.ds(at, size)], sems.at[3 * i]),
-                pltpu.make_async_copy(first, full.at[pl.ds(at_a, q)], sems.at[3 * i + 1]),
-                pltpu.make_async_copy(second, full.at[pl.ds(at_b, q)], sems.at[3 * i + 2]),
-            )
-        )
-    for group in copies:
-        for copy in group:
-            copy.start()
+    turn = Turn()
+    turn.hello(4)
     b_output, first_gain, first_shift = vec_ref[2:3, :], vec_ref[3:4, :], vec_ref[4:5, :]
     b_outer, second_gain, second_shift = vec_ref[5:6, :], vec_ref[6:7, :], vec_ref[7:8, :]
     mixed = jnp.concatenate([a_ref[g][:, :GROUP] for g in range(4)], axis=1)
     af_ref[...] = mixed
-    for copy in copies[0]:
-        copy.wait()
     hidden = x_ref[...].astype(F32) + nn(mixed, w_o[...]) + b_output
     normal1, inverse1 = norm(hidden)
     normed = normal1 * first_gain + first_shift
     low = normed.astype(BF)
     yb_ref[...] = low
-    for group in copies[1:]:
-        for copy in group:
-            copy.wait()
     second_in = normed + b_outer
     for j in range(4):
         cut = slice(j * D, (j + 1) * D)
@@ -568,27 +646,35 @@
     da = nt(dz, w_o[...]).astype(BF)
     pad = jnp.zeros((ROWS, 64), BF)
     for g in range(4):
-        da_ref[g] = jnp.concatenate([da[:, g * GROUP : (g + 1) * GROUP], pad], axis=1)
-
-
-def block(x, ct, a, weights, vec, b_inner):
+        da_out[g] = jnp.concatenate([da[:, g * GROUP : (g + 1) * GROUP], pad], axis=1)
+    turn.ready(4)
+    turn.start(4, lambda k: da_out.at[turn.ahead(k)[1]], da_ref.at[turn.z], outs, ins)
+    turn.end_first(da_ref.at[turn.z], outs, ins)
+
+    def done(k, carry):
+        turn.end(k, da_ref.at[turn.behind(k)[1]], outs, ins)
+        return carry
+
+    lax.fori_loop(1, 4, done, 0)
+
+
+def block(*arrays):
     return pl.pallas_call(
         block_kernel,
         name="block",
         cost_estimate=cost(12),
         out_shape=(
-            shape(ROWS, D), shape(ROWS, D, dtype=F32), shape(4, ROWS, 256), shape(ROWS, D), shape(ROWS, D),
+            plain_shape(ROWS, D), shape(ROWS, D, dtype=F32), shape(4, ROWS, 256), shape(ROWS, D), shape(ROWS, D),
             shape(ROWS, FF), shape(ROWS, D), shape(ROWS, FF), shape(ROWS, D),
             shape(2, 16, HALF, dtype=F32),
         ),
-        in_specs=[VM, VM, VM] + [ANY] * 9 + [VM, VM],
+        in_specs=[VM] * 8,
         out_specs=(VM,) * 10,
         scratch_shapes=[
-            pltpu.VMEM((D, D), BF), pltpu.VMEM((D, FF), BF), pltpu.VMEM((FF, D), BF),
-            pltpu.VMEM((ROWS, FF), F32), pltpu.SemaphoreType.DMA((9,)),
+            pltpu.VMEM((ROWS, FF), F32), pltpu.VMEM((4, ROWS, 256), BF), DMA((4,)), DMA((4,)),
         ],
-        compiler_params=plain(),
-    )(x, ct, a, *weights, vec, b_inner)
+        compiler_params=remote(2),
+    )(arrays[0], arrays[1], *map(vm, arrays[2:]))
 
 
 def put(ref, at, value):
@@ -653,12 +739,12 @@
     return pl.pallas_call(
         tail_kernel,
         name="tail",
-        out_shape=(shape(ROWS, D, dtype=F32), shape(3, ROWS, D), shape(2, 16, HALF, dtype=F32)),
+        out_shape=(plain_shape(ROWS, D, dtype=F32), shape(3, ROWS, D), shape(2, 16, HALF, dtype=F32)),
         in_specs=[VM] * 5,
         out_specs=(VM,) * 3,
         compiler_params=plain(),
         cost_estimate=cost(6),
-    )(*arrays)
+    )(*map(vm, arrays))
 
 
 def narrow_kernel(x, x_o, low, low_o, attn_ref, zero_ref):
@@ -939,7 +1025,7 @@
             collective_id=5, has_side_effects=True, vmem_limit_bytes=LIMIT
         ),
         cost_estimate=cost(80),
-    )(g0, g1, g2, vg)
+    )(*map(vm, (g0, g1, g2, vg)))
 
 
 def spell_kernel(zero, one, two, q_ref, k_ref, v_ref, o_ref, i_ref, u_ref):
@@ -959,7 +1045,7 @@
         name="spell",
         grid=(8,),
         out_shape=tuple(
-            shape(*dims, dtype=F32) for dims in ((HALF, D), (HALF, D), (HALF, D), (HALF, D), (HALF, FF), (1536, D))
+            plain_shape(*dims, dtype=F32) for dims in ((HALF, D), (HALF, D), (HALF, D), (HALF, D), (HALF, FF), (1536, D))
         ),
         in_specs=[
             pl.BlockSpec((2, 1, 4, 1, 48, HALF), lambda i: (0, 0, 0, i, 0, 0)),
@@ -972,16 +1058,6 @@
     )(summed, summed, summed)
 
 
-def swap_halves(array):
-    pairs = []
-    for ctx in range(32):
-        for core in range(2):
-            for half in range(2):
-                there = (ctx // 2) * 2 + (1 - ctx % 2)
-                pairs.append(((ctx * 2 + core) * 2 + half, (there * 2 + core) * 2 + 1 - half))
-    return lax.ppermute(array, AXES, pairs)
-
-
 def swap_cores(array):
     return lax.ppermute(array, "seq", [(0, 1), (1, 0)])
 
@@ -990,31 +1066,12 @@
     tokens, cotangent, w_query, w_key, w_value, w_output, b_query, b_value, b_output,
     first_gain, first_shift, w_inner, b_inner, w_outer, b_outer, second_gain, second_shift,
 ):
-    core = lax.axis_index("seq")
-    half = lax.axis_index("fsdp")
     x = tokens[0]
-
-    def share(w):
-        return lax.dynamic_slice_in_dim(w, core * (w.shape[0] // 2), w.shape[0] // 2, 0)
-
-    rows = [b_query, b_value, b_output, first_gain, first_shift, b_outer, second_gain, second_shift]
-    small = jnp.concatenate(
-        [v.reshape(1, HALF) for v in rows] + [b_inner.reshape(4, HALF), jnp.zeros((4, HALF), BF)], axis=0
+    mixed, q_all, kv_all, mixed_t, lse, w_qkv, w_i, w_u, w_o, vec, bi = front(
+        x, w_query, w_key, w_value, b_query, b_value, b_output, first_gain, first_shift, b_outer, second_gain,
+        second_shift, b_inner, w_inner, w_outer, w_output,
     )
-    q, kv, w_qkv, vec, bi = project(x, w_query, w_key, w_value, small)
-    later = tuple(share(w) for w in (w_output, w_inner, w_outer))
-    later, q = lax.optimization_barrier((later, q))
-    later = [swap_halves(w) for w in later]
-    q_all, kv_all = spread(q, kv)
-    mixed, mixed_t, lse = attend(q_all, kv_all)
-    mixed, later = lax.optimization_barrier((mixed, later))
-    others = [swap_cores(w) for w in later]
-    mixed = mates("mates_out", 2, mixed)
-    weights = []
-    for own, a, b in zip((w_output, w_inner, w_outer), later, others):
-        weights += [own, a, b]
-    layer_out, dh1, da, a_full, yb, g, df, du, dz, vg = block(x, cotangent[0], mixed, weights, vec, bi)
-    da_all = mates("mates_in", 3, da)
+    layer_out, dh1, da_all, a_full, yb, g, df, du, dz, vg = block(x, cotangent[0], mixed, w_i, w_u, w_o, vec, bi)
     acts = (yb, g, a_full, df, du, dz)
     acts_o = [swap_cores(v) for v in acts]
     x_o = swap_cores(x)

time: 332 us -> 279 us (0.84)
  Pallas kernels: 297 us -> 256 us
  local copies, waits for them, and re-layouts: 22.5 us -> 14.9 us
    pallas_call x7 -> x3, Pallas kernels: 124 us -> 98.6 us  [the longest x1 90.5 us: front(): pl.pallas_call(front_kernel, name='front', cost_estimate=cost(70), out_sh...]
    unnamed x38 -> x29, local copies, waits for them, and re-layouts: 4.11 us -> 13.6 us
    reshape x9 -> x0, local copies, waits for them, and re-layouts: 9.11 us -> none  [the longest x8 8.41 us: local(): v.reshape(1, HALF)]
    pallas_call x1, Pallas kernels: 36 us -> 30.1 us  [collect(): pl.pallas_call(collect_kernel, name='collect', out_shape=(shape(4, ROWS,...]
    ppermute x3 -> x0, starting transfers between devices: 4.76 us -> none  [swap_halves(): return lax.ppermute(array, AXES, pairs)]
    pallas_call x1, Pallas kernels: 6.24 us -> 2.05 us  [wide(): pl.pallas_call(wide_kernel, name='wide', cost_estimate=cost(6), out_shape...]
    dynamic_slice x3 -> x0, local copies, waits for them, and re-layouts: 4.14 us -> none  [share(): lax.dynamic_slice_in_dim(w, core * (w.shape[0] // 2), w.shape[0] // 2, 0)]
    pallas_call x1, Pallas kernels: 25.3 us -> 21.9 us  [attend_back(): pl.pallas_call(attend_back_kernel, name='attend_back', cost_estimate=cost...]
  transfers between devices with their start and end apart: 14 -> 8, of which waited for: 3 -> 2; matrix products, arithmetic and copies ran while one was open for 0% -> 0% of each run, Pallas kernels for 46% -> 20%
where the time goes in v3:
time: 279 us; the launch traced here: 278 us
  Pallas kernels  256 us (92%)
  local copies, waits for them, and re-layouts  14.9 us (5%)
  starting transfers between devices  4.91 us (2%)
    pallas_call x1, Pallas kernels, front(): pl.pallas_call(front_kernel, name='front', cost_estimate=cost(70), out_sh...  90.5 us
    pallas_call x1, Pallas kernels, reduce(): pl.pallas_call(reduce_kernel, name='reduce', out_shape=(shape(2, 3, 4, 4,...  89.6 us
    pallas_call x1, Pallas kernels, collect(): pl.pallas_call(collect_kernel, name='collect', out_shape=(shape(4, ROWS,...  30.1 us
    pallas_call x1, Pallas kernels, attend_back(): pl.pallas_call(attend_back_kernel, name='attend_back', cost_estimate=cost...  21.9 us
    unnamed x29, local copies, waits for them, and re-layouts  13.6 us
    pallas_call x1, Pallas kernels, block(): pl.pallas_call(block_kernel, name='block', cost_estimate=cost(12), out_sh...  12.7 us
    pallas_call x1, Pallas kernels, spell(): pl.pallas_call(spell_kernel, name='spell', grid=(8,), out_shape=tuple((pl...  6.11 us
  transfers between devices with their start and end apart: 8, of which 2 were waited for; matrix products, arithmetic and copies ran while one was open for 0% of the time, Pallas kernels for 20%

profile of v3, /device:TPU:1, one launch (start us, length us, event | category | flops | bytes accessed | tf_op | source)
XLA Modules:
  0.0 278.5 jit_solution(8548247536808668814)
XLA Ops:
  0.7 0.9 copy-done.2
  1.6 0.7 copy-done.5
  2.3 0.7 copy-done.6
  3.0 0.7 copy-done.7
  3.6 0.7 copy-done.8
  4.3 0.7 copy-done.9
  5.0 0.7 copy-done.10
  5.7 0.7 copy-done.11
  6.4 0.7 copy-done.12
  7.0 0.7 copy-done.13
  7.7 90.5 %front.1 = (bf16[4,128,256]{2,1,0:T(8,128)(2,1)S(1)}, bf16[4,128,256]{2,1,0:T(8,128)(2,1)S(1)}, bf16[4,4,2,128,384]{4,3,2,1,0:T(8,128)(2,1)S(1)}, f32[3,64,512]{...) custom-call(bf16[128,768]{1,0:T(8,128)(2,1)S(1)} %bitcast.8, ...), custom_call_target="tpu_custom_call" | custom-call | bytes 210000000 | tf_op jit(solution)/shard_map/front/pallas_call | solution.py:497
  98.3 12.7 %block.1 = (bf16[128,768]{1,0:T(8,128)(2,1)S(1)}, f32[128,768]{1,0:T(8,128)S(1)}, bf16[4,128,256]{2,1,0:T(8,128)(2,1)S(1)}, bf16[128,768]{1,0:T(8,128)(2,1)S(1)}...) custom-call(bf16[128,768]{1,0:T(8,128)(2,1)S(1)} %bitcast.9, ...), custom_call_target="tpu_custom_call" | custom-call | bytes 36000000 | tf_op jit(solution)/shard_map/block/pallas_call | solution.py:662
  111.0 1.9 collective-permute-start.3
  113.0 0.4 collective-permute-start.2
  113.4 21.9 %attend_back.1 = (bf16[4,128,256]{2,1,0:T(8,128)(2,1)S(1)}, bf16[4,4,2,128,384]{4,3,2,1,0:T(8,128)(2,1)S(1)}) custom-call(bf16[4,128,256]{2,1,0:T(8,128)(2,1)S(1)} %get-tuple-element.63.q_ref, bf16[4,4,2,128,384]{4,3,2,1,0:T(8,128)(2,1)S(1)} %get-tuple-element.64.kv_ref, bf16[4,128,256]{2,1,0:T(8,128)(2,1)S(1)} %get-tuple-element.65.da_ref, ...), custom_call_target="tpu_custom_call" | custom-call | bytes 75000000 | tf_op jit(solution)/shard_map/attend_back/pallas_call | solution.py:556
  135.3 30.1 %collect.1 = (bf16[4,128,256]{2,1,0:T(8,128)(2,1)S(1)}, bf16[4,4,128,384]{3,2,1,0:T(8,128)(2,1)S(1)}) custom-call(bf16[4,128,256]{2,1,0:T(8,128)(2,1)S(1)} %get-tuple-element.68.q_ref, bf16[4,4,2,128,384]{4,3,2,1,0:T(8,128)(2,1)S(1)} %get-tuple-element.69.kv_ref), custom_call_target="tpu_custom_call" | custom-call | bytes 90000000 | tf_op jit(solution)/shard_map/collect/pallas_call | solution.py:210
  165.4 2.0 tail.1
  167.4 1.4 collective-permute-start.1
  168.7 0.5 collective-permute-start.5
  169.2 1.4 collective-permute-done.4.a_o
  170.6 0.4 collective-permute-start.7
  171.0 0.3 collective-permute-start
  171.3 0.8 collective-permute-done.7.dz_o
  172.1 2.0 wide.1
  174.2 0.8 narrow.1.g0
  175.0 89.6 %reduce.17 = (bf16[2,3,4,4,2,48,384]{6,5,4,3,2,1,0:T(8,128)(2,1)S(1)}, f32[16,384]{1,0:T(8,128)S(1)}) custom-call(bf16[2,4,4,2,48,384]{5,4,3,2,1,0:T(8,128)(2,1)S(1)} %narrow.1.g0, bf16[2,4,4,2,48,384]{5,4,3,2,1,0:T(8,128)(2,1)S(1)} %get-tuple-element.84.g1, bf16[2,4,4,2,48,384]{5,4,3,2,1,0:T(8,128)(2,1)S(1)} %get-tuple-element.85.g2, ...), custom_call_target="tpu_custom_call" | custom-call | bytes 240000000 | tf_op jit(solution)/shard_map/reduce/pallas_call | solution.py:1009
  264.6 2.9 %copy-done = bf16[2,3,4,4,2,48,384]{6,5,4,3,2,1,0:T(8,128)(2,1)} copy-done((bf16[2,3,4,4,2,48,384]{6,5,4,3,2,1,0:T(8,128)(2,1)}, bf16[2,3,4,4,2,48,384]{6,5,4,3,2,1,0:T(8,128)(2,1)S(1)}, u32[]{:S(2)}) %copy-start) | copy-done | bytes 7077912
  267.5 0.6 slice_reduce_fusion
  268.1 0.6 reshape.41
  268.7 3.0 %copy-done.1 = bf16[2,3,4,4,2,48,384]{6,5,4,3,2,1,0:T(8,128)(2,1)S(1)} copy-done((bf16[2,3,4,4,2,48,384]{6,5,4,3,2,1,0:T(8,128)(2,1)S(1)}, bf16[2,3,4,4,2,48,384]{6,5,4,3,2,1,0:T(8,128)(2,1)}, u32[]{:S(2)}) %copy-start.1) | copy-done | bytes 7077912
  271.7 6.1 %spell.1 = (f32[384,768]{1,0:T(8,128)}, f32[384,768]{1,0:T(8,128)}, f32[384,768]{1,0:T(8,128)}, f32[384,768]{1,0:T(8,128)}, f32[384,3072]{1,0:T(8,128)}, /*index=5*/f32[1536,768]{1,0:T(8,128)}) custom-call(bf16[2,3,4,8,48,384]{5,4,3,2,1,0:T(8,128)(2,1)S(1)} %bitcast.5, bf16[2,3,4,8,48,384]{5,4,3,2,1,0:T(8,128)(2,1)S(1)} %bitcast.6, ...), custom_call_target="tpu_custom_call" | custom-call | bytes 18000000 | tf_op jit(solution)/shard_map/spell/pallas_call | solution.py:1043
  277.8 0.7 copy.35
  (25 shorter events, 0.1 us)
Async XLA Ops:
  0.7 0.9 copy-start.2
  1.6 0.7 copy-start.5
  2.3 0.7 copy-start.6
  3.0 0.7 copy-start.7
  3.6 0.7 copy-start.8
  4.3 0.7 copy-start.9
  5.0 0.7 copy-start.10
  5.7 0.7 copy-start.11
  6.4 0.7 copy-start.12
  7.0 0.7 copy-start.13
  7.7 90.6 %copy-start.4 = (bf16[1,128,768]{2,1,0:T(8,128)(2,1)S(1)}, bf16[1,128,768]{2,1,0:T(8,128)(2,1)}, u32[]{:S(2)}) copy-start(bf16[1,128,768]{2,1,0:T(8,128)(2,1)} %param.18) | copy-start | bytes 589828
  111.0 61.1 %collective-permute-start.3 = (bf16[128,3072]{1,0:T(8,128)(2,1)S(1)}, bf16[128,3072]{1,0:T(8,128)(2,1)S(1)}, u32[]{:S(2)}, u32[]{:S(2)}) collective-permute-start(bf16[128,3072]{1,0:T(8,128)(2,1)S(1)} %get-tuple-element.78.g), channel_id=1, source_target_pairs={{0,2},{2,0},{1,3},{3,1},{4,6},{6,4},{5,7},{7,5},{8,10},{10,8},{9,1... | collective-permute-start | bytes 2359304 | tf_op jit(solution)/shard_map/ppermute | solution.py:1062
  112.9 59.2 %collective-permute-start.6 = (bf16[128,3072]{1,0:T(8,128)(2,1)S(1)}, bf16[128,3072]{1,0:T(8,128)(2,1)S(1)}, u32[]{:S(2)}, u32[]{:S(2)}) collective-permute-start(bf16[128,3072]{1,0:T(8,128)(2,1)S(1)} %get-tuple-element.81.du), channel_id=1, source_target_pairs={{0,2},{2,0},{1,3},{3,1},{4,6},{6,4},{5,7},{7,5},{8,10},{10,8},{9,1... | collective-permute-start | bytes 2359304 | tf_op jit(solution)/shard_map/ppermute | solution.py:1062
  113.0 55.7 %collective-permute-start.2 = (bf16[128,768]{1,0:T(8,128)(2,1)S(1)}, bf16[128,768]{1,0:T(8,128)(2,1)S(1)}, u32[]{:S(2)}, u32[]{:S(2)}) collective-permute-start(bf16[128,768]{1,0:T(8,128)(2,1)S(1)} %get-tuple-element.77.yb), channel_id=1, source_target_pairs={{0,2},{2,0},{1,3},{3,1},{4,6},{6,4},{5,7},{7,5},{8,10},{10,8},{9,1... | collective-permute-start | bytes 589832 | tf_op jit(solution)/shard_map/ppermute | solution.py:1062
  165.4 5.6 %copy-start.3 = (bf16[1,128,768]{2,1,0:T(8,128)(2,1)S(1)}, bf16[1,128,768]{2,1,0:T(8,128)(2,1)}, u32[]{:S(2)}) copy-start(bf16[1,128,768]{2,1,0:T(8,128)(2,1)} %param.17) | copy-start | bytes 589828
  167.4 6.8 %collective-permute-start.1 = (bf16[3,128,768]{2,1,0:T(8,128)(2,1)S(1)}, bf16[3,128,768]{2,1,0:T(8,128)(2,1)S(1)}, u32[]{:S(2)}, u32[]{:S(2)}) collective-permute-start(bf16[3,128,768]{2,1,0:T(8,128)(2,1)S(1)} %get-tuple-element.76.low), channel_id=1, source_target_pairs={{0,2},{2,0},{1,3},{3,1},{4,6},{6,4},{5,7},{7,5},{8,10},{10,8},{9,1... | collective-permute-start | bytes 1769480 | tf_op jit(solution)/shard_map/ppermute | solution.py:1062
  168.7 1.9 collective-permute-start.4
  168.7 2.3 collective-permute-start.5
  170.6 1.4 collective-permute-start.7
  171.0 3.1 %collective-permute-start = (bf16[128,768]{1,0:T(8,128)(2,1)S(1)}, bf16[128,768]{1,0:T(8,128)(2,1)S(1)}, u32[]{:S(2)}, u32[]{:S(2)}) collective-permute-start(bf16[128,768]{1,0:T(8,128)(2,1)S(1)} %bitcast.10), channel_id=1, source_target_pairs={{0,2},{2,0},{1,3},{3,1},{4,6},{6,4},{5,7},{7,5},{8,10},{10,8},{9,1... | collective-permute-start | bytes 589832 | tf_op jit(solution)/shard_map/ppermute | solution.py:1062
  264.5 2.9 %copy-start = (bf16[2,3,4,4,2,48,384]{6,5,4,3,2,1,0:T(8,128)(2,1)}, bf16[2,3,4,4,2,48,384]{6,5,4,3,2,1,0:T(8,128)(2,1)S(1)}, u32[]{:S(2)}) copy-start(bf16[2,3,4,4,2,48,384]{6,5,4,3,2,1,0:T(8,128)(2,1)S(1)} %get-tuple-element.87) | copy-start | bytes 21233668
  268.7 3.0 %copy-start.1 = (bf16[2,3,4,4,2,48,384]{6,5,4,3,2,1,0:T(8,128)(2,1)S(1)}, bf16[2,3,4,4,2,48,384]{6,5,4,3,2,1,0:T(8,128)(2,1)}, u32[]{:S(2)}) copy-start(bf16[2,3,4,4,2,48,384]{6,5,4,3,2,1,0:T(8,128)(2,1)} %copy-done) | copy-start | bytes 21233668

commit v4 on v3

v4 whole, which is shorter than its diff:
```python
import functools

import jax
import jax.numpy as jnp
from jax import lax
from jax.experimental import pallas as pl
from jax.experimental.pallas import tpu as pltpu
from jax.sharding import PartitionSpec as P

AXES = ("ctx", "seq", "fsdp")
MESH = pl.DeviceIdType.MESH
BF = jnp.bfloat16
F32 = jnp.float32
D = 768
FF = 3072
HALF = 384
GROUP = 192
HD = 64
ROWS = 128
EPS = 1e-12
LIMIT = 12 << 20
VM = pl.BlockSpec(memory_space=pltpu.VMEM)
ANY = pl.BlockSpec(memory_space=pltpu.HBM)


def plain_shape(*dims, dtype=BF):
    return jax.ShapeDtypeStruct(dims, dtype)


def shape(*dims, dtype=BF):
    return pltpu.VMEM(dims, dtype)


def hbm(array):
    return pltpu.with_memory_space_constraint(array, pltpu.HBM)


def vm(array):
    return pltpu.with_memory_space_constraint(array, pltpu.VMEM)


def nn(left, right):
    return jnp.dot(left, right, preferred_element_type=F32)


def nt(left, right):
    return lax.dot_general(left, right, (((1,), (1,)), ((), ())), preferred_element_type=F32)


def tn(left, right):
    return lax.dot_general(left, right, (((0,), (0,)), ((), ())), preferred_element_type=F32)


def wrap(value, size):
    return lax.rem(value + size, size)


def place():
    ctx = lax.axis_index("ctx")
    y = lax.div(ctx, 8)
    z = lax.rem(lax.div(ctx, 2), 4)
    return y, z, lax.rem(ctx, 2), lax.axis_index("seq"), lax.axis_index("fsdp")


def device(y, z, xl, core, half):
    return ((y * 4 + z) * 2 + xl, core, half)


def send(src, dst, out_sem, in_sem, where):
    pltpu.make_async_remote_copy(
        src_ref=src, dst_ref=dst, send_sem=out_sem, recv_sem=in_sem,
        device_id=where, device_id_type=MESH,
    ).start()


def finish(src, dst, out_sem, in_sem, where):
    copy = pltpu.make_async_remote_copy(
        src_ref=src, dst_ref=dst, send_sem=out_sem, recv_sem=in_sem,
        device_id=where, device_id_type=MESH,
    )
    copy.wait_send()
    copy.wait_recv()


def arrived(got, in_sem, where):
    pltpu.make_async_remote_copy(
        src_ref=got, dst_ref=got, send_sem=in_sem, recv_sem=in_sem, device_id=where, device_id_type=MESH
    ).wait_recv()


def left_here(src, out_sem, where):
    pltpu.make_async_remote_copy(
        src_ref=src, dst_ref=src, send_sem=out_sem, recv_sem=out_sem, device_id=where, device_id_type=MESH
    ).wait_send()


def greet(barrier, where):
    pl.semaphore_signal(barrier, inc=1, device_id=where, device_id_type=MESH)


def pair(k):
    return lax.div(k, 4), lax.rem(k, 4)


class Turn:
    def __init__(self):
        self.y, self.z, self.xl, self.core, self.half = place()
        self.stays = self.xl == self.core

    def step(self, k, count):
        if count == 4:
            return 0, k
        return lax.rem(k + lax.div(k, 4), 4), lax.rem(k, 4)

    def partner(self, k, count):
        i, j = self.ahead(k, count)
        return device(i, j, self.core, self.xl, self.half)

    def ahead(self, k, count):
        i, j = self.step(k, count)
        return wrap(self.y + i, 4), wrap(self.z + j, 4)

    def behind(self, k, count):
        i, j = self.step(k, count)
        return wrap(self.y - i, 4), wrap(self.z - j, 4)

    def sibling(self):
        return device(self.y, self.z, self.xl, 1 - self.core, self.half)

    def hello(self, count, others=()):
        barrier = pltpu.get_barrier_semaphore()

        def one(k, carry):
            greet(barrier, self.partner(k, count))
            return carry

        lax.fori_loop(1, count, one, 0)
        for where in others:
            greet(barrier, where)

        @pl.when(jnp.logical_not(self.stays))
        def _():
            greet(barrier, self.partner(0, count))

    def ready(self, count, others=0):
        barrier = pltpu.get_barrier_semaphore()
        pl.semaphore_wait(barrier, count - 1 + others + lax.rem(self.xl + self.core, 2))

    def push(self, k, count, src, dst, outs, ins):
        send(src, dst, outs.at[k], ins.at[k], self.partner(k, count))

    def first(self, count, src, dst, outs, ins):
        @pl.when(self.stays)
        def _():
            pltpu.make_async_copy(src, dst, ins.at[0]).start()

        @pl.when(jnp.logical_not(self.stays))
        def _():
            self.push(0, count, src, dst, outs, ins)

    def start(self, count, src, dst, outs, ins):
        self.first(count, src(0), dst, outs, ins)

        def one(k, carry):
            self.push(k, count, src(k), dst, outs, ins)
            return carry

        lax.fori_loop(1, count, one, 0)

    def end(self, k, count, got, outs, ins):
        finish(got, got, outs.at[k], ins.at[k], self.partner(k, count))

    def end_first(self, count, got, outs, ins):
        @pl.when(self.stays)
        def _():
            pltpu.make_async_copy(got, got, ins.at[0]).wait()

        @pl.when(jnp.logical_not(self.stays))
        def _():
            self.end(0, count, got, outs, ins)

    def mates(self, src, dst, outs, ins):
        self.start(4, lambda k: src.at[self.ahead(k, 4)[1]], dst.at[self.z], outs, ins)

    def mates_end(self, dst, outs, ins):
        self.end_first(4, dst.at[self.z], outs, ins)

        def one(k, carry):
            self.end(k, 4, dst.at[self.behind(k, 4)[1]], outs, ins)
            return carry

        lax.fori_loop(1, 4, one, 0)


def cost(us):
    return pl.CostEstimate(flops=0, transcendentals=0, bytes_accessed=int(us * 3e6))


def remote(number):
    return pltpu.CompilerParams(collective_id=number, has_side_effects=True, vmem_limit_bytes=LIMIT)


def plain():
    return pltpu.CompilerParams(vmem_limit_bytes=LIMIT)


DMA = pltpu.SemaphoreType.DMA


CHUNK = 256
WINDOW = 6


def load_chunk(ref, at):
    return ref[at].reshape(CHUNK, HALF)


def stack_head(ref, h):
    return jnp.concatenate([ref[i][:, h * HD : (h + 1) * HD] for i in range(4)], axis=0)


def turned(rows):
    return rows.astype(F32).T.astype(BF)


class Fetch:
    def __init__(self, turn, sources, fulls, own, sems):
        self.core, self.half = turn.core, turn.half
        y, z, xl = turn.y, turn.z, turn.xl
        self.odd = (lax.rem(y, 2), lax.rem(z, 2), xl)
        self.across = device(y, z, 1 - xl, turn.core, 1 - turn.half)
        self.beside = (
            device(y + 1 - 2 * self.odd[0], z, xl, turn.core, turn.half),
            device(y, z + 1 - 2 * self.odd[1], xl, turn.core, turn.half),
            device(y, z, 1 - xl, turn.core, turn.half),
        )
        self.sibling = turn.sibling()
        self.sources, self.fulls, self.own = sources, fulls, own
        self.sizes = (HALF, FF // 2, HALF)
        self.xs, self.xr, self.ys, self.yr, self.ds, self.dr, self.es, self.er = sems

    def rows(self, n, c, odd):
        size = self.sizes[n]
        if n == 2:
            return odd * (size // 2), size // 2
        return c * (size // 6) + odd * (size // 12), size // 12

    def piece(self, n, half, c, odd):
        start, size = self.rows(n, c, odd)
        return self.fulls[n].at[pl.ds(pl.multiple_of(half * self.sizes[n] + start, 32), size)]

    def each(self, act, flip=False):
        pl.when(self.core == (1 if flip else 0))(lambda: act(0))
        pl.when(self.core == (0 if flip else 1))(lambda: act(1))

    def keep(self):
        for n in range(3):
            rows = self.fulls[n].at[pl.ds(pl.multiple_of(self.half * self.sizes[n], 32), self.sizes[n])]
            yield pltpu.make_async_copy(self.sources[n], rows, self.own.at[n])

    def give(self, n, c, slot):
        odd = 1 - self.odd[2] if c % 3 == 2 else self.odd[c % 3]
        start, size = self.rows(n, c, odd)
        src = self.sources[n].at[pl.ds(pl.multiple_of(start, 32), size)]
        send(src, self.piece(n, self.half, c, odd), self.xs.at[slot], self.xr.at[slot], self.across)

    def own_rows(self):
        for copy in self.keep():
            copy.start()

    def issue(self, c):
        if c == 0:
            pl.when(self.core == 1)(lambda: self.give(2, 1, 6))
        if c < 6:
            self.each(lambda n: self.give(n, c, c))

    def pass_x(self, n, c, slot):
        piece = self.piece(n, 1 - self.half, c, self.odd[c % 3])
        finish(piece, piece, self.xs.at[slot], self.xr.at[slot], self.across)
        send(piece, piece, self.ys.at[slot], self.yr.at[slot], self.beside[c % 3])
        send(piece, piece, self.ds.at[slot], self.dr.at[slot], self.sibling)

    def pass_y(self, n, c, slot):
        piece = self.piece(n, 1 - self.half, c, 1 - self.odd[c % 3])
        finish(piece, piece, self.ys.at[slot], self.yr.at[slot], self.beside[c % 3])
        send(piece, piece, self.es.at[slot], self.er.at[slot], self.sibling)

    def step_x(self, c):
        self.each(lambda n: self.pass_x(n, c, c))
        if c == 0:
            pl.when(self.core == 1)(lambda: self.pass_x(2, 1, 6))

    def step_y(self, c):
        self.each(lambda n: self.pass_y(n, c, c))
        if c == 0:
            pl.when(self.core == 1)(lambda: self.pass_y(2, 1, 6))

    def between(self, n, c, odd, out_sem, in_sem):
        piece = self.piece(n, 1 - self.half, c, odd)
        return pltpu.make_async_remote_copy(
            src_ref=piece, dst_ref=piece, send_sem=out_sem, recv_sem=in_sem,
            device_id=self.sibling, device_id_type=MESH,
        )

    def end(self):
        def sent(n, c, slot):
            odd = self.odd[c % 3]
            self.between(n, c, odd, self.ds.at[slot], self.dr.at[slot]).wait_send()
            self.between(n, c, 1 - odd, self.es.at[slot], self.er.at[slot]).wait_send()

        def came(n, c, slot):
            odd = self.odd[c % 3]
            self.between(n, c, odd, self.ds.at[slot], self.dr.at[slot]).wait_recv()
            self.between(n, c, 1 - odd, self.es.at[slot], self.er.at[slot]).wait_recv()

        def act(n):
            for c in range(6):
                sent(n, c, c)
                came(1 - n, c, c)

        self.each(act)
        pl.when(self.core == 1)(lambda: sent(2, 1, 6))
        pl.when(self.core == 0)(lambda: came(2, 1, 6))
        for copy in self.keep():
            copy.wait()


def front_kernel(
    x_ref, wq, wk, wv, v0, v1, v2, v3, v4, v5, v6, v7, v8, wi, wu, wo,
    a_ref, qo_ref, kvo_ref, ot_ref, lse_ref, w_ref, w_i, w_u, w_o, vec_ref, bi_ref, xo_ref,
    q_ref, kv_ref, small, small_o, o_ref, qt, top, total,
    own_sem, a_out, a_in, b_out, b_in, qs, qr, ks, kr, fs, fr, os, om, own, *rest,
):
    sems, lines = rest[:8], rest[8:]
    turn = Turn()
    y, z, xl, core, half = turn.y, turn.z, turn.xl, turn.core, turn.half
    fetch = Fetch(turn, (wi, wu, wo), (w_i, w_u, w_o), own, sems)
    across, sibling = fetch.across, fetch.sibling
    barrier = pltpu.get_barrier_semaphore()
    greet(barrier, across)
    greet(barrier, sibling)
    greet(barrier, fetch.beside[2])

    def hello(k, carry):
        greet(barrier, turn.partner(k, 16))
        return carry

    lax.fori_loop(1, 16, hello, 0)

    @pl.when(jnp.logical_not(turn.stays))
    def _():
        greet(barrier, turn.partner(0, 16))
        greet(barrier, fetch.beside[0])
        greet(barrier, fetch.beside[1])

    start = pl.multiple_of(core * GROUP, GROUP)
    rows = pl.multiple_of(half * HALF, HALF)
    give = pl.ds(pl.multiple_of(half * HALF + core * GROUP, GROUP), GROUP)
    take = pl.ds(pl.multiple_of((1 - half) * HALF + core * GROUP, GROUP), GROUP)
    last = pl.ds(pl.multiple_of((1 - half) * HALF + (1 - core) * GROUP, GROUP), GROUP)
    mine = [
        pltpu.make_async_copy(w, w_ref.at[i, pl.ds(rows, HALF)], own_sem.at[i]) for i, w in enumerate((wq, wk, wv))
    ]
    for copy in mine:
        copy.start()
    fetch.own_rows()
    vectors = (v0, v1, v2, v3, v4, v5, v6, v7, v8)
    loads = [pltpu.make_async_copy(v, line, own_sem.at[3 + i]) for i, (v, line) in enumerate(zip(vectors, lines))]
    for copy in loads:
        copy.start()
    for copy in loads:
        copy.wait()
    small[...] = jnp.zeros_like(small)
    for i in range(8):
        small[i : i + 1, :] = lines[i][...].astype(F32).reshape(1, HALF)
    for i in range(4):
        small[8 + i : 9 + i, :] = lines[8][i * HALF : (i + 1) * HALF].astype(F32).reshape(1, HALF)
    pl.semaphore_wait(barrier, 18 + 3 * lax.rem(xl + core, 2))
    send(small, small_o, a_out.at[3], a_in.at[3], across)
    for i, w in enumerate((wk, wv, wq)):
        i = (1, 2, 0)[i]
        send(w.at[pl.ds(start, GROUP)], w_ref.at[i, give], a_out.at[i], a_in.at[i], across)
    finish(small_o, small_o, a_out.at[3], a_in.at[3], across)
    near, far = small[...], small_o[...]
    ahead = jnp.where(half == 0, near, far)
    behind = jnp.where(half == 0, far, near)
    vec_ref[:, :HALF] = ahead[:8]
    vec_ref[:, HALF:] = behind[:8]
    for i in range(4):
        bi_ref[:, i * HALF : (i + 1) * HALF] = ahead[8 + i : 9 + i]
        bi_ref[:, 1536 + i * HALF : 1536 + (i + 1) * HALF] = behind[8 + i : 9 + i]
    def spread(k):
        src = kv_ref.at[turn.ahead(k, 16)[1]]
        if isinstance(k, int) and k == 0:
            turn.first(16, src, kvo_ref.at[y, z, xl], ks, kr)
        else:
            turn.push(k, 16, src, kvo_ref.at[y, z, xl], ks, kr)

    send(x_ref, xo_ref, a_out.at[4], a_in.at[4], sibling)
    x = x_ref[...]
    for i in (1, 2, 0):
        piece = w_ref.at[i, take]
        finish(piece, piece, a_out.at[i], a_in.at[i], across)
        send(piece, piece, b_out.at[i], b_in.at[i], sibling)
    for c in range(6):
        fetch.issue(c)
    done = {}
    for i in (1, 2, 0):
        piece = w_ref.at[i, last]
        finish(piece, piece, b_out.at[i], b_in.at[i], sibling)
        mine[i].wait()
        done[i] = nn(x, w_ref[i])
        if i == 2:
            keys = done[1].astype(BF)
            values = (done[2] + vec_ref[1:2, :]).astype(BF)
            for g in range(4):
                cut = slice(g * GROUP, (g + 1) * GROUP)
                kv_ref[g] = jnp.concatenate([keys[:, cut], values[:, cut]], axis=1)
            for k in range(WINDOW):
                spread(k)
    pad = jnp.zeros((ROWS, 64), BF)
    query = (done[0] + vec_ref[0:1, :]).astype(BF) * BF(0.125)
    for g in range(4):
        q_ref[g] = jnp.concatenate([query[:, g * GROUP : (g + 1) * GROUP], pad], axis=1)
    turn.mates(q_ref, qo_ref, qs, qr)

    def onward(k):
        i, j = turn.behind(k, 16)
        piece = kvo_ref.at[i, j, core]
        send(piece, piece, fs.at[k], fr.at[k], sibling)

    turn.mates_end(qo_ref, qs, qr)
    turn.end_first(16, kvo_ref.at[y, z, core], ks, kr)
    onward(0)
    for h in range(3):
        qt[h] = turned(stack_head(qo_ref, h))
    top[...] = jnp.full_like(top, -jnp.inf)
    total[...] = jnp.zeros_like(total)
    ot_ref[...] = jnp.zeros_like(ot_ref)

    def work(k):
        i, j = turn.behind(k, 16)
        piece = kvo_ref.at[i, j, 1 - core]
        finish(piece, piece, fs.at[k], fr.at[k], sibling)
        kv = load_chunk(kvo_ref, (i, j))
        for h in range(3):
            scores = nn(kv[:, h * HD : (h + 1) * HD], qt[h])
            old = top[h]
            new = jnp.maximum(old, jnp.max(scores, axis=0, keepdims=True))
            shrink = jnp.exp(old - new)
            weights = jnp.exp(scores - new)
            total[h] = total[h] * shrink + jnp.sum(weights, axis=0, keepdims=True)
            mixed = tn(kv[:, GROUP + h * HD : GROUP + (h + 1) * HD], weights.astype(BF))
            ot_ref[h] = ot_ref[h] * shrink + mixed
            top[h] = new

    def relay(k, carry):
        i, j = turn.behind(k, 16)
        turn.end(k, 16, kvo_ref.at[i, j, core], ks, kr)
        pl.when(k + WINDOW - 1 < 16)(lambda: spread(k + WINDOW - 1))
        onward(k)
        work(k - 1)

        for c in range(6):
            pl.when(k == c + 10)(functools.partial(fetch.step_x, c))
        return carry

    lax.fori_loop(1, 16, relay, 0)
    work(15)
    heads = []
    for h in range(3):
        lse_ref[h] = top[h] + jnp.log(total[h])
        normal = ot_ref[h] / total[h]
        ot_ref[h] = normal
        heads.append(normal.T.astype(BF))
    heads.append(jnp.zeros((512, 64), BF))
    out = jnp.concatenate(heads, axis=1)
    for i in range(4):
        o_ref[i] = out[i * ROWS : (i + 1) * ROWS]
    turn.mates(o_ref, a_ref, os, om)
    for c in range(6):
        fetch.step_y(c)
    turn.mates_end(a_ref, os, om)
    finish(xo_ref, xo_ref, a_out.at[4], a_in.at[4], sibling)
    fetch.end()


def front(*arrays):
    return pl.pallas_call(
        front_kernel,
        name="front",
        cost_estimate=cost(70),
        out_shape=(
            shape(4, ROWS, 256), shape(4, ROWS, 256), shape(4, 4, 2, ROWS, HALF),
            shape(3, HD, 512, dtype=F32), shape(3, 1, 512, dtype=F32),
            shape(3, D, D), shape(D, FF), shape(FF, D), shape(D, D), shape(8, D, dtype=F32), shape(1, FF, dtype=F32),
            shape(ROWS, D),
        ),
        in_specs=[VM, ANY, ANY, ANY] + [ANY] * 9 + [ANY] * 3,
        out_specs=(VM,) * 12,
        scratch_shapes=[
            pltpu.VMEM((4, ROWS, 256), BF), pltpu.VMEM((4, ROWS, HALF), BF),
            pltpu.VMEM((16, HALF), F32), pltpu.VMEM((16, HALF), F32),
            pltpu.VMEM((4, ROWS, 256), BF),
            pltpu.VMEM((3, HD, 512), BF), pltpu.VMEM((3, 1, 512), F32), pltpu.VMEM((3, 1, 512), F32),
            DMA((12,)), DMA((5,)), DMA((5,)), DMA((3,)), DMA((3,)),
            DMA((4,)), DMA((4,)), DMA((16,)), DMA((16,)), DMA((16,)), DMA((16,)), DMA((4,)), DMA((4,)), DMA((3,)),
        ] + [DMA((7,))] * 8 + [pltpu.VMEM((HALF,), BF)] * 8 + [pltpu.VMEM((1536,), BF)],
        compiler_params=remote(1),
    )(arrays[0], *map(hbm, arrays[1:]))


def norm(hidden):
    centred = hidden - jnp.mean(hidden, axis=-1, keepdims=True)
    inverse = lax.rsqrt(jnp.mean(centred * centred, axis=-1, keepdims=True) + EPS)
    return centred * inverse, inverse


def norm_back(scaled, normal, inverse):
    centre = jnp.mean(scaled, axis=-1, keepdims=True)
    along = jnp.mean(scaled * normal, axis=-1, keepdims=True)
    return inverse * (scaled - centre - normal * along)


def column(value):
    return jnp.sum(value, axis=0, keepdims=True)


def block_kernel(
    x_ref, ct_ref, a_ref, w_i, w_u, w_o, vec_ref, bi_ref,
    out_ref, dh1_ref, da_ref, af_ref, yb_ref, g_ref, df_ref, du_ref, dz_ref, vg_ref,
    af_o, yb_o, g_o, df_o, du_o, dz_o, slope, da_out, outs, ins, p_out, p_in,
):
    turn = Turn()
    turn.hello(4, (turn.sibling(),))
    passed = ((af_ref, af_o), (yb_ref, yb_o), (g_ref, g_o), (df_ref, df_o), (du_ref, du_o), (dz_ref, dz_o))

    def pass_on(n):
        send(*passed[n], p_out.at[n], p_in.at[n], turn.sibling())

    b_output, first_gain, first_shift = vec_ref[2:3, :], vec_ref[3:4, :], vec_ref[4:5, :]
    b_outer, second_gain, second_shift = vec_ref[5:6, :], vec_ref[6:7, :], vec_ref[7:8, :]
    mixed = jnp.concatenate([a_ref[g][:, :GROUP] for g in range(4)], axis=1)
    af_ref[...] = mixed
    hidden = x_ref[...].astype(F32) + nn(mixed, w_o[...]) + b_output
    normal1, inverse1 = norm(hidden)
    normed = normal1 * first_gain + first_shift
    low = normed.astype(BF)
    yb_ref[...] = low
    turn.ready(4, 1)
    pass_on(0)
    pass_on(1)
    second_in = normed + b_outer
    for j in range(4):
        cut = slice(j * D, (j + 1) * D)
        inner = nn(low, w_i[:, cut]) + bi_ref[:, cut]
        cdf = 0.5 * (1.0 + lax.erf(inner * (0.5**0.5)))
        active = (inner * cdf).astype(BF)
        slope[:, cut] = cdf + inner * jnp.exp(inner * inner * -0.5) * 0.3989422804014327
        g_ref[:, cut] = active
        second_in = second_in + nn(active, w_u[cut, :])
    pass_on(2)
    normal2, inverse2 = norm(second_in)
    out_ref[...] = (normal2 * second_gain + second_shift).astype(BF)
    upper = ct_ref[...].astype(F32)


    def note(row, value):
        for h in range(2):
            vg_ref[h, row : row + 1, :] = value[:, h * HALF : (h + 1) * HALF]

    vg_ref[...] = jnp.zeros_like(vg_ref)
    note(6, column(upper * normal2))
    note(7, column(upper))
    dh2 = norm_back(upper * second_gain, normal2, inverse2)
    df = dh2.astype(BF)
    df_ref[...] = df
    pass_on(3)
    note(5, column(df.astype(F32)))
    dy1 = dh2
    for j in range(4):
        cut = slice(j * D, (j + 1) * D)
        du = (slope[:, cut] * nt(df, w_u[cut, :])).astype(BF)
        du_ref[:, cut] = du
        sums = column(du.astype(F32))
        for i in range(2):
            n = 2 * j + i
            vg_ref[n // 4, 8 + n % 4 : 9 + n % 4, :] = sums[:, i * HALF : (i + 1) * HALF]
        dy1 = dy1 + nt(du, w_i[:, cut])
    pass_on(4)
    note(3, column(dy1 * normal1))
    note(4, column(dy1))
    dh1 = norm_back(dy1 * first_gain, normal1, inverse1)
    dh1_ref[...] = dh1
    dz = dh1.astype(BF)
    dz_ref[...] = dz
    pass_on(5)
    note(2, column(dz.astype(F32)))
    da = nt(dz, w_o[...]).astype(BF)
    pad = jnp.zeros((ROWS, 64), BF)
    for g in range(4):
        da_out[g] = jnp.concatenate([da[:, g * GROUP : (g + 1) * GROUP], pad], axis=1)
    turn.mates(da_out, da_ref, outs, ins)
    turn.mates_end(da_ref, outs, ins)
    for n, (src, got) in enumerate(passed):
        finish(src, got, p_out.at[n], p_in.at[n], turn.sibling())


def block(*arrays):
    return pl.pallas_call(
        block_kernel,
        name="block",
        cost_estimate=cost(12),
        out_shape=(
            plain_shape(ROWS, D), shape(ROWS, D, dtype=F32), shape(4, ROWS, 256), shape(ROWS, D), shape(ROWS, D),
            shape(ROWS, FF), shape(ROWS, D), shape(ROWS, FF), shape(ROWS, D),
            shape(2, 16, HALF, dtype=F32), shape(ROWS, D), shape(ROWS, D), shape(ROWS, FF), shape(ROWS, D),
            shape(ROWS, FF), shape(ROWS, D),
        ),
        in_specs=[VM] * 8,
        out_specs=(VM,) * 16,
        scratch_shapes=[
            pltpu.VMEM((ROWS, FF), F32), pltpu.VMEM((4, ROWS, 256), BF), DMA((4,)), DMA((4,)), DMA((6,)), DMA((6,)),
        ],
        compiler_params=remote(2),
    )(arrays[0], arrays[1], *map(vm, arrays[2:]))


EARLY = (0, 3)
LATE = (3, 1)


def back_kernel(
    q_ref, kv_ref, da_ref, ot_ref, lse_ref, x, x_o, yb, yb_o, g, g_o, a, a_o, df, df_o, du, du_o, dz, dz_o,
    dh1_ref, w_ref, vg_in,
    grad_ref, out, vo,
    rows_q, qt, rows_d, dt, delta, acc, dkv, other, dq, dqo, home, low, low_o, vg,
    g0, g1, g2, r0, r1, r2, s0, s1, s2, t0, t1, t2, rv, sv, tv, uv,
    fs, fr, ks, kr, qs, qr, ls, lr, a_out, a_in, b_out, b_in, c_out, c_in, d_out, d_in, e_out, e_in,
):
    turn = Turn()
    y, z, xl, core, half = turn.y, turn.z, turn.xl, turn.core, turn.half
    x_at = half * 2 + xl
    sibling = turn.sibling()
    barrier = pltpu.get_barrier_semaphore()

    def at(x_to, y_to, z_to):
        return device(y_to, z_to, lax.rem(x_to, 2), core, lax.div(x_to, 2))

    def along_x(k):
        return at(wrap(x_at + k, 4), y, z)

    def at_yz(k):
        i, j = pair(k)
        return at(x_at, wrap(y + i, 4), wrap(z + j, 4))

    def at_xz(k):
        i, j = pair(k)
        return at(wrap(x_at + i, 4), y, wrap(z + j, 4))

    def at_xy(k):
        i, j = pair(k)
        return at(wrap(x_at + i, 4), wrap(y + j, 4), z)

    def hello_yz(k, carry):
        greet(barrier, at_yz(k))
        return carry

    def hello_x(k, carry):
        i = lax.div(k - 1, 3) + 1
        j = lax.rem(k - 1, 3) + 1
        greet(barrier, at_xz(i * 4 + j))
        greet(barrier, at_xy(i * 4 + j))
        return carry

    def hello_row(k, carry):
        greet(barrier, along_x(k))
        return carry

    def hello_turn(k, carry):
        greet(barrier, turn.partner(k, 16))
        return carry

    lax.fori_loop(1, 16, hello_yz, 0)
    lax.fori_loop(1, 10, hello_x, 0)
    lax.fori_loop(1, 4, hello_row, 0)
    greet(barrier, sibling)

    @pl.when(jnp.logical_not(turn.stays))
    def _():
        lax.fori_loop(0, 16, hello_turn, 0)

    def put(slab, f, m, value):
        blocks = value.astype(BF).reshape(4, 2, 48, HALF)
        if slab == 1:
            g1[f, :, m] = blocks
        else:
            (g0 if slab == 0 else g2)[f, m] = blocks

    def right(ref, second, start):
        cols = pl.ds(pl.multiple_of(start + core * HALF, HALF), HALF)
        return jnp.concatenate([ref[:, cols], second[:, cols]], axis=0)

    def left(ref, second, start):
        return jnp.concatenate([ref[:, start : start + HALF], second[:, start : start + HALF]], axis=0)

    outer = right(df, df_o, 0)
    attn = right(dz, dz_o, 0)
    for f in range(2):
        for m in range(4):
            put(*((1, f, m) if m < 3 else (0, f, 0)), tn(left(g, g_o, f * 1536 + m * HALF), outer))
        rows = left(yb, yb_o, f * HALF)
        for m in range(4):
            put(*((2, f, m) if m < 3 else (0, f, 1)), tn(rows, right(du, du_o, m * D)))
        put(0, f, 2, tn(left(a, a_o, f * HALF), attn))
    pl.semaphore_wait(barrier, 37 + 16 * lax.rem(xl + core, 2))

    def first(part):
        m, n = part
        late = 0 if part is EARLY else 4

        def one(k, carry):
            e = wrap(x_at + k, 4)
            send(
                g1.at[:, wrap(y + k, 4), pl.ds(m, n)], r1.at[k - 1, :, pl.ds(m, n)],
                a_out.at[late + 1, k], a_in.at[late + 1, k], at_yz(k * 4),
            )
            send(
                g2.at[:, pl.ds(m, n), wrap(z + k, 4)], r2.at[k - 1, :, pl.ds(m, n)],
                a_out.at[late + 2, k], a_in.at[late + 2, k], at_yz(k),
            )
            send(
                g0.at[lax.div(e, 2), pl.ds(m, n), :, lax.rem(e, 2)], r0.at[k - 1, pl.ds(m, n)],
                a_out.at[late, k], a_in.at[late, k], along_x(k),
            )
            return carry

        lax.fori_loop(1, 4, one, 0)

    first(EARLY)

    for h in range(3):
        rows = stack_head(q_ref, h)
        rows_q[h] = rows
        qt[h] = turned(rows)
        rows = stack_head(da_ref, h)
        rows_d[h] = rows
        flipped = rows.astype(F32).T
        dt[h] = flipped.astype(BF)
        delta[h] = jnp.sum(flipped * ot_ref[h], axis=0, keepdims=True)
    acc[...] = jnp.zeros_like(acc)

    def work(k):
        i, j = turn.ahead(k, 16)
        kv = load_chunk(kv_ref, (i, j))
        keys, values = [], []
        for h in range(3):
            key = kv[:, h * HD : (h + 1) * HD]
            value = kv[:, GROUP + h * HD : GROUP + (h + 1) * HD]
            probs = jnp.exp(nn(key, qt[h]) - lse_ref[h])
            slopes = (probs * (nn(value, dt[h]) - delta[h])).astype(BF)
            keys.append(nn(slopes, rows_q[h]).astype(BF))
            values.append(nn(probs.astype(BF), rows_d[h]).astype(BF))
            acc[h] += tn(key, slopes)
        dkv[i, j] = jnp.concatenate(keys + values, axis=1).reshape(2, ROWS, HALF)
        send(dkv.at[i, j, 1 - core], other.at[i, j], fs.at[k], fr.at[k], sibling)

    def join(k):
        i, j = turn.ahead(k, 16)
        finish(other.at[i, j], other.at[i, j], fs.at[k], fr.at[k], sibling)
        other[i, j] = (dkv[i, j, core].astype(F32) + other[i, j].astype(F32)).astype(BF)

    def relay(k):
        join(k)
        turn.push(k, 16, other.at[turn.ahead(k, 16)], home.at[y, z], ks, kr)

    work(0)
    work(1)
    join(0)
    turn.first(16, other.at[y, z], home.at[y, z], ks, kr)

    def step(k, carry):
        work(k)
        relay(k - 1)
        return carry

    lax.fori_loop(2, 16, step, 0)
    relay(15)
    heads = [(acc[h] * 0.125).T.astype(BF) for h in range(3)]
    heads.append(jnp.zeros((512, 64), BF))
    turned_back = jnp.concatenate(heads, axis=1)
    for i in range(4):
        dq[i] = turned_back[i * ROWS : (i + 1) * ROWS]
    turn.mates(dq, dqo, qs, qr)

    here = device(y, z, xl, core, half)

    def second(part):
        m, n = part
        late = 0 if part is EARLY else 4

        def add(slab, own, got, to, count, where):
            for k in range(1, 4):
                piece = got.at[k - 1, pl.ds(m, n)] if slab == 0 else got.at[k - 1, :, pl.ds(m, n)]
                finish(piece, piece, a_out.at[late + slab, k], a_in.at[late + slab, k], here)

            def one(i, carry):
                p = where(i)
                total = own(p).astype(F32)
                for k in range(3):
                    total = total + got[(k,) + p].astype(F32)
                to[p] = total.astype(BF)
                return carry

            lax.fori_loop(0, count, one, 0)

        def push(slab, src, got, k, where):
            @pl.when(k > 0)
            def _():
                send(src, got.at[k], b_out.at[slab, k], b_in.at[slab, k], where)

        def spot(i):
            return lax.div(i, 2 * n), m + lax.rem(lax.div(i, 2), n), lax.rem(i, 2)

        add(1, lambda p: g1[p[0], y, p[1], p[2]], r1, s1, 4 * n, spot)

        def push1(i, carry):
            e, to = wrap(x_at + lax.div(i, n), 4), m + lax.rem(i, n)
            k = lax.div(i, n) * 4 + wrap(to - z, 4)
            push(1, s1.at[lax.div(e, 2), to, lax.rem(e, 2)], t1, k, at(e, y, to))
            return carry

        lax.fori_loop(0, 4 * n, push1, 0)
        add(2, lambda p: g2[p[0], p[1], z, p[2]], r2, s2, 4 * n, spot)

        def push2(i, carry):
            e, to = wrap(x_at + lax.div(i, n), 4), m + lax.rem(i, n)
            k = lax.div(i, n) * 4 + wrap(to - y, 4)
            push(2, s2.at[lax.div(e, 2), to, lax.rem(e, 2)], t2, k, at(e, to, z))
            return carry

        lax.fori_loop(0, 4 * n, push2, 0)
        add(
            0, lambda p: g0[half, p[0], p[1], xl], r0, s0, 4 * n,
            lambda i: (m + lax.div(i, 4), lax.rem(i, 4)),
        )

        def push0(i, carry):
            e, to = wrap(z + lax.div(i, n), 4), m + lax.rem(i, n)
            k = wrap(to - y, 4) * 4 + lax.div(i, n)
            push(0, s0.at[to, e], t0, k, at(x_at, to, e))
            return carry

        lax.fori_loop(0, 4 * n, push0, 0)

    second(EARLY)

    turn.mates_end(dqo, qs, qr)
    turn.end_first(16, home.at[y, z], ks, kr)

    def done(k, carry):
        turn.end(k, 16, home.at[turn.behind(k, 16)], ks, kr)
        return carry

    lax.fori_loop(1, 16, done, 0)
    low[0] = jnp.concatenate([dqo[i][:, :GROUP] for i in range(4)], axis=1)
    sums = []
    for i in range(4):
        total = home[0, i].astype(F32)
        for k in range(1, 4):
            total = total + home[k, i].astype(F32)
        sums.append(total.astype(BF))
    low[1] = jnp.concatenate([v[:, :GROUP] for v in sums], axis=1)
    low[2] = jnp.concatenate([v[:, GROUP:] for v in sums], axis=1)
    send(low, low_o, ls, lr, sibling)
    grad = dh1_ref[...]
    for i in range(3):
        grad = grad + nt(low[i], w_ref[i])
    grad_ref[...] = grad
    vg[...] = vg_in[...]
    for row, i in ((0, 0), (1, 2)):
        value = column(low[i].astype(F32))
        for f in range(2):
            vg[f, row : row + 1, :] = value[:, f * HALF : (f + 1) * HALF]

    def first3(k, carry):
        src = vg.at[lax.div(wrap(x_at + k, 4), 2)]
        send(src, rv.at[k - 1], a_out.at[3, k], a_in.at[3, k], along_x(k))
        return carry

    lax.fori_loop(1, 4, first3, 0)
    finish(low, low_o, ls, lr, sibling)
    cols = pl.ds(pl.multiple_of(core * HALF, HALF), HALF)
    both_low = [jnp.concatenate([low[i, :, cols], low_o[i, :, cols]], axis=0) for i in range(3)]
    for f in range(2):
        rows = left(x, x_o, f * HALF)
        for i, slab in enumerate((2, 1, 0)):
            put(slab, f, 3, tn(rows, both_low[i]))
    first(LATE)

    def third(part):
        early = part is EARLY

        def whole(own, got, slab):
            def wait(k, carry):
                arrived(got.at[k], b_in.at[slab, k], here)
                return carry

            lax.fori_loop(1, 16, wait, 0)

            def one(k, total):
                return total + got[k].astype(F32)

            out[core, slab, y, z, xl] = lax.fori_loop(1, 16, one, own.astype(F32)).astype(BF)

        def spread(slab, count, where):
            mine = out.at[core, slab, y, z, xl]

            def one(k, carry):
                send(mine, mine, c_out.at[slab, k], c_in.at[slab, k], where(k))
                return carry

            lax.fori_loop(1, count, one, 0)

        @pl.when(z < 3 if early else z == 3)
        def _():
            whole(s1[half, z, xl], t1, 1)
            spread(1, 8, lambda k: device(y, wrap(z + lax.div(k, 2), 4), wrap(xl + lax.rem(k, 2), 2), core, half))

        @pl.when(y < 3 if early else y == 3)
        def _():
            whole(s2[half, y, xl], t2, 2)
            spread(2, 8, lambda k: device(wrap(y + lax.div(k, 2), 4), z, wrap(xl + lax.rem(k, 2), 2), core, half))
            whole(s0[y, z], t0, 0)
            spread(0, 16, at_yz)

    def fourth(part):
        m, n = part
        late = 0 if part is EARLY else 3

        def wait(slab, piece, k):
            @pl.when(k > 0)
            def _():
                arrived(piece, c_in.at[slab, k], here)

        def got1(i, carry):
            zz, xx = m + lax.div(i, 2), lax.rem(i, 2)
            wait(1, out.at[core, 1, y, zz, xx], wrap(z - zz, 4) * 2 + wrap(xl - xx, 2))
            return carry

        lax.fori_loop(0, 2 * n, got1, 0)

        def push1(k, carry):
            mine = out.at[core, 1, y, pl.ds(m, n)]
            send(mine, mine, d_out.at[late + 1, k], d_in.at[late + 1, k], at_yz(k * 4))
            return carry

        lax.fori_loop(1, 4, push1, 0)

        def got2(i, carry):
            yy, xx = m + lax.div(i, 2), lax.rem(i, 2)
            wait(2, out.at[core, 2, yy, z, xx], wrap(y - yy, 4) * 2 + wrap(xl - xx, 2))
            return carry

        lax.fori_loop(0, 2 * n, got2, 0)

        def push2(k, carry):
            mine = out.at[core, 2, pl.ds(m, n), z]
            send(mine, mine, d_out.at[late + 2, k], d_in.at[late + 2, k], at_yz(k))
            return carry

        lax.fori_loop(1, 4, push2, 0)

        def got0(i, carry):
            yy, zz = m + lax.div(i, 4), lax.rem(i, 4)
            wait(0, out.at[core, 0, yy, zz, xl], wrap(y - yy, 4) * 4 + wrap(z - zz, 4))
            return carry

        lax.fori_loop(0, 4 * n, got0, 0)
        mine0 = out.at[core, 0, pl.ds(m, n), :, xl]
        send(mine0, mine0, d_out.at[late, 1], d_in.at[late, 1], device(y, z, 1 - xl, core, half))

    def own_part(slab, who, part):
        m, n = part
        return out.at[who, 1, :, pl.ds(m, n)] if slab == 1 else out.at[who, slab, pl.ds(m, n)]

    def last(part):
        m, n = part
        late = 0 if part is EARLY else 3

        def got1(k, carry):
            piece = out.at[core, 1, wrap(y - k, 4), pl.ds(m, n)]
            finish(piece, piece, d_out.at[late + 1, k], d_in.at[late + 1, k], here)
            return carry

        def got2(k, carry):
            piece = out.at[core, 2, pl.ds(m, n), wrap(z - k, 4)]
            finish(piece, piece, d_out.at[late + 2, k], d_in.at[late + 2, k], here)
            return carry

        def onward(slab):
            piece = own_part(slab, core, part)
            send(piece, piece, e_out.at[late + slab], e_in.at[late + slab], sibling)

        lax.fori_loop(1, 4, got1, 0)
        onward(1)
        lax.fori_loop(1, 4, got2, 0)
        onward(2)
        piece0 = out.at[core, 0, pl.ds(m, n), :, 1 - xl]
        finish(piece0, piece0, d_out.at[late, 1], d_in.at[late, 1], here)
        onward(0)

    third(EARLY)
    for k in range(1, 4):
        finish(rv.at[k - 1], rv.at[k - 1], a_out.at[3, k], a_in.at[3, k], here)
    part_sum = vg[half] + rv[0] + rv[1] + rv[2]
    sv[...] = part_sum.astype(BF)

    def second3(k, carry):
        send(sv, tv.at[k], b_out.at[3, k], b_in.at[3, k], at_yz(k))
        return carry

    lax.fori_loop(1, 16, second3, 0)
    second(LATE)
    fourth(EARLY)
    third(LATE)

    def done3(k, total):
        finish(tv.at[k], tv.at[k], b_out.at[3, k], b_in.at[3, k], here)
        return total + tv[k].astype(F32)

    vo[...] = lax.fori_loop(1, 16, done3, part_sum)
    send(vo, uv, e_out.at[6], e_in.at[6], sibling)
    fourth(LATE)
    last(EARLY)
    last(LATE)
    for late, part in ((0, EARLY), (3, LATE)):
        for slab in range(3):
            piece = own_part(slab, 1 - core, part)
            finish(piece, piece, e_out.at[late + slab], e_in.at[late + slab], here)
    for slab, count, own, got in ((1, 8, s1, t1), (2, 8, s2, t2), (0, 16, s0, t0)):
        mine = out.at[core, slab, y, z, xl]

        def gone2(k, carry):
            left_here(got.at[k], b_out.at[slab, k], here)
            return carry

        def gone3(k, carry):
            left_here(mine, c_out.at[slab, k], here)
            return carry

        lax.fori_loop(1, 16, gone2, 0)
        lax.fori_loop(1, count, gone3, 0)
    finish(uv, uv, e_out.at[6], e_in.at[6], here)
    vo[...] = vo[...] + uv[...]


def back(*arrays):
    blk = (48, HALF)
    scratch = [
        ((3, 512, HD), BF), ((3, HD, 512), BF), ((3, 512, HD), BF), ((3, HD, 512), BF), ((3, 1, 512), F32),
        ((3, HD, 512), F32), ((4, 4, 2, ROWS, HALF), BF), ((4, 4, ROWS, HALF), BF),
        ((4, ROWS, 256), BF), ((4, ROWS, 256), BF), ((4, 4, ROWS, HALF), BF), ((3, ROWS, D), BF), ((3, ROWS, D), BF),
        ((2, 16, HALF), F32),
        ((2, 4, 4, 2, *blk), BF), ((2, 4, 4, 2, *blk), BF), ((2, 4, 4, 2, *blk), BF),
        ((3, 4, 4, *blk), BF), ((3, 2, 4, 2, *blk), BF), ((3, 2, 4, 2, *blk), BF),
        ((4, 4, *blk), BF), ((2, 4, 2, *blk), BF), ((2, 4, 2, *blk), BF),
        ((16, *blk), BF), ((16, *blk), BF), ((16, *blk), BF),
        ((3, 16, HALF), F32), ((16, HALF), BF), ((16, 16, HALF), BF), ((16, HALF), F32),
    ]
    return pl.pallas_call(
        back_kernel,
        name="back",
        cost_estimate=cost(100),
        out_shape=(
            plain_shape(ROWS, D, dtype=F32), shape(2, 3, 4, 4, 2, *blk), shape(16, HALF, dtype=F32),
        ),
        in_specs=[VM] * 22,
        out_specs=(VM,) * 3,
        scratch_shapes=[pltpu.VMEM(*v) for v in scratch] + [
            DMA((16,)), DMA((16,)), DMA((16,)), DMA((16,)), DMA((4,)), DMA((4,)), DMA, DMA,
            DMA((7, 4)), DMA((7, 4)), DMA((4, 16)), DMA((4, 16)), DMA((3, 16)), DMA((3, 16)),
            DMA((6, 4)), DMA((6, 4)), DMA((7,)), DMA((7,)),
        ],
        compiler_params=pltpu.CompilerParams(
            collective_id=3, has_side_effects=True, vmem_limit_bytes=29 << 20
        ),
    )(*map(vm, arrays))


def spell_kernel(full, q_ref, k_ref, v_ref, o_ref, i_ref, u_ref, stage, sems):
    def copies(n):
        slot = stage.at[n % 2]
        rows = slice(n * 48, (n + 1) * 48)
        made = [
            pltpu.make_async_copy(slot.at[m], ref.at[rows], sems.at[n % 2, m])
            for m, ref in enumerate((q_ref, k_ref, v_ref, o_ref))
        ]
        for m in range(4):
            made.append(pltpu.make_async_copy(
                slot.at[4 + m], i_ref.at[rows, m * D : (m + 1) * D], sems.at[n % 2, 4 + m]
            ))
            made.append(pltpu.make_async_copy(
                slot.at[8 + m], u_ref.at[m * HALF + n * 48 : m * HALF + (n + 1) * 48], sems.at[n % 2, 8 + m]
            ))
        return made

    for n in range(8):
        if n >= 2:
            for copy in copies(n - 2):
                copy.wait()
        i, xl = n // 2, n % 2
        for c in range(2):
            cols = slice(c * HALF, (c + 1) * HALF)
            units = [(2, 3), (1, 3), (0, 3), (0, 2), (2, 0), (2, 1), (2, 2), (0, 1), (1, 0), (1, 1), (1, 2), (0, 0)]
            for m, (slab, unit) in enumerate(units):
                piece = full[c, 1, i, unit, xl] if slab == 1 else full[c, slab, unit, i, xl]
                stage[n % 2, m, :, cols] = piece.astype(F32)
        for copy in copies(n):
            copy.start()
    for n in (6, 7):
        for copy in copies(n):
            copy.wait()


def spell(summed):
    return pl.pallas_call(
        spell_kernel,
        name="spell",
        out_shape=tuple(
            plain_shape(*dims, dtype=F32)
            for dims in ((HALF, D), (HALF, D), (HALF, D), (HALF, D), (HALF, FF), (1536, D))
        ),
        in_specs=[VM],
        out_specs=(ANY,) * 6,
        scratch_shapes=[pltpu.VMEM((2, 12, 48, D), F32), DMA((2, 12))],
        compiler_params=plain(),
        cost_estimate=cost(6),
    )(vm(summed))


def local(
    tokens, cotangent, w_query, w_key, w_value, w_output, b_query, b_value, b_output,
    first_gain, first_shift, w_inner, b_inner, w_outer, b_outer, second_gain, second_shift,
):
    x = tokens[0]
    mixed, q_all, kv_all, mixed_t, lse, w_qkv, w_i, w_u, w_o, vec, bi, x_o = front(
        x, w_query, w_key, w_value, b_query, b_value, b_output, first_gain, first_shift, b_outer, second_gain,
        second_shift, b_inner, w_inner, w_outer, w_output,
    )
    layer_out, dh1, da_all, a, yb, g, df, du, dz, vg, a_o, yb_o, g_o, df_o, du_o, dz_o = block(
        x, cotangent[0], mixed, w_i, w_u, w_o, vec, bi
    )
    tokens_grad, summed, vecs = back(
        q_all, kv_all, da_all, mixed_t, lse, x, x_o, yb, yb_o, g, g_o, a, a_o, df, df_o, du, du_o, dz, dz_o,
        dh1, w_qkv, vg,
    )
    gq, gk, gv, go, gi, gu = spell(summed)
    return (
        layer_out[None], tokens_grad[None], gq, gk, gv, go,
        vecs[0], vecs[1], vecs[2], vecs[3], vecs[4], gi, vecs[8:12].reshape(1536), gu, vecs[5], vecs[6], vecs[7],
    )


def solution(mesh):
    rows = P(("seq", "fsdp"), "ctx", None)
    mat = P("fsdp", None)
    vec = P("fsdp")
    return jax.shard_map(
        local,
        mesh=mesh,
        in_specs=(rows, rows, mat, mat, mat, mat, vec, vec, vec, vec, vec, mat, vec, mat, vec, vec, vec),
        out_specs=(rows, rows, mat, mat, mat, mat, vec, vec, vec, vec, vec, mat, vec, mat, vec, vec, vec),
        check_vma=False,
    )
```

time: 279 us -> 232 us (0.83)
  Pallas kernels: 256 us -> 221 us
  local copies, waits for them, and re-layouts: 14.9 us -> 9.51 us
  starting transfers between devices: 4.91 us -> 0 us
    pallas_call x7 -> x2, Pallas kernels: 152 us -> 127 us  [the longest x1 121 us: back(): pl.pallas_call(back_kernel, name='back', cost_estimate=cost(100), out_sha...]
    pallas_call x1, Pallas kernels: 90.5 us -> 80.6 us  [front(): pl.pallas_call(front_kernel, name='front', cost_estimate=cost(70), out_sh...]
    unnamed x29 -> x12, local copies, waits for them, and re-layouts: 13.6 us -> 8.27 us
    ppermute x8 -> x0, starting transfers between devices: 4.91 us -> none  [swap_cores(): return lax.ppermute(array, 'seq', [(0, 1), (1, 0)])]
  transfers between devices with their start and end apart: 8 -> 0, of which waited for: 2 -> 0; matrix products, arithmetic and copies ran while one was open for 0% -> 0% of each run, Pallas kernels for 20% -> 0%
where the time goes in v4:
time: 232 us
  Pallas kernels  221 us (95%)
  local copies, waits for them, and re-layouts  9.51 us (4%)
    pallas_call x1, Pallas kernels, back(): pl.pallas_call(back_kernel, name='back', cost_estimate=cost(100), out_sha...  121 us
    pallas_call x1, Pallas kernels, front(): pl.pallas_call(front_kernel, name='front', cost_estimate=cost(70), out_sh...  80.6 us
    pallas_call x1, Pallas kernels, block(): pl.pallas_call(block_kernel, name='block', cost_estimate=cost(12), out_sh...  13.9 us
    unnamed x12, local copies, waits for them, and re-layouts  8.27 us
    pallas_call x1, Pallas kernels, spell(): pl.pallas_call(spell_kernel, name='spell', out_shape=tuple((plain_shape(*...  5.88 us

profile of v4, /device:TPU:1, one launch (start us, length us, event | category | flops | bytes accessed | tf_op | source)
XLA Modules:
  0.0 231.6 jit_solution(15800549871172064244)
XLA Ops:
  0.7 0.0 copy-start.2
  0.7 0.9 copy-done.2
  1.6 0.0 copy-start.4
  1.6 80.6 %front.1 = (bf16[4,128,256]{2,1,0:T(8,128)(2,1)S(1)}, bf16[4,128,256]{2,1,0:T(8,128)(2,1)S(1)}, bf16[4,4,2,128,384]{4,3,2,1,0:T(8,128)(2,1)S(1)}, f32[3,64,512]{...) custom-call(bf16[128,768]{1,0:T(8,128)(2,1)S(1)} %bitcast.4, ...), custom_call_target="tpu_custom_call" | custom-call | bytes 210000000 | tf_op jit(solution)/shard_map/front/pallas_call | solution.py:489
  82.2 0.0 copy-done.4
  82.2 0.0 copy-start.3
  82.2 13.9 %block.1 = (bf16[128,768]{1,0:T(8,128)(2,1)S(1)}, f32[128,768]{1,0:T(8,128)S(1)}, bf16[4,128,256]{2,1,0:T(8,128)(2,1)S(1)}, bf16[128,768]{1,0:T(8,128)(2,1)S(1)}...) custom-call(bf16[128,768]{1,0:T(8,128)(2,1)S(1)} %bitcast.5, ...), custom_call_target="tpu_custom_call" | custom-call | bytes 36000000 | tf_op jit(solution)/shard_map/block/pallas_call | solution.py:610
  96.2 0.0 copy-done.3
  96.2 120.9 %back.1 = (f32[128,768]{1,0:T(8,128)S(1)}, bf16[2,3,4,4,2,48,384]{6,5,4,3,2,1,0:T(8,128)(2,1)S(1)}, f32[16,384]{1,0:T(8,128)S(1)}) custom-call(bf16[4,128,256]{2,1,0:T(8,128)(2,1)S(1)} %get-tuple-element.61.q_ref, bf16[4,4,2,128,384]{4,3,2,1,0:T(8,128)(2,1)S(1)} %get-tuple-element.62.kv_ref, bf16[4,128,256]{2,1,0:T(8,128)(2,1)S(1)} %get-tuple-element.63.da_ref, ...), custom_call_target="tpu_custom_call" | custom-call | bytes 300000000 | tf_op jit(solution)/shard_map/back/pallas_call | solution.py:1071
  217.1 0.0 copy-start
  217.1 2.9 %copy-done = bf16[2,3,4,4,2,48,384]{6,5,4,3,2,1,0:T(8,128)(2,1)} copy-done((bf16[2,3,4,4,2,48,384]{6,5,4,3,2,1,0:T(8,128)(2,1)}, bf16[2,3,4,4,2,48,384]{6,5,4,3,2,1,0:T(8,128)(2,1)S(1)}, u32[]{:S(2)}) %copy-start) | copy-done | bytes 7077912
  220.0 0.6 slice_reduce_fusion
  220.7 0.6 reshape.37
  221.3 0.0 copy-start.1
  221.3 3.0 %copy-done.1 = bf16[2,3,4,4,2,48,384]{6,5,4,3,2,1,0:T(8,128)(2,1)S(1)} copy-done((bf16[2,3,4,4,2,48,384]{6,5,4,3,2,1,0:T(8,128)(2,1)S(1)}, bf16[2,3,4,4,2,48,384]{6,5,4,3,2,1,0:T(8,128)(2,1)}, u32[]{:S(2)}) %copy-start.1) | copy-done | bytes 7077912
  224.3 5.9 %spell.1 = (f32[384,768]{1,0:T(8,128)}, f32[384,768]{1,0:T(8,128)}, f32[384,768]{1,0:T(8,128)}, f32[384,768]{1,0:T(8,128)}, f32[384,3072]{1,0:T(8,128)}, /*index=5*/f32[1536,768]{1,0:T(8,128)}) custom-call(bf16[2,3,4,4,2,48,384]{6,5,4,3,2,1,0:T(8,128)(2,1)S(1)} %copy-done.1), custom_call_target="tpu_custom_call" | custom-call | bytes 18000000 | tf_op jit(solution)/shard_map/spell/pallas_call | solution.py:1127
  230.2 0.7 copy.36
  230.8 0.7 copy.37
  (1 shorter events, 0.0 us)
Async XLA Ops:
  0.7 0.9 copy-start.2
  1.6 80.6 %copy-start.4 = (bf16[1,128,768]{2,1,0:T(8,128)(2,1)S(1)}, bf16[1,128,768]{2,1,0:T(8,128)(2,1)}, u32[]{:S(2)}) copy-start(bf16[1,128,768]{2,1,0:T(8,128)(2,1)} %param.18) | copy-start | bytes 589828
  82.2 13.9 %copy-start.3 = (bf16[1,128,768]{2,1,0:T(8,128)(2,1)S(1)}, bf16[1,128,768]{2,1,0:T(8,128)(2,1)}, u32[]{:S(2)}) copy-start(bf16[1,128,768]{2,1,0:T(8,128)(2,1)} %param.17) | copy-start | bytes 589828
  217.1 2.9 %copy-start = (bf16[2,3,4,4,2,48,384]{6,5,4,3,2,1,0:T(8,128)(2,1)}, bf16[2,3,4,4,2,48,384]{6,5,4,3,2,1,0:T(8,128)(2,1)S(1)}, u32[]{:S(2)}) copy-start(bf16[2,3,4,4,2,48,384]{6,5,4,3,2,1,0:T(8,128)(2,1)S(1)} %get-tuple-element.83.full) | copy-start | bytes 21233668
  221.3 3.0 %copy-start.1 = (bf16[2,3,4,4,2,48,384]{6,5,4,3,2,1,0:T(8,128)(2,1)S(1)}, bf16[2,3,4,4,2,48,384]{6,5,4,3,2,1,0:T(8,128)(2,1)}, u32[]{:S(2)}) copy-start(bf16[2,3,4,4,2,48,384]{6,5,4,3,2,1,0:T(8,128)(2,1)} %copy-done) | copy-start | bytes 21233668

commit v5 on v4

--- a/solution.py
+++ b/solution.py
@@ -329,7 +329,7 @@
     x_ref, wq, wk, wv, v0, v1, v2, v3, v4, v5, v6, v7, v8, wi, wu, wo,
     a_ref, qo_ref, kvo_ref, ot_ref, lse_ref, w_ref, w_i, w_u, w_o, vec_ref, bi_ref, xo_ref,
     q_ref, kv_ref, small, small_o, o_ref, qt, top, total,
-    own_sem, a_out, a_in, b_out, b_in, qs, qr, ks, kr, fs, fr, os, om, own, *rest,
+    own_sem, a_out, a_in, b_out, b_in, p_out, p_in, qs, qr, ks, kr, fs, fr, os, om, own, *rest,
 ):
     sems, lines = rest[:8], rest[8:]
     turn = Turn()
@@ -353,11 +353,12 @@
         greet(barrier, fetch.beside[0])
         greet(barrier, fetch.beside[1])
 
-    start = pl.multiple_of(core * GROUP, GROUP)
     rows = pl.multiple_of(half * HALF, HALF)
-    give = pl.ds(pl.multiple_of(half * HALF + core * GROUP, GROUP), GROUP)
-    take = pl.ds(pl.multiple_of((1 - half) * HALF + core * GROUP, GROUP), GROUP)
-    last = pl.ds(pl.multiple_of((1 - half) * HALF + (1 - core) * GROUP, GROUP), GROUP)
+    quarter = GROUP // 2
+
+    def share(i, of, odd, who):
+        return w_ref.at[i, pl.ds(pl.multiple_of(of * HALF + odd * GROUP + who * quarter, quarter), quarter)]
+
     mine = [
         pltpu.make_async_copy(w, w_ref.at[i, pl.ds(rows, HALF)], own_sem.at[i]) for i, w in enumerate((wq, wk, wv))
     ]
@@ -377,9 +378,10 @@
         small[8 + i : 9 + i, :] = lines[8][i * HALF : (i + 1) * HALF].astype(F32).reshape(1, HALF)
     pl.semaphore_wait(barrier, 18 + 3 * lax.rem(xl + core, 2))
     send(small, small_o, a_out.at[3], a_in.at[3], across)
-    for i, w in enumerate((wk, wv, wq)):
-        i = (1, 2, 0)[i]
-        send(w.at[pl.ds(start, GROUP)], w_ref.at[i, give], a_out.at[i], a_in.at[i], across)
+    for i in (1, 2, 0):
+        odd = 1 - fetch.odd[2] if i == 2 else fetch.odd[i]
+        src = (wq, wk, wv)[i].at[pl.ds(pl.multiple_of(odd * GROUP + core * quarter, quarter), quarter)]
+        send(src, share(i, half, odd, core), a_out.at[i], a_in.at[i], across)
     finish(small_o, small_o, a_out.at[3], a_in.at[3], across)
     near, far = small[...], small_o[...]
     ahead = jnp.where(half == 0, near, far)
@@ -399,15 +401,21 @@
     send(x_ref, xo_ref, a_out.at[4], a_in.at[4], sibling)
     x = x_ref[...]
     for i in (1, 2, 0):
-        piece = w_ref.at[i, take]
+        piece = share(i, 1 - half, fetch.odd[i], core)
         finish(piece, piece, a_out.at[i], a_in.at[i], across)
+        send(piece, piece, p_out.at[i], p_in.at[i], fetch.beside[i])
         send(piece, piece, b_out.at[i], b_in.at[i], sibling)
     for c in range(6):
         fetch.issue(c)
+    for i in (1, 2, 0):
+        piece = share(i, 1 - half, 1 - fetch.odd[i], core)
+        finish(piece, piece, p_out.at[i], p_in.at[i], fetch.beside[i])
+        send(piece, piece, b_out.at[3 + i], b_in.at[3 + i], sibling)
     done = {}
     for i in (1, 2, 0):
-        piece = w_ref.at[i, last]
-        finish(piece, piece, b_out.at[i], b_in.at[i], sibling)
+        for n, odd in ((i, fetch.odd[i]), (3 + i, 1 - fetch.odd[i])):
+            piece = share(i, 1 - half, odd, 1 - core)
+            finish(piece, piece, b_out.at[n], b_in.at[n], sibling)
         mine[i].wait()
         done[i] = nn(x, w_ref[i])
         if i == 2:
@@ -503,7 +511,7 @@
             pltpu.VMEM((16, HALF), F32), pltpu.VMEM((16, HALF), F32),
             pltpu.VMEM((4, ROWS, 256), BF),
             pltpu.VMEM((3, HD, 512), BF), pltpu.VMEM((3, 1, 512), F32), pltpu.VMEM((3, 1, 512), F32),
-            DMA((12,)), DMA((5,)), DMA((5,)), DMA((3,)), DMA((3,)),
+            DMA((12,)), DMA((5,)), DMA((5,)), DMA((6,)), DMA((6,)), DMA((3,)), DMA((3,)),
             DMA((4,)), DMA((4,)), DMA((16,)), DMA((16,)), DMA((16,)), DMA((16,)), DMA((4,)), DMA((4,)), DMA((3,)),
         ] + [DMA((7,))] * 8 + [pltpu.VMEM((HALF,), BF)] * 8 + [pltpu.VMEM((1536,), BF)],
         compiler_params=remote(1),
@@ -612,7 +620,7 @@
         name="block",
         cost_estimate=cost(12),
         out_shape=(
-            plain_shape(ROWS, D), shape(ROWS, D, dtype=F32), shape(4, ROWS, 256), shape(ROWS, D), shape(ROWS, D),
+            shape(ROWS, D), shape(ROWS, D, dtype=F32), shape(4, ROWS, 256), shape(ROWS, D), shape(ROWS, D),
             shape(ROWS, FF), shape(ROWS, D), shape(ROWS, FF), shape(ROWS, D),
             shape(2, 16, HALF, dtype=F32), shape(ROWS, D), shape(ROWS, D), shape(ROWS, FF), shape(ROWS, D),
             shape(ROWS, FF), shape(ROWS, D),
@@ -689,6 +697,17 @@
     @pl.when(jnp.logical_not(turn.stays))
     def _():
         lax.fori_loop(0, 16, hello_turn, 0)
+
+    for h in range(3):
+        rows = stack_head(q_ref, h)
+        rows_q[h] = rows
+        qt[h] = turned(rows)
+        rows = stack_head(da_ref, h)
+        rows_d[h] = rows
+        flipped = rows.astype(F32).T
+        dt[h] = flipped.astype(BF)
+        delta[h] = jnp.sum(flipped * ot_ref[h], axis=0, keepdims=True)
+    acc[...] = jnp.zeros_like(acc)
 
     def put(slab, f, m, value):
         blocks = value.astype(BF).reshape(4, 2, 48, HALF)
@@ -739,17 +758,6 @@
 
     first(EARLY)
 
-    for h in range(3):
-        rows = stack_head(q_ref, h)
-        rows_q[h] = rows
-        qt[h] = turned(rows)
-        rows = stack_head(da_ref, h)
-        rows_d[h] = rows
-        flipped = rows.astype(F32).T
-        dt[h] = flipped.astype(BF)
-        delta[h] = jnp.sum(flipped * ot_ref[h], axis=0, keepdims=True)
-    acc[...] = jnp.zeros_like(acc)
-
     def work(k):
         i, j = turn.ahead(k, 16)
         kv = load_chunk(kv_ref, (i, j))
@@ -853,8 +861,6 @@
 
         lax.fori_loop(0, 4 * n, push0, 0)
 
-    second(EARLY)
-
     turn.mates_end(dqo, qs, qr)
     turn.end_first(16, home.at[y, z], ks, kr)
 
@@ -873,6 +879,15 @@
     low[1] = jnp.concatenate([v[:, :GROUP] for v in sums], axis=1)
     low[2] = jnp.concatenate([v[:, GROUP:] for v in sums], axis=1)
     send(low, low_o, ls, lr, sibling)
+    second(EARLY)
+    finish(low, low_o, ls, lr, sibling)
+    cols = pl.ds(pl.multiple_of(core * HALF, HALF), HALF)
+    both_low = [jnp.concatenate([low[i, :, cols], low_o[i, :, cols]], axis=0) for i in range(3)]
+    for f in range(2):
+        rows = left(x, x_o, f * HALF)
+        for i, slab in enumerate((2, 1, 0)):
+            put(slab, f, 3, tn(rows, both_low[i]))
+    first(LATE)
     grad = dh1_ref[...]
     for i in range(3):
         grad = grad + nt(low[i], w_ref[i])
@@ -889,14 +904,6 @@
         return carry
 
     lax.fori_loop(1, 4, first3, 0)
-    finish(low, low_o, ls, lr, sibling)
-    cols = pl.ds(pl.multiple_of(core * HALF, HALF), HALF)
-    both_low = [jnp.concatenate([low[i, :, cols], low_o[i, :, cols]], axis=0) for i in range(3)]
-    for f in range(2):
-        rows = left(x, x_o, f * HALF)
-        for i, slab in enumerate((2, 1, 0)):
-            put(slab, f, 3, tn(rows, both_low[i]))
-    first(LATE)
 
     def third(part):
         early = part is EARLY
@@ -1073,7 +1080,7 @@
         name="back",
         cost_estimate=cost(100),
         out_shape=(
-            plain_shape(ROWS, D, dtype=F32), shape(2, 3, 4, 4, 2, *blk), shape(16, HALF, dtype=F32),
+            shape(ROWS, D, dtype=F32), shape(2, 3, 4, 4, 2, *blk), shape(16, HALF, dtype=F32),
         ),
         in_specs=[VM] * 22,
         out_specs=(VM,) * 3,
@@ -1088,7 +1095,18 @@
     )(*map(vm, arrays))
 
 
-def spell_kernel(full, q_ref, k_ref, v_ref, o_ref, i_ref, u_ref, stage, sems):
+def spell_kernel(full, vo, layer, grad, *refs):
+    q_ref, k_ref, v_ref, o_ref, i_ref, u_ref, layer_ref, grad_ref = refs[:8]
+    lines, (stage, sems, direct) = refs[8:17], refs[17:]
+    straight = [
+        pltpu.make_async_copy(layer, layer_ref, direct.at[0]), pltpu.make_async_copy(grad, grad_ref, direct.at[1])
+    ]
+    for copy in straight:
+        copy.start()
+    for i in range(8):
+        lines[i][...] = vo[i : i + 1, :].reshape(HALF)
+    lines[8][...] = jnp.concatenate([vo[8 + i : 9 + i, :] for i in range(4)], axis=1).reshape(1536)
+
     def copies(n):
         slot = stage.at[n % 2]
         rows = slice(n * 48, (n + 1) * 48)
@@ -1121,22 +1139,25 @@
     for n in (6, 7):
         for copy in copies(n):
             copy.wait()
-
-
-def spell(summed):
+    for copy in straight:
+        copy.wait()
+
+
+def spell(*arrays):
     return pl.pallas_call(
         spell_kernel,
         name="spell",
         out_shape=tuple(
             plain_shape(*dims, dtype=F32)
             for dims in ((HALF, D), (HALF, D), (HALF, D), (HALF, D), (HALF, FF), (1536, D))
-        ),
-        in_specs=[VM],
-        out_specs=(ANY,) * 6,
-        scratch_shapes=[pltpu.VMEM((2, 12, 48, D), F32), DMA((2, 12))],
+        ) + (plain_shape(ROWS, D), plain_shape(ROWS, D, dtype=F32))
+        + (plain_shape(HALF, dtype=F32),) * 8 + (plain_shape(1536, dtype=F32),),
+        in_specs=[VM] * 4,
+        out_specs=(ANY,) * 8 + (VM,) * 9,
+        scratch_shapes=[pltpu.VMEM((2, 12, 48, D), F32), DMA((2, 12)), DMA((2,))],
         compiler_params=plain(),
         cost_estimate=cost(6),
-    )(vm(summed))
+    )(*map(vm, arrays))
 
 
 def local(
@@ -1155,10 +1176,10 @@
         q_all, kv_all, da_all, mixed_t, lse, x, x_o, yb, yb_o, g, g_o, a, a_o, df, df_o, du, du_o, dz, dz_o,
         dh1, w_qkv, vg,
     )
-    gq, gk, gv, go, gi, gu = spell(summed)
+    gq, gk, gv, go, gi, gu, layer_out, tokens_grad, *vecs = spell(summed, vecs, layer_out, tokens_grad)
     return (
         layer_out[None], tokens_grad[None], gq, gk, gv, go,
-        vecs[0], vecs[1], vecs[2], vecs[3], vecs[4], gi, vecs[8:12].reshape(1536), gu, vecs[5], vecs[6], vecs[7],
+        vecs[0], vecs[1], vecs[2], vecs[3], vecs[4], gi, vecs[8], gu, vecs[5], vecs[6], vecs[7],
     )
 
 

time: 232 us -> 215 us (0.927); the launches traced: 232 us -> 212 us
  Pallas kernels: 221 us -> 210 us
  local copies, waits for them, and re-layouts: 9.51 us -> 0.93 us
    unnamed x12 -> x6, local copies, waits for them, and re-layouts: 8.27 us -> 0.93 us
    pallas_call x1, Pallas kernels: 121 us -> 114 us  [back(): pl.pallas_call(back_kernel, name='back', cost_estimate=cost(100), out_sha...]
    pallas_call x1, Pallas kernels: 80.6 us -> 75.4 us  [front(): pl.pallas_call(front_kernel, name='front', cost_estimate=cost(70), out_sh...]
where the time goes in v5:
time: 215 us; the launch traced here: 212 us
  Pallas kernels  210 us (98%)
    pallas_call x1, Pallas kernels, back(): pl.pallas_call(back_kernel, name='back', cost_estimate=cost(100), out_sha...  114 us
    pallas_call x1, Pallas kernels, front(): pl.pallas_call(front_kernel, name='front', cost_estimate=cost(70), out_sh...  75.4 us
    pallas_call x1, Pallas kernels, block(): pl.pallas_call(block_kernel, name='block', cost_estimate=cost(12), out_sh...  14 us
    pallas_call x1, Pallas kernels, spell(): pl.pallas_call(spell_kernel, name='spell', out_shape=tuple((plain_shape(*...  6.68 us

profile of v5, /device:TPU:1, one launch (start us, length us, event | category | flops | bytes accessed | tf_op | source)
XLA Modules:
  0.0 211.8 jit_solution(4733357261159317217)
XLA Ops:
  0.7 0.0 copy-start
  0.7 0.9 copy-done
  1.6 0.0 copy-start.2
  1.6 75.4 %front.1 = (bf16[4,128,256]{2,1,0:T(8,128)(2,1)S(1)}, bf16[4,128,256]{2,1,0:T(8,128)(2,1)S(1)}, bf16[4,4,2,128,384]{4,3,2,1,0:T(8,128)(2,1)S(1)}, f32[3,64,512]{...) custom-call(bf16[128,768]{1,0:T(8,128)(2,1)S(1)} %bitcast.4, ...), custom_call_target="tpu_custom_call" | custom-call | bytes 210000000 | tf_op jit(solution)/shard_map/front/pallas_call | solution.py:497
  77.0 0.0 copy-done.2
  77.0 0.0 copy-start.1
  77.0 14.0 %block.1 = (bf16[128,768]{1,0:T(8,128)(2,1)S(1)}, f32[128,768]{1,0:T(8,128)S(1)}, bf16[4,128,256]{2,1,0:T(8,128)(2,1)S(1)}, bf16[128,768]{1,0:T(8,128)(2,1)S(1)}...) custom-call(bf16[128,768]{1,0:T(8,128)(2,1)S(1)} %bitcast.5, ...), custom_call_target="tpu_custom_call" | custom-call | bytes 36000000 | tf_op jit(solution)/shard_map/block/pallas_call | solution.py:618
  91.0 0.0 copy-done.1
  91.0 113.9 %back.1 = (f32[128,768]{1,0:T(8,128)S(1)}, bf16[2,3,4,4,2,48,384]{6,5,4,3,2,1,0:T(8,128)(2,1)S(1)}, f32[16,384]{1,0:T(8,128)S(1)}) custom-call(bf16[4,128,256]{2,1,0:T(8,128)(2,1)S(1)} %get-tuple-element.65.q_ref, bf16[4,4,2,128,384]{4,3,2,1,0:T(8,128)(2,1)S(1)} %get-tuple-element.66.kv_ref, bf16[4,128,256]{2,1,0:T(8,128)(2,1)S(1)} %get-tuple-element.73.da_ref, ...), custom_call_target="tpu_custom_call" | custom-call | bytes 300000000 | tf_op jit(solution)/shard_map/back/pallas_call | solution.py:1078
  204.9 6.7 %spell.1 = (f32[384,768]{1,0:T(8,128)}, f32[384,768]{1,0:T(8,128)}, f32[384,768]{1,0:T(8,128)}, f32[384,768]{1,0:T(8,128)}, f32[384,3072]{1,0:T(8,128)}, /*index...) custom-call(bf16[2,3,4,4,2,48,384]{6,5,4,3,2,1,0:T(8,128)(2,1)S(1)} , ...), custom_call_target="tpu_custom_call" | custom-call | bytes 18000000 | tf_op jit(solution)/shard_map/spell/pallas_call | solution.py:1147
Async XLA Ops:
  0.7 0.9 copy-start
  1.6 75.4 %copy-start.2 = (bf16[1,128,768]{2,1,0:T(8,128)(2,1)S(1)}, bf16[1,128,768]{2,1,0:T(8,128)(2,1)}, u32[]{:S(2)}) copy-start(bf16[1,128,768]{2,1,0:T(8,128)(2,1)} %param.18) | copy-start | bytes 589828
  77.0 14.1 %copy-start.1 = (bf16[1,128,768]{2,1,0:T(8,128)(2,1)S(1)}, bf16[1,128,768]{2,1,0:T(8,128)(2,1)}, u32[]{:S(2)}) copy-start(bf16[1,128,768]{2,1,0:T(8,128)(2,1)} %param.17) | copy-start | bytes 589828

commit v6 on v5

--- a/solution.py
+++ b/solution.py
@@ -179,8 +179,9 @@
         def _():
             self.end(0, count, got, outs, ins)
 
-    def mates(self, src, dst, outs, ins):
-        self.start(4, lambda k: src.at[self.ahead(k, 4)[1]], dst.at[self.z], outs, ins)
+    def mates(self, src, dst, outs, ins, own=None):
+        slot = dst.at[self.z] if own is None else dst.at[self.z, own]
+        self.start(4, lambda k: src.at[self.ahead(k, 4)[1]], slot, outs, ins)
 
     def mates_end(self, dst, outs, ins):
         self.end_first(4, dst.at[self.z], outs, ins)
@@ -208,7 +209,6 @@
 
 
 CHUNK = 256
-WINDOW = 6
 
 
 def load_chunk(ref, at):
@@ -259,7 +259,7 @@
             yield pltpu.make_async_copy(self.sources[n], rows, self.own.at[n])
 
     def give(self, n, c, slot):
-        odd = 1 - self.odd[2] if c % 3 == 2 else self.odd[c % 3]
+        odd = 1 - self.odd[2] if c % 2 else self.odd[1]
         start, size = self.rows(n, c, odd)
         src = self.sources[n].at[pl.ds(pl.multiple_of(start, 32), size)]
         send(src, self.piece(n, self.half, c, odd), self.xs.at[slot], self.xr.at[slot], self.across)
@@ -275,14 +275,14 @@
             self.each(lambda n: self.give(n, c, c))
 
     def pass_x(self, n, c, slot):
-        piece = self.piece(n, 1 - self.half, c, self.odd[c % 3])
+        piece = self.piece(n, 1 - self.half, c, self.odd[1 + c % 2])
         finish(piece, piece, self.xs.at[slot], self.xr.at[slot], self.across)
-        send(piece, piece, self.ys.at[slot], self.yr.at[slot], self.beside[c % 3])
+        send(piece, piece, self.ys.at[slot], self.yr.at[slot], self.beside[1 + c % 2])
         send(piece, piece, self.ds.at[slot], self.dr.at[slot], self.sibling)
 
     def pass_y(self, n, c, slot):
-        piece = self.piece(n, 1 - self.half, c, 1 - self.odd[c % 3])
-        finish(piece, piece, self.ys.at[slot], self.yr.at[slot], self.beside[c % 3])
+        piece = self.piece(n, 1 - self.half, c, 1 - self.odd[1 + c % 2])
+        finish(piece, piece, self.ys.at[slot], self.yr.at[slot], self.beside[1 + c % 2])
         send(piece, piece, self.es.at[slot], self.er.at[slot], self.sibling)
 
     def step_x(self, c):
@@ -304,12 +304,12 @@
 
     def end(self):
         def sent(n, c, slot):
-            odd = self.odd[c % 3]
+            odd = self.odd[1 + c % 2]
             self.between(n, c, odd, self.ds.at[slot], self.dr.at[slot]).wait_send()
             self.between(n, c, 1 - odd, self.es.at[slot], self.er.at[slot]).wait_send()
 
         def came(n, c, slot):
-            odd = self.odd[c % 3]
+            odd = self.odd[1 + c % 2]
             self.between(n, c, odd, self.ds.at[slot], self.dr.at[slot]).wait_recv()
             self.between(n, c, 1 - odd, self.es.at[slot], self.er.at[slot]).wait_recv()
 
@@ -329,7 +329,7 @@
     x_ref, wq, wk, wv, v0, v1, v2, v3, v4, v5, v6, v7, v8, wi, wu, wo,
     a_ref, qo_ref, kvo_ref, ot_ref, lse_ref, w_ref, w_i, w_u, w_o, vec_ref, bi_ref, xo_ref,
     q_ref, kv_ref, small, small_o, o_ref, qt, top, total,
-    own_sem, a_out, a_in, b_out, b_in, p_out, p_in, qs, qr, ks, kr, fs, fr, os, om, own, *rest,
+    own_sem, a_out, a_in, b_out, b_in, p_out, p_in, qs, qr, ks, kr, ms, mr, fs, fr, os, om, own, *rest,
 ):
     sems, lines = rest[:8], rest[8:]
     turn = Turn()
@@ -341,16 +341,16 @@
     greet(barrier, sibling)
     greet(barrier, fetch.beside[2])
 
-    def hello(k, carry):
-        greet(barrier, turn.partner(k, 16))
-        return carry
-
-    lax.fori_loop(1, 16, hello, 0)
+    def mate(dy):
+        return device(wrap(y + dy, 4), z, xl, core, half)
+
+    for k in range(1, 4):
+        greet(barrier, mate(k))
+        greet(barrier, turn.partner(k, 4))
 
     @pl.when(jnp.logical_not(turn.stays))
     def _():
-        greet(barrier, turn.partner(0, 16))
-        greet(barrier, fetch.beside[0])
+        greet(barrier, turn.partner(0, 4))
         greet(barrier, fetch.beside[1])
 
     rows = pl.multiple_of(half * HALF, HALF)
@@ -376,7 +376,7 @@
         small[i : i + 1, :] = lines[i][...].astype(F32).reshape(1, HALF)
     for i in range(4):
         small[8 + i : 9 + i, :] = lines[8][i * HALF : (i + 1) * HALF].astype(F32).reshape(1, HALF)
-    pl.semaphore_wait(barrier, 18 + 3 * lax.rem(xl + core, 2))
+    pl.semaphore_wait(barrier, 9 + 2 * lax.rem(xl + core, 2))
     send(small, small_o, a_out.at[3], a_in.at[3], across)
     for i in (1, 2, 0):
         odd = 1 - fetch.odd[2] if i == 2 else fetch.odd[i]
@@ -391,13 +391,6 @@
     for i in range(4):
         bi_ref[:, i * HALF : (i + 1) * HALF] = ahead[8 + i : 9 + i]
         bi_ref[:, 1536 + i * HALF : 1536 + (i + 1) * HALF] = behind[8 + i : 9 + i]
-    def spread(k):
-        src = kv_ref.at[turn.ahead(k, 16)[1]]
-        if isinstance(k, int) and k == 0:
-            turn.first(16, src, kvo_ref.at[y, z, xl], ks, kr)
-        else:
-            turn.push(k, 16, src, kvo_ref.at[y, z, xl], ks, kr)
-
     send(x_ref, xo_ref, a_out.at[4], a_in.at[4], sibling)
     x = x_ref[...]
     for i in (1, 2, 0):
@@ -405,8 +398,8 @@
         finish(piece, piece, a_out.at[i], a_in.at[i], across)
         send(piece, piece, p_out.at[i], p_in.at[i], fetch.beside[i])
         send(piece, piece, b_out.at[i], b_in.at[i], sibling)
-    for c in range(6):
-        fetch.issue(c)
+    fetch.issue(0)
+    fetch.issue(1)
     for i in (1, 2, 0):
         piece = share(i, 1 - half, 1 - fetch.odd[i], core)
         finish(piece, piece, p_out.at[i], p_in.at[i], fetch.beside[i])
@@ -424,30 +417,34 @@
             for g in range(4):
                 cut = slice(g * GROUP, (g + 1) * GROUP)
                 kv_ref[g] = jnp.concatenate([keys[:, cut], values[:, cut]], axis=1)
-            for k in range(WINDOW):
-                spread(k)
+            turn.mates(kv_ref, kvo_ref.at[y], ks, kr, own=xl)
+    fetch.issue(2)
+    fetch.issue(3)
     pad = jnp.zeros((ROWS, 64), BF)
     query = (done[0] + vec_ref[0:1, :]).astype(BF) * BF(0.125)
     for g in range(4):
         q_ref[g] = jnp.concatenate([query[:, g * GROUP : (g + 1) * GROUP], pad], axis=1)
     turn.mates(q_ref, qo_ref, qs, qr)
 
-    def onward(k):
-        i, j = turn.behind(k, 16)
+    def spot(t):
+        g, k = lax.div(t, 4), lax.rem(t, 4)
+        dy = g + lax.div(g, 2) * (5 - 2 * g)
+        return dy, k, wrap(y - dy, 4), wrap(z - k, 4)
+
+    def onward(t):
+        dy, k, i, j = spot(t)
         piece = kvo_ref.at[i, j, core]
-        send(piece, piece, fs.at[k], fr.at[k], sibling)
-
-    turn.mates_end(qo_ref, qs, qr)
-    turn.end_first(16, kvo_ref.at[y, z, core], ks, kr)
+        send(piece, piece, fs.at[t], fr.at[t], sibling)
+
+    def hand(piece, dy, n):
+        send(piece, piece, ms.at[n], mr.at[n], mate(dy))
+
+    turn.end_first(4, kvo_ref.at[y, z, core], ks, kr)
+    hand(kvo_ref.at[y, z, core], 1, 4)
+    hand(kvo_ref.at[y, z, core], 3, 12)
     onward(0)
-    for h in range(3):
-        qt[h] = turned(stack_head(qo_ref, h))
-    top[...] = jnp.full_like(top, -jnp.inf)
-    total[...] = jnp.zeros_like(total)
-    ot_ref[...] = jnp.zeros_like(ot_ref)
-
     def work(k):
-        i, j = turn.behind(k, 16)
+        _, _, i, j = spot(k)
         piece = kvo_ref.at[i, j, 1 - core]
         finish(piece, piece, fs.at[k], fr.at[k], sibling)
         kv = load_chunk(kvo_ref, (i, j))
@@ -462,18 +459,47 @@
             ot_ref[h] = ot_ref[h] * shrink + mixed
             top[h] = new
 
+    def arrive(k):
+        dy, n, i, j = spot(k)
+        piece = kvo_ref.at[i, j, core]
+
+        @pl.when(dy == 0)
+        def _():
+            turn.end(n, 4, piece, ks, kr)
+            hand(piece, 1, 4 + n)
+            hand(piece, 3, 12 + n)
+
+        @pl.when(dy > 0)
+        def _():
+            finish(piece, piece, ms.at[dy * 4 + n], mr.at[dy * 4 + n], mate(1))
+
+        pl.when((dy == 1) & (lax.rem(n, 2) == 0))(lambda: hand(piece, 1, 8 + n))
+        pl.when((dy == 3) & (lax.rem(n, 2) == 1))(lambda: hand(piece, 3, 8 + n))
+        onward(k)
+
+    for k in range(1, 4):
+        arrive(k)
+    fetch.issue(4)
+    fetch.issue(5)
+    turn.mates_end(qo_ref, qs, qr)
+    for h in range(3):
+        qt[h] = turned(stack_head(qo_ref, h))
+    top[...] = jnp.full_like(top, -jnp.inf)
+    total[...] = jnp.zeros_like(total)
+    ot_ref[...] = jnp.zeros_like(ot_ref)
+
+    for k in range(3):
+        work(k)
+
     def relay(k, carry):
-        i, j = turn.behind(k, 16)
-        turn.end(k, 16, kvo_ref.at[i, j, core], ks, kr)
-        pl.when(k + WINDOW - 1 < 16)(lambda: spread(k + WINDOW - 1))
-        onward(k)
+        arrive(k)
         work(k - 1)
 
-        for c in range(6):
-            pl.when(k == c + 10)(functools.partial(fetch.step_x, c))
+        for c, when in enumerate((4, 5, 7, 8, 11, 12)):
+            pl.when(k == when)(functools.partial(fetch.step_x, c))
         return carry
 
-    lax.fori_loop(1, 16, relay, 0)
+    lax.fori_loop(4, 16, relay, 0)
     work(15)
     heads = []
     for h in range(3):
@@ -512,7 +538,8 @@
             pltpu.VMEM((4, ROWS, 256), BF),
             pltpu.VMEM((3, HD, 512), BF), pltpu.VMEM((3, 1, 512), F32), pltpu.VMEM((3, 1, 512), F32),
             DMA((12,)), DMA((5,)), DMA((5,)), DMA((6,)), DMA((6,)), DMA((3,)), DMA((3,)),
-            DMA((4,)), DMA((4,)), DMA((16,)), DMA((16,)), DMA((16,)), DMA((16,)), DMA((4,)), DMA((4,)), DMA((3,)),
+            DMA((4,)), DMA((4,)), DMA((4,)), DMA((4,)), DMA((16,)), DMA((16,)), DMA((16,)), DMA((16,)),
+            DMA((4,)), DMA((4,)), DMA((3,)),
         ] + [DMA((7,))] * 8 + [pltpu.VMEM((HALF,), BF)] * 8 + [pltpu.VMEM((1536,), BF)],
         compiler_params=remote(1),
     )(arrays[0], *map(hbm, arrays[1:]))
@@ -534,13 +561,11 @@
     return jnp.sum(value, axis=0, keepdims=True)
 
 
-def block_kernel(
-    x_ref, ct_ref, a_ref, w_i, w_u, w_o, vec_ref, bi_ref,
+def block_part(
+    turn, ready, x_ref, ct_ref, a_ref, w_i, w_u, w_o, vec_ref, bi_ref,
     out_ref, dh1_ref, da_ref, af_ref, yb_ref, g_ref, df_ref, du_ref, dz_ref, vg_ref,
     af_o, yb_o, g_o, df_o, du_o, dz_o, slope, da_out, outs, ins, p_out, p_in,
 ):
-    turn = Turn()
-    turn.hello(4, (turn.sibling(),))
     passed = ((af_ref, af_o), (yb_ref, yb_o), (g_ref, g_o), (df_ref, df_o), (du_ref, du_o), (dz_ref, dz_o))
 
     def pass_on(n):
@@ -555,7 +580,7 @@
     normed = normal1 * first_gain + first_shift
     low = normed.astype(BF)
     yb_ref[...] = low
-    turn.ready(4, 1)
+    ready()
     pass_on(0)
     pass_on(1)
     second_in = normed + b_outer
@@ -609,44 +634,22 @@
     for g in range(4):
         da_out[g] = jnp.concatenate([da[:, g * GROUP : (g + 1) * GROUP], pad], axis=1)
     turn.mates(da_out, da_ref, outs, ins)
-    turn.mates_end(da_ref, outs, ins)
     for n, (src, got) in enumerate(passed):
         finish(src, got, p_out.at[n], p_in.at[n], turn.sibling())
 
 
-def block(*arrays):
-    return pl.pallas_call(
-        block_kernel,
-        name="block",
-        cost_estimate=cost(12),
-        out_shape=(
-            shape(ROWS, D), shape(ROWS, D, dtype=F32), shape(4, ROWS, 256), shape(ROWS, D), shape(ROWS, D),
-            shape(ROWS, FF), shape(ROWS, D), shape(ROWS, FF), shape(ROWS, D),
-            shape(2, 16, HALF, dtype=F32), shape(ROWS, D), shape(ROWS, D), shape(ROWS, FF), shape(ROWS, D),
-            shape(ROWS, FF), shape(ROWS, D),
-        ),
-        in_specs=[VM] * 8,
-        out_specs=(VM,) * 16,
-        scratch_shapes=[
-            pltpu.VMEM((ROWS, FF), F32), pltpu.VMEM((4, ROWS, 256), BF), DMA((4,)), DMA((4,)), DMA((6,)), DMA((6,)),
-        ],
-        compiler_params=remote(2),
-    )(arrays[0], arrays[1], *map(vm, arrays[2:]))
-
-
 EARLY = (0, 3)
 LATE = (3, 1)
 
 
-def back_kernel(
-    q_ref, kv_ref, da_ref, ot_ref, lse_ref, x, x_o, yb, yb_o, g, g_o, a, a_o, df, df_o, du, du_o, dz, dz_o,
+def back_part(
+    turn, da_end, q_ref, kv_ref, da_ref, ot_ref, lse_ref, x, x_o, yb, yb_o, g, g_o, a, a_o, df, df_o, du, du_o, dz, dz_o,
     dh1_ref, w_ref, vg_in,
     grad_ref, out, vo,
     rows_q, qt, rows_d, dt, delta, acc, dkv, other, dq, dqo, home, low, low_o, vg,
     g0, g1, g2, r0, r1, r2, s0, s1, s2, t0, t1, t2, rv, sv, tv, uv,
     fs, fr, ks, kr, qs, qr, ls, lr, a_out, a_in, b_out, b_in, c_out, c_in, d_out, d_in, e_out, e_in,
 ):
-    turn = Turn()
     y, z, xl, core, half = turn.y, turn.z, turn.xl, turn.core, turn.half
     x_at = half * 2 + xl
     sibling = turn.sibling()
@@ -689,384 +692,428 @@
         greet(barrier, turn.partner(k, 16))
         return carry
 
-    lax.fori_loop(1, 16, hello_yz, 0)
-    lax.fori_loop(1, 10, hello_x, 0)
-    lax.fori_loop(1, 4, hello_row, 0)
-    greet(barrier, sibling)
-
-    @pl.when(jnp.logical_not(turn.stays))
-    def _():
-        lax.fori_loop(0, 16, hello_turn, 0)
-
-    for h in range(3):
-        rows = stack_head(q_ref, h)
-        rows_q[h] = rows
-        qt[h] = turned(rows)
-        rows = stack_head(da_ref, h)
-        rows_d[h] = rows
-        flipped = rows.astype(F32).T
-        dt[h] = flipped.astype(BF)
-        delta[h] = jnp.sum(flipped * ot_ref[h], axis=0, keepdims=True)
-    acc[...] = jnp.zeros_like(acc)
-
-    def put(slab, f, m, value):
-        blocks = value.astype(BF).reshape(4, 2, 48, HALF)
-        if slab == 1:
-            g1[f, :, m] = blocks
-        else:
-            (g0 if slab == 0 else g2)[f, m] = blocks
-
-    def right(ref, second, start):
-        cols = pl.ds(pl.multiple_of(start + core * HALF, HALF), HALF)
-        return jnp.concatenate([ref[:, cols], second[:, cols]], axis=0)
-
-    def left(ref, second, start):
-        return jnp.concatenate([ref[:, start : start + HALF], second[:, start : start + HALF]], axis=0)
-
-    outer = right(df, df_o, 0)
-    attn = right(dz, dz_o, 0)
-    for f in range(2):
-        for m in range(4):
-            put(*((1, f, m) if m < 3 else (0, f, 0)), tn(left(g, g_o, f * 1536 + m * HALF), outer))
-        rows = left(yb, yb_o, f * HALF)
-        for m in range(4):
-            put(*((2, f, m) if m < 3 else (0, f, 1)), tn(rows, right(du, du_o, m * D)))
-        put(0, f, 2, tn(left(a, a_o, f * HALF), attn))
-    pl.semaphore_wait(barrier, 37 + 16 * lax.rem(xl + core, 2))
-
-    def first(part):
-        m, n = part
-        late = 0 if part is EARLY else 4
-
-        def one(k, carry):
-            e = wrap(x_at + k, 4)
-            send(
-                g1.at[:, wrap(y + k, 4), pl.ds(m, n)], r1.at[k - 1, :, pl.ds(m, n)],
-                a_out.at[late + 1, k], a_in.at[late + 1, k], at_yz(k * 4),
+    def hello_all():
+        lax.fori_loop(1, 16, hello_yz, 0)
+        lax.fori_loop(1, 10, hello_x, 0)
+        lax.fori_loop(1, 4, hello_row, 0)
+        greet(barrier, sibling)
+
+        @pl.when(jnp.logical_not(turn.stays))
+        def _():
+            lax.fori_loop(0, 16, hello_turn, 0)
+
+    def ready():
+        pl.semaphore_wait(barrier, 37 + 16 * lax.rem(xl + core, 2))
+
+    def run():
+        def put(slab, f, m, value):
+            blocks = value.astype(BF).reshape(4, 2, 48, HALF)
+            if slab == 1:
+                g1[f, :, m] = blocks
+            else:
+                (g0 if slab == 0 else g2)[f, m] = blocks
+
+        def right(ref, second, start):
+            cols = pl.ds(pl.multiple_of(start + core * HALF, HALF), HALF)
+            return jnp.concatenate([ref[:, cols], second[:, cols]], axis=0)
+
+        def left(ref, second, start):
+            return jnp.concatenate([ref[:, start : start + HALF], second[:, start : start + HALF]], axis=0)
+
+        outer = right(df, df_o, 0)
+        attn = right(dz, dz_o, 0)
+        for f in range(2):
+            for m in range(4):
+                put(*((1, f, m) if m < 3 else (0, f, 0)), tn(left(g, g_o, f * 1536 + m * HALF), outer))
+            rows = left(yb, yb_o, f * HALF)
+            for m in range(4):
+                put(*((2, f, m) if m < 3 else (0, f, 1)), tn(rows, right(du, du_o, m * D)))
+            put(0, f, 2, tn(left(a, a_o, f * HALF), attn))
+
+        def first(part):
+            m, n = part
+            late = 0 if part is EARLY else 4
+
+            def one(k, carry):
+                e = wrap(x_at + k, 4)
+                send(
+                    g1.at[:, wrap(y + k, 4), pl.ds(m, n)], r1.at[k - 1, :, pl.ds(m, n)],
+                    a_out.at[late + 1, k], a_in.at[late + 1, k], at_yz(k * 4),
+                )
+                send(
+                    g2.at[:, pl.ds(m, n), wrap(z + k, 4)], r2.at[k - 1, :, pl.ds(m, n)],
+                    a_out.at[late + 2, k], a_in.at[late + 2, k], at_yz(k),
+                )
+                send(
+                    g0.at[lax.div(e, 2), pl.ds(m, n), :, lax.rem(e, 2)], r0.at[k - 1, pl.ds(m, n)],
+                    a_out.at[late, k], a_in.at[late, k], along_x(k),
+                )
+                return carry
+
+            lax.fori_loop(1, 4, one, 0)
+
+        first(EARLY)
+
+        da_end()
+        for h in range(3):
+            rows = stack_head(q_ref, h)
+            rows_q[h] = rows
+            qt[h] = turned(rows)
+            rows = stack_head(da_ref, h)
+            rows_d[h] = rows
+            flipped = rows.astype(F32).T
+            dt[h] = flipped.astype(BF)
+            delta[h] = jnp.sum(flipped * ot_ref[h], axis=0, keepdims=True)
+        acc[...] = jnp.zeros_like(acc)
+
+        def compute(k):
+            i, j = turn.ahead(k, 16)
+            kv = load_chunk(kv_ref, (i, j))
+            keys, values = [], []
+            for h in range(3):
+                key = kv[:, h * HD : (h + 1) * HD]
+                value = kv[:, GROUP + h * HD : GROUP + (h + 1) * HD]
+                probs = jnp.exp(nn(key, qt[h]) - lse_ref[h])
+                slopes = (probs * (nn(value, dt[h]) - delta[h])).astype(BF)
+                keys.append(nn(slopes, rows_q[h]).astype(BF))
+                values.append(nn(probs.astype(BF), rows_d[h]).astype(BF))
+                acc[h] += tn(key, slopes)
+            dkv[lax.rem(k, 4)] = jnp.concatenate(keys + values, axis=1).reshape(2, ROWS, HALF)
+
+        def work(k):
+            compute(k)
+            pass_half(k)
+
+        def pass_half(k):
+            i, j = turn.ahead(k, 16)
+            send(dkv.at[lax.rem(k, 4), 1 - core], other.at[i, j], fs.at[k], fr.at[k], sibling)
+
+        def join(k):
+            i, j = turn.ahead(k, 16)
+            finish(other.at[i, j], other.at[i, j], fs.at[k], fr.at[k], sibling)
+            other[i, j] = (dkv[lax.rem(k, 4), core].astype(F32) + other[i, j].astype(F32)).astype(BF)
+
+        def relay(k):
+            join(k)
+            turn.push(k, 16, other.at[turn.ahead(k, 16)], home.at[y, z], ks, kr)
+
+        for k in range(3):
+            work(k)
+        join(0)
+        turn.first(16, other.at[y, z], home.at[y, z], ks, kr)
+
+        def step(k, carry):
+            work(k)
+            relay(k - 2)
+            return carry
+
+        def finish_up(k, carry):
+            relay(k)
+            return carry
+
+        lax.fori_loop(3, 16, step, 0)
+        lax.fori_loop(14, 16, finish_up, 0)
+        heads = [(acc[h] * 0.125).T.astype(BF) for h in range(3)]
+        heads.append(jnp.zeros((512, 64), BF))
+        turned_back = jnp.concatenate(heads, axis=1)
+        for i in range(4):
+            dq[i] = turned_back[i * ROWS : (i + 1) * ROWS]
+        turn.mates(dq, dqo, qs, qr)
+
+        here = device(y, z, xl, core, half)
+
+        def second(part):
+            m, n = part
+            late = 0 if part is EARLY else 4
+
+            def add(slab, own, got, to, count, where):
+                for k in range(1, 4):
+                    piece = got.at[k - 1, pl.ds(m, n)] if slab == 0 else got.at[k - 1, :, pl.ds(m, n)]
+                    finish(piece, piece, a_out.at[late + slab, k], a_in.at[late + slab, k], here)
+
+                def one(i, carry):
+                    p = where(i)
+                    total = own(p).astype(F32)
+                    for k in range(3):
+                        total = total + got[(k,) + p].astype(F32)
+                    to[p] = total.astype(BF)
+                    return carry
+
+                lax.fori_loop(0, count, one, 0)
+
+            def push(slab, src, got, k, where):
+                @pl.when(k > 0)
+                def _():
+                    send(src, got.at[k], b_out.at[slab, k], b_in.at[slab, k], where)
+
+            def spot(i):
+                return lax.div(i, 2 * n), m + lax.rem(lax.div(i, 2), n), lax.rem(i, 2)
+
+            add(1, lambda p: g1[p[0], y, p[1], p[2]], r1, s1, 4 * n, spot)
+
+            def push1(i, carry):
+                e, to = wrap(x_at + lax.div(i, n), 4), m + lax.rem(i, n)
+                k = lax.div(i, n) * 4 + wrap(to - z, 4)
+                push(1, s1.at[lax.div(e, 2), to, lax.rem(e, 2)], t1, k, at(e, y, to))
+                return carry
+
+            lax.fori_loop(0, 4 * n, push1, 0)
+            add(2, lambda p: g2[p[0], p[1], z, p[2]], r2, s2, 4 * n, spot)
+
+            def push2(i, carry):
+                e, to = wrap(x_at + lax.div(i, n), 4), m + lax.rem(i, n)
+                k = lax.div(i, n) * 4 + wrap(to - y, 4)
+                push(2, s2.at[lax.div(e, 2), to, lax.rem(e, 2)], t2, k, at(e, to, z))
+                return carry
+
+            lax.fori_loop(0, 4 * n, push2, 0)
+            add(
+                0, lambda p: g0[half, p[0], p[1], xl], r0, s0, 4 * n,
+                lambda i: (m + lax.div(i, 4), lax.rem(i, 4)),
             )
-            send(
-                g2.at[:, pl.ds(m, n), wrap(z + k, 4)], r2.at[k - 1, :, pl.ds(m, n)],
-                a_out.at[late + 2, k], a_in.at[late + 2, k], at_yz(k),
-            )
-            send(
-                g0.at[lax.div(e, 2), pl.ds(m, n), :, lax.rem(e, 2)], r0.at[k - 1, pl.ds(m, n)],
-                a_out.at[late, k], a_in.at[late, k], along_x(k),
-            )
+
+            def push0(i, carry):
+                e, to = wrap(z + lax.div(i, n), 4), m + lax.rem(i, n)
+                k = wrap(to - y, 4) * 4 + lax.div(i, n)
+                push(0, s0.at[to, e], t0, k, at(x_at, to, e))
+                return carry
+
+            lax.fori_loop(0, 4 * n, push0, 0)
+
+        turn.mates_end(dqo, qs, qr)
+        turn.end_first(16, home.at[y, z], ks, kr)
+
+        def done(k, carry):
+            turn.end(k, 16, home.at[turn.behind(k, 16)], ks, kr)
             return carry
 
-        lax.fori_loop(1, 4, one, 0)
-
-    first(EARLY)
-
-    def work(k):
-        i, j = turn.ahead(k, 16)
-        kv = load_chunk(kv_ref, (i, j))
-        keys, values = [], []
-        for h in range(3):
-            key = kv[:, h * HD : (h + 1) * HD]
-            value = kv[:, GROUP + h * HD : GROUP + (h + 1) * HD]
-            probs = jnp.exp(nn(key, qt[h]) - lse_ref[h])
-            slopes = (probs * (nn(value, dt[h]) - delta[h])).astype(BF)
-            keys.append(nn(slopes, rows_q[h]).astype(BF))
-            values.append(nn(probs.astype(BF), rows_d[h]).astype(BF))
-            acc[h] += tn(key, slopes)
-        dkv[i, j] = jnp.concatenate(keys + values, axis=1).reshape(2, ROWS, HALF)
-        send(dkv.at[i, j, 1 - core], other.at[i, j], fs.at[k], fr.at[k], sibling)
-
-    def join(k):
-        i, j = turn.ahead(k, 16)
-        finish(other.at[i, j], other.at[i, j], fs.at[k], fr.at[k], sibling)
-        other[i, j] = (dkv[i, j, core].astype(F32) + other[i, j].astype(F32)).astype(BF)
-
-    def relay(k):
-        join(k)
-        turn.push(k, 16, other.at[turn.ahead(k, 16)], home.at[y, z], ks, kr)
-
-    work(0)
-    work(1)
-    join(0)
-    turn.first(16, other.at[y, z], home.at[y, z], ks, kr)
-
-    def step(k, carry):
-        work(k)
-        relay(k - 1)
-        return carry
-
-    lax.fori_loop(2, 16, step, 0)
-    relay(15)
-    heads = [(acc[h] * 0.125).T.astype(BF) for h in range(3)]
-    heads.append(jnp.zeros((512, 64), BF))
-    turned_back = jnp.concatenate(heads, axis=1)
-    for i in range(4):
-        dq[i] = turned_back[i * ROWS : (i + 1) * ROWS]
-    turn.mates(dq, dqo, qs, qr)
-
-    here = device(y, z, xl, core, half)
-
-    def second(part):
-        m, n = part
-        late = 0 if part is EARLY else 4
-
-        def add(slab, own, got, to, count, where):
+        lax.fori_loop(1, 16, done, 0)
+        low[0] = jnp.concatenate([dqo[i][:, :GROUP] for i in range(4)], axis=1)
+        sums = []
+        for i in range(4):
+            total = home[0, i].astype(F32)
             for k in range(1, 4):
-                piece = got.at[k - 1, pl.ds(m, n)] if slab == 0 else got.at[k - 1, :, pl.ds(m, n)]
-                finish(piece, piece, a_out.at[late + slab, k], a_in.at[late + slab, k], here)
-
-            def one(i, carry):
-                p = where(i)
-                total = own(p).astype(F32)
-                for k in range(3):
-                    total = total + got[(k,) + p].astype(F32)
-                to[p] = total.astype(BF)
+                total = total + home[k, i].astype(F32)
+            sums.append(total.astype(BF))
+        low[1] = jnp.concatenate([v[:, :GROUP] for v in sums], axis=1)
+        low[2] = jnp.concatenate([v[:, GROUP:] for v in sums], axis=1)
+        send(low, low_o, ls, lr, sibling)
+        second(EARLY)
+        finish(low, low_o, ls, lr, sibling)
+        cols = pl.ds(pl.multiple_of(core * HALF, HALF), HALF)
+        both_low = [jnp.concatenate([low[i, :, cols], low_o[i, :, cols]], axis=0) for i in range(3)]
+        for f in range(2):
+            rows = left(x, x_o, f * HALF)
+            for i, slab in enumerate((2, 1, 0)):
+                put(slab, f, 3, tn(rows, both_low[i]))
+        first(LATE)
+        grad = dh1_ref[...]
+        for i in range(3):
+            grad = grad + nt(low[i], w_ref[i])
+        grad_ref[...] = grad
+        vg[...] = vg_in[...]
+        for row, i in ((0, 0), (1, 2)):
+            value = column(low[i].astype(F32))
+            for f in range(2):
+                vg[f, row : row + 1, :] = value[:, f * HALF : (f + 1) * HALF]
+
+        def first3(k, carry):
+            src = vg.at[lax.div(wrap(x_at + k, 4), 2)]
+            send(src, rv.at[k - 1], a_out.at[3, k], a_in.at[3, k], along_x(k))
+            return carry
+
+        lax.fori_loop(1, 4, first3, 0)
+
+        def third(part):
+            early = part is EARLY
+
+            def whole(own, got, slab):
+                def wait(k, carry):
+                    arrived(got.at[k], b_in.at[slab, k], here)
+                    return carry
+
+                lax.fori_loop(1, 16, wait, 0)
+
+                def one(k, total):
+                    return total + got[k].astype(F32)
+
+                out[core, slab, y, z, xl] = lax.fori_loop(1, 16, one, own.astype(F32)).astype(BF)
+
+            def spread(slab, count, where):
+                mine = out.at[core, slab, y, z, xl]
+
+                def one(k, carry):
+                    send(mine, mine, c_out.at[slab, k], c_in.at[slab, k], where(k))
+                    return carry
+
+                lax.fori_loop(1, count, one, 0)
+
+            @pl.when(z < 3 if early else z == 3)
+            def _():
+                whole(s1[half, z, xl], t1, 1)
+                spread(1, 8, lambda k: device(y, wrap(z + lax.div(k, 2), 4), wrap(xl + lax.rem(k, 2), 2), core, half))
+
+            @pl.when(y < 3 if early else y == 3)
+            def _():
+                whole(s2[half, y, xl], t2, 2)
+                spread(2, 8, lambda k: device(wrap(y + lax.div(k, 2), 4), z, wrap(xl + lax.rem(k, 2), 2), core, half))
+                whole(s0[y, z], t0, 0)
+                spread(0, 16, at_yz)
+
+        def fourth(part):
+            m, n = part
+            late = 0 if part is EARLY else 3
+
+            def wait(slab, piece, k):
+                @pl.when(k > 0)
+                def _():
+                    arrived(piece, c_in.at[slab, k], here)
+
+            def got1(i, carry):
+                zz, xx = m + lax.div(i, 2), lax.rem(i, 2)
+                wait(1, out.at[core, 1, y, zz, xx], wrap(z - zz, 4) * 2 + wrap(xl - xx, 2))
                 return carry
 
-            lax.fori_loop(0, count, one, 0)
-
-        def push(slab, src, got, k, where):
-            @pl.when(k > 0)
-            def _():
-                send(src, got.at[k], b_out.at[slab, k], b_in.at[slab, k], where)
-
-        def spot(i):
-            return lax.div(i, 2 * n), m + lax.rem(lax.div(i, 2), n), lax.rem(i, 2)
-
-        add(1, lambda p: g1[p[0], y, p[1], p[2]], r1, s1, 4 * n, spot)
-
-        def push1(i, carry):
-            e, to = wrap(x_at + lax.div(i, n), 4), m + lax.rem(i, n)
-            k = lax.div(i, n) * 4 + wrap(to - z, 4)
-            push(1, s1.at[lax.div(e, 2), to, lax.rem(e, 2)], t1, k, at(e, y, to))
+            lax.fori_loop(0, 2 * n, got1, 0)
+
+            def push1(k, carry):
+                mine = out.at[core, 1, y, pl.ds(m, n)]
+                send(mine, mine, d_out.at[late + 1, k], d_in.at[late + 1, k], at_yz(k * 4))
+                return carry
+
+            lax.fori_loop(1, 4, push1, 0)
+
+            def got2(i, carry):
+                yy, xx = m + lax.div(i, 2), lax.rem(i, 2)
+                wait(2, out.at[core, 2, yy, z, xx], wrap(y - yy, 4) * 2 + wrap(xl - xx, 2))
+                return carry
+
+            lax.fori_loop(0, 2 * n, got2, 0)
+
+            def push2(k, carry):
+                mine = out.at[core, 2, pl.ds(m, n), z]
+                send(mine, mine, d_out.at[late + 2, k], d_in.at[late + 2, k], at_yz(k))
+                return carry
+
+            lax.fori_loop(1, 4, push2, 0)
+
+            def got0(i, carry):
+                yy, zz = m + lax.div(i, 4), lax.rem(i, 4)
+                wait(0, out.at[core, 0, yy, zz, xl], wrap(y - yy, 4) * 4 + wrap(z - zz, 4))
+                return carry
+
+            lax.fori_loop(0, 4 * n, got0, 0)
+            mine0 = out.at[core, 0, pl.ds(m, n), :, xl]
+            send(mine0, mine0, d_out.at[late, 1], d_in.at[late, 1], device(y, z, 1 - xl, core, half))
+
+        def own_part(slab, who, part):
+            m, n = part
+            return out.at[who, 1, :, pl.ds(m, n)] if slab == 1 else out.at[who, slab, pl.ds(m, n)]
+
+        def last(part):
+            m, n = part
+            late = 0 if part is EARLY else 3
+
+            def got1(k, carry):
+                piece = out.at[core, 1, wrap(y - k, 4), pl.ds(m, n)]
+                finish(piece, piece, d_out.at[late + 1, k], d_in.at[late + 1, k], here)
+                return carry
+
+            def got2(k, carry):
+                piece = out.at[core, 2, pl.ds(m, n), wrap(z - k, 4)]
+                finish(piece, piece, d_out.at[late + 2, k], d_in.at[late + 2, k], here)
+                return carry
+
+            def onward(slab):
+                piece = own_part(slab, core, part)
+                send(piece, piece, e_out.at[late + slab], e_in.at[late + slab], sibling)
+
+            lax.fori_loop(1, 4, got1, 0)
+            onward(1)
+            lax.fori_loop(1, 4, got2, 0)
+            onward(2)
+            piece0 = out.at[core, 0, pl.ds(m, n), :, 1 - xl]
+            finish(piece0, piece0, d_out.at[late, 1], d_in.at[late, 1], here)
+            onward(0)
+
+        third(EARLY)
+        for k in range(1, 4):
+            finish(rv.at[k - 1], rv.at[k - 1], a_out.at[3, k], a_in.at[3, k], here)
+        part_sum = vg[half] + rv[0] + rv[1] + rv[2]
+        sv[...] = part_sum.astype(BF)
+
+        def second3(k, carry):
+            send(sv, tv.at[k], b_out.at[3, k], b_in.at[3, k], at_yz(k))
             return carry
 
-        lax.fori_loop(0, 4 * n, push1, 0)
-        add(2, lambda p: g2[p[0], p[1], z, p[2]], r2, s2, 4 * n, spot)
-
-        def push2(i, carry):
-            e, to = wrap(x_at + lax.div(i, n), 4), m + lax.rem(i, n)
-            k = lax.div(i, n) * 4 + wrap(to - y, 4)
-            push(2, s2.at[lax.div(e, 2), to, lax.rem(e, 2)], t2, k, at(e, to, z))
-            return carry
-
-        lax.fori_loop(0, 4 * n, push2, 0)
-        add(
-            0, lambda p: g0[half, p[0], p[1], xl], r0, s0, 4 * n,
-            lambda i: (m + lax.div(i, 4), lax.rem(i, 4)),
-        )
-
-        def push0(i, carry):
-            e, to = wrap(z + lax.div(i, n), 4), m + lax.rem(i, n)
-            k = wrap(to - y, 4) * 4 + lax.div(i, n)
-            push(0, s0.at[to, e], t0, k, at(x_at, to, e))
-            return carry
-
-        lax.fori_loop(0, 4 * n, push0, 0)
-
-    turn.mates_end(dqo, qs, qr)
-    turn.end_first(16, home.at[y, z], ks, kr)
-
-    def done(k, carry):
-        turn.end(k, 16, home.at[turn.behind(k, 16)], ks, kr)
-        return carry
-
-    lax.fori_loop(1, 16, done, 0)
-    low[0] = jnp.concatenate([dqo[i][:, :GROUP] for i in range(4)], axis=1)
-    sums = []
-    for i in range(4):
-        total = home[0, i].astype(F32)
-        for k in range(1, 4):
-            total = total + home[k, i].astype(F32)
-        sums.append(total.astype(BF))
-    low[1] = jnp.concatenate([v[:, :GROUP] for v in sums], axis=1)
-    low[2] = jnp.concatenate([v[:, GROUP:] for v in sums], axis=1)
-    send(low, low_o, ls, lr, sibling)
-    second(EARLY)
-    finish(low, low_o, ls, lr, sibling)
-    cols = pl.ds(pl.multiple_of(core * HALF, HALF), HALF)
-    both_low = [jnp.concatenate([low[i, :, cols], low_o[i, :, cols]], axis=0) for i in range(3)]
-    for f in range(2):
-        rows = left(x, x_o, f * HALF)
-        for i, slab in enumerate((2, 1, 0)):
-            put(slab, f, 3, tn(rows, both_low[i]))
-    first(LATE)
-    grad = dh1_ref[...]
-    for i in range(3):
-        grad = grad + nt(low[i], w_ref[i])
-    grad_ref[...] = grad
-    vg[...] = vg_in[...]
-    for row, i in ((0, 0), (1, 2)):
-        value = column(low[i].astype(F32))
-        for f in range(2):
-            vg[f, row : row + 1, :] = value[:, f * HALF : (f + 1) * HALF]
-
-    def first3(k, carry):
-        src = vg.at[lax.div(wrap(x_at + k, 4), 2)]
-        send(src, rv.at[k - 1], a_out.at[3, k], a_in.at[3, k], along_x(k))
-        return carry
-
-    lax.fori_loop(1, 4, first3, 0)
-
-    def third(part):
-        early = part is EARLY
-
-        def whole(own, got, slab):
-            def wait(k, carry):
-                arrived(got.at[k], b_in.at[slab, k], here)
+        lax.fori_loop(1, 16, second3, 0)
+        second(LATE)
+        fourth(EARLY)
+        third(LATE)
+
+        def done3(k, total):
+            finish(tv.at[k], tv.at[k], b_out.at[3, k], b_in.at[3, k], here)
+            return total + tv[k].astype(F32)
+
+        vo[...] = lax.fori_loop(1, 16, done3, part_sum)
+        send(vo, uv, e_out.at[6], e_in.at[6], sibling)
+        fourth(LATE)
+        last(EARLY)
+        last(LATE)
+        for late, part in ((0, EARLY), (3, LATE)):
+            for slab in range(3):
+                piece = own_part(slab, 1 - core, part)
+                finish(piece, piece, e_out.at[late + slab], e_in.at[late + slab], here)
+        for slab, count, own, got in ((1, 8, s1, t1), (2, 8, s2, t2), (0, 16, s0, t0)):
+            mine = out.at[core, slab, y, z, xl]
+
+            def gone2(k, carry):
+                left_here(got.at[k], b_out.at[slab, k], here)
                 return carry
 
-            lax.fori_loop(1, 16, wait, 0)
-
-            def one(k, total):
-                return total + got[k].astype(F32)
-
-            out[core, slab, y, z, xl] = lax.fori_loop(1, 16, one, own.astype(F32)).astype(BF)
-
-        def spread(slab, count, where):
-            mine = out.at[core, slab, y, z, xl]
-
-            def one(k, carry):
-                send(mine, mine, c_out.at[slab, k], c_in.at[slab, k], where(k))
+            def gone3(k, carry):
+                left_here(mine, c_out.at[slab, k], here)
                 return carry
 
-            lax.fori_loop(1, count, one, 0)
-
-        @pl.when(z < 3 if early else z == 3)
-        def _():
-            whole(s1[half, z, xl], t1, 1)
-            spread(1, 8, lambda k: device(y, wrap(z + lax.div(k, 2), 4), wrap(xl + lax.rem(k, 2), 2), core, half))
-
-        @pl.when(y < 3 if early else y == 3)
-        def _():
-            whole(s2[half, y, xl], t2, 2)
-            spread(2, 8, lambda k: device(wrap(y + lax.div(k, 2), 4), z, wrap(xl + lax.rem(k, 2), 2), core, half))
-            whole(s0[y, z], t0, 0)
-            spread(0, 16, at_yz)
-
-    def fourth(part):
-        m, n = part
-        late = 0 if part is EARLY else 3
-
-        def wait(slab, piece, k):
-            @pl.when(k > 0)
-            def _():
-                arrived(piece, c_in.at[slab, k], here)
-
-        def got1(i, carry):
-            zz, xx = m + lax.div(i, 2), lax.rem(i, 2)
-            wait(1, out.at[core, 1, y, zz, xx], wrap(z - zz, 4) * 2 + wrap(xl - xx, 2))
-            return carry
-
-        lax.fori_loop(0, 2 * n, got1, 0)
-
-        def push1(k, carry):
-            mine = out.at[core, 1, y, pl.ds(m, n)]
-            send(mine, mine, d_out.at[late + 1, k], d_in.at[late + 1, k], at_yz(k * 4))
-            return carry
-
-        lax.fori_loop(1, 4, push1, 0)
-
-        def got2(i, carry):
-            yy, xx = m + lax.div(i, 2), lax.rem(i, 2)
-            wait(2, out.at[core, 2, yy, z, xx], wrap(y - yy, 4) * 2 + wrap(xl - xx, 2))
-            return carry
-
-        lax.fori_loop(0, 2 * n, got2, 0)
-
-        def push2(k, carry):
-            mine = out.at[core, 2, pl.ds(m, n), z]
-            send(mine, mine, d_out.at[late + 2, k], d_in.at[late + 2, k], at_yz(k))
-            return carry
-
-        lax.fori_loop(1, 4, push2, 0)
-
-        def got0(i, carry):
-            yy, zz = m + lax.div(i, 4), lax.rem(i, 4)
-            wait(0, out.at[core, 0, yy, zz, xl], wrap(y - yy, 4) * 4 + wrap(z - zz, 4))
-            return carry
-
-        lax.fori_loop(0, 4 * n, got0, 0)
-        mine0 = out.at[core, 0, pl.ds(m, n), :, xl]
-        send(mine0, mine0, d_out.at[late, 1], d_in.at[late, 1], device(y, z, 1 - xl, core, half))
-
-    def own_part(slab, who, part):
-        m, n = part
-        return out.at[who, 1, :, pl.ds(m, n)] if slab == 1 else out.at[who, slab, pl.ds(m, n)]
-
-    def last(part):
-        m, n = part
-        late = 0 if part is EARLY else 3
-
-        def got1(k, carry):
-            piece = out.at[core, 1, wrap(y - k, 4), pl.ds(m, n)]
-            finish(piece, piece, d_out.at[late + 1, k], d_in.at[late + 1, k], here)
-            return carry
-
-        def got2(k, carry):
-            piece = out.at[core, 2, pl.ds(m, n), wrap(z - k, 4)]
-            finish(piece, piece, d_out.at[late + 2, k], d_in.at[late + 2, k], here)
-            return carry
-
-        def onward(slab):
-            piece = own_part(slab, core, part)
-            send(piece, piece, e_out.at[late + slab], e_in.at[late + slab], sibling)
-
-        lax.fori_loop(1, 4, got1, 0)
-        onward(1)
-        lax.fori_loop(1, 4, got2, 0)
-        onward(2)
-        piece0 = out.at[core, 0, pl.ds(m, n), :, 1 - xl]
-        finish(piece0, piece0, d_out.at[late, 1], d_in.at[late, 1], here)
-        onward(0)
-
-    third(EARLY)
-    for k in range(1, 4):
-        finish(rv.at[k - 1], rv.at[k - 1], a_out.at[3, k], a_in.at[3, k], here)
-    part_sum = vg[half] + rv[0] + rv[1] + rv[2]
-    sv[...] = part_sum.astype(BF)
-
-    def second3(k, carry):
-        send(sv, tv.at[k], b_out.at[3, k], b_in.at[3, k], at_yz(k))
-        return carry
-
-    lax.fori_loop(1, 16, second3, 0)
-    second(LATE)
-    fourth(EARLY)
-    third(LATE)
-
-    def done3(k, total):
-        finish(tv.at[k], tv.at[k], b_out.at[3, k], b_in.at[3, k], here)
-        return total + tv[k].astype(F32)
-
-    vo[...] = lax.fori_loop(1, 16, done3, part_sum)
-    send(vo, uv, e_out.at[6], e_in.at[6], sibling)
-    fourth(LATE)
-    last(EARLY)
-    last(LATE)
-    for late, part in ((0, EARLY), (3, LATE)):
-        for slab in range(3):
-            piece = own_part(slab, 1 - core, part)
-            finish(piece, piece, e_out.at[late + slab], e_in.at[late + slab], here)
-    for slab, count, own, got in ((1, 8, s1, t1), (2, 8, s2, t2), (0, 16, s0, t0)):
-        mine = out.at[core, slab, y, z, xl]
-
-        def gone2(k, carry):
-            left_here(got.at[k], b_out.at[slab, k], here)
-            return carry
-
-        def gone3(k, carry):
-            left_here(mine, c_out.at[slab, k], here)
-            return carry
-
-        lax.fori_loop(1, 16, gone2, 0)
-        lax.fori_loop(1, count, gone3, 0)
-    finish(uv, uv, e_out.at[6], e_in.at[6], here)
-    vo[...] = vo[...] + uv[...]
-
-
-def back(*arrays):
+            lax.fori_loop(1, 16, gone2, 0)
+            lax.fori_loop(1, count, gone3, 0)
+        finish(uv, uv, e_out.at[6], e_in.at[6], here)
+        vo[...] = vo[...] + uv[...]
+
+    return hello_all, ready, run
+
+
+BLOCK_ACTS = ((ROWS, D), (ROWS, D), (ROWS, FF), (ROWS, D), (ROWS, FF), (ROWS, D))
+
+
+def rest_kernel(
+    x, ct, mixed, w_i, w_u, w_o, vec, bi, q, kv, ot, lse, x_o, w_qkv,
+    layer_ref, grad_ref, out, vo,
+    dh1, da, vg_in, a, yb, g, df, du, dz, a_o, yb_o, g_o, df_o, du_o, dz_o, slope, da_out, *more,
+):
+    (outs, ins, p_out, p_in), more = more[:4], more[4:]
+    turn = Turn()
+    hello_all, ready, run = back_part(
+        turn, lambda: turn.mates_end(da, outs, ins), q, kv, da, ot, lse, x, x_o, yb, yb_o, g, g_o, a, a_o, df, df_o,
+        du, du_o, dz, dz_o, dh1, w_qkv, vg_in, grad_ref, out, vo, *more,
+    )
+    hello_all()
+    block_part(
+        turn, ready, x, ct, mixed, w_i, w_u, w_o, vec, bi, layer_ref, dh1, da, a, yb, g, df, du, dz, vg_in,
+        a_o, yb_o, g_o, df_o, du_o, dz_o, slope, da_out, outs, ins, p_out, p_in,
+    )
+    run()
+
+
+def rest(*arrays):
     blk = (48, HALF)
-    scratch = [
+    acts = [(v, BF) for v in BLOCK_ACTS]
+    first = [((ROWS, D), F32), ((4, ROWS, 256), BF), ((2, 16, HALF), F32)] + acts + acts + [
+        ((ROWS, FF), F32), ((4, ROWS, 256), BF),
+    ]
+    second = [
         ((3, 512, HD), BF), ((3, HD, 512), BF), ((3, 512, HD), BF), ((3, HD, 512), BF), ((3, 1, 512), F32),
-        ((3, HD, 512), F32), ((4, 4, 2, ROWS, HALF), BF), ((4, 4, ROWS, HALF), BF),
+        ((3, HD, 512), F32), ((4, 2, ROWS, HALF), BF), ((4, 4, ROWS, HALF), BF),
         ((4, ROWS, 256), BF), ((4, ROWS, 256), BF), ((4, 4, ROWS, HALF), BF), ((3, ROWS, D), BF), ((3, ROWS, D), BF),
         ((2, 16, HALF), F32),
         ((2, 4, 4, 2, *blk), BF), ((2, 4, 4, 2, *blk), BF), ((2, 4, 4, 2, *blk), BF),
@@ -1076,21 +1123,22 @@
         ((3, 16, HALF), F32), ((16, HALF), BF), ((16, 16, HALF), BF), ((16, HALF), F32),
     ]
     return pl.pallas_call(
-        back_kernel,
-        name="back",
-        cost_estimate=cost(100),
+        rest_kernel,
+        name="rest",
+        cost_estimate=cost(130),
         out_shape=(
-            shape(ROWS, D, dtype=F32), shape(2, 3, 4, 4, 2, *blk), shape(16, HALF, dtype=F32),
+            shape(ROWS, D), shape(ROWS, D, dtype=F32), shape(2, 3, 4, 4, 2, *blk), shape(16, HALF, dtype=F32),
         ),
-        in_specs=[VM] * 22,
-        out_specs=(VM,) * 3,
-        scratch_shapes=[pltpu.VMEM(*v) for v in scratch] + [
+        in_specs=[VM] * 14,
+        out_specs=(VM,) * 4,
+        scratch_shapes=[pltpu.VMEM(*v) for v in first] + [DMA((4,)), DMA((4,)), DMA((6,)), DMA((6,))]
+        + [pltpu.VMEM(*v) for v in second] + [
             DMA((16,)), DMA((16,)), DMA((16,)), DMA((16,)), DMA((4,)), DMA((4,)), DMA, DMA,
             DMA((7, 4)), DMA((7, 4)), DMA((4, 16)), DMA((4, 16)), DMA((3, 16)), DMA((3, 16)),
             DMA((6, 4)), DMA((6, 4)), DMA((7,)), DMA((7,)),
         ],
         compiler_params=pltpu.CompilerParams(
-            collective_id=3, has_side_effects=True, vmem_limit_bytes=29 << 20
+            collective_id=3, has_side_effects=True, vmem_limit_bytes=34 << 20
         ),
     )(*map(vm, arrays))
 
@@ -1169,12 +1217,8 @@
         x, w_query, w_key, w_value, b_query, b_value, b_output, first_gain, first_shift, b_outer, second_gain,
         second_shift, b_inner, w_inner, w_outer, w_output,
     )
-    layer_out, dh1, da_all, a, yb, g, df, du, dz, vg, a_o, yb_o, g_o, df_o, du_o, dz_o = block(
-        x, cotangent[0], mixed, w_i, w_u, w_o, vec, bi
-    )
-    tokens_grad, summed, vecs = back(
-        q_all, kv_all, da_all, mixed_t, lse, x, x_o, yb, yb_o, g, g_o, a, a_o, df, df_o, du, du_o, dz, dz_o,
-        dh1, w_qkv, vg,
+    layer_out, tokens_grad, summed, vecs = rest(
+        x, cotangent[0], mixed, w_i, w_u, w_o, vec, bi, q_all, kv_all, mixed_t, lse, x_o, w_qkv
     )
     gq, gk, gv, go, gi, gu, layer_out, tokens_grad, *vecs = spell(summed, vecs, layer_out, tokens_grad)
     return (

time: 215 us -> 200 us (0.930)
  Pallas kernels: 210 us -> 196 us
    pallas_call x1, Pallas kernels: 75.4 us -> 63.4 us  [front(): pl.pallas_call(front_kernel, name='front', cost_estimate=cost(70), out_sh...]
    pallas_call x2 -> x1, Pallas kernels: 128 us -> 125 us  [rest(): pl.pallas_call(rest_kernel, name='rest', cost_estimate=cost(130), out_sha...]
where the time goes in v6:
time: 200 us; the launch traced here: 197 us
  Pallas kernels  196 us (98%)
    pallas_call x1, Pallas kernels, rest(): pl.pallas_call(rest_kernel, name='rest', cost_estimate=cost(130), out_sha...  125 us
    pallas_call x1, Pallas kernels, front(): pl.pallas_call(front_kernel, name='front', cost_estimate=cost(70), out_sh...  63.4 us
    pallas_call x1, Pallas kernels, spell(): pl.pallas_call(spell_kernel, name='spell', out_shape=tuple((plain_shape(*...  6.68 us

profile of v6, /device:TPU:1, one launch (start us, length us, event | category | flops | bytes accessed | tf_op | source)
XLA Modules:
  0.0 197.3 jit_solution(8672217615611695597)
XLA Ops:
  0.7 0.0 copy-start
  0.7 0.9 copy-done
  1.6 0.0 copy-start.1
  1.6 0.0 copy-start.2
  1.6 63.4 %front.1 = (bf16[4,128,256]{2,1,0:T(8,128)(2,1)S(1)}, bf16[4,128,256]{2,1,0:T(8,128)(2,1)S(1)}, bf16[4,4,2,128,384]{4,3,2,1,0:T(8,128)(2,1)S(1)}, f32[3,64,512]{...) custom-call(bf16[128,768]{1,0:T(8,128)(2,1)S(1)} %bitcast.4, ...), custom_call_target="tpu_custom_call" | custom-call | bytes 210000000 | tf_op jit(solution)/shard_map/front/pallas_call | solution.py:523
  65.0 0.0 copy-done.1
  65.0 0.0 copy-done.2
  65.0 125.5 %rest.1 = (bf16[128,768]{1,0:T(8,128)(2,1)S(1)}, f32[128,768]{1,0:T(8,128)S(1)}, bf16[2,3,4,4,2,48,384]{6,5,4,3,2,1,0:T(8,128)(2,1)S(1)}, f32[16,384]{1,0:T(8,128)S(1)}) custom-call(bf16[128,768]{1,0:T(8,128)(2,1)S(1)} %bitcast.5, bf16[128,768]{1,0:T(8,128)(2,1)S(1)} %bitcast.6, bf16[4,128,256]{2,1,0:T(8,128)(2,1)S(1)} %get-tuple-element.50.mixed, ...), custom_call_target="tpu_custom_call" | custom-call | bytes 390000000 | tf_op jit(solution)/shard_map/rest/pallas_call | solution.py:1125
  190.5 6.7 %spell.1 = (f32[384,768]{1,0:T(8,128)}, f32[384,768]{1,0:T(8,128)}, f32[384,768]{1,0:T(8,128)}, f32[384,768]{1,0:T(8,128)}, f32[384,3072]{1,0:T(8,128)}, /*index...) custom-call(bf16[2,3,4,4,2,48,384]{6,5,4,3,2,1,0:T(8,128)(2,1)S(1)} , ...), custom_call_target="tpu_custom_call" | custom-call | bytes 18000000 | tf_op jit(solution)/shard_map/spell/pallas_call | solution.py:1195
Async XLA Ops:
  0.7 0.9 copy-start
  1.6 63.4 %copy-start.1 = (bf16[1,128,768]{2,1,0:T(8,128)(2,1)S(1)}, bf16[1,128,768]{2,1,0:T(8,128)(2,1)}, u32[]{:S(2)}) copy-start(bf16[1,128,768]{2,1,0:T(8,128)(2,1)} %param.17) | copy-start | bytes 589828
  1.6 63.4 %copy-start.2 = (bf16[1,128,768]{2,1,0:T(8,128)(2,1)S(1)}, bf16[1,128,768]{2,1,0:T(8,128)(2,1)}, u32[]{:S(2)}) copy-start(bf16[1,128,768]{2,1,0:T(8,128)(2,1)} %param.18) | copy-start | bytes 589828

commit v7 on v6

--- a/solution.py
+++ b/solution.py
@@ -215,8 +215,29 @@
     return ref[at].reshape(CHUNK, HALF)
 
 
+def packed(heads):
+    low = ROWS // 2
+    return jnp.concatenate(
+        [jnp.concatenate(heads[:2], axis=1), jnp.concatenate([heads[2][:low], heads[2][low:]], axis=1)], axis=0
+    )
+
+
+def packed_columns(value):
+    return packed([value[:, h * HD : (h + 1) * HD] for h in range(3)])
+
+
+def head_of(piece, h):
+    if h < 2:
+        return piece[:ROWS, h * HD : (h + 1) * HD]
+    return jnp.concatenate([piece[ROWS:, :HD], piece[ROWS:, HD:]], axis=0)
+
+
+def unpacked(piece):
+    return jnp.concatenate([piece[:ROWS], head_of(piece, 2)], axis=1)
+
+
 def stack_head(ref, h):
-    return jnp.concatenate([ref[i][:, h * HD : (h + 1) * HD] for i in range(4)], axis=0)
+    return jnp.concatenate([head_of(ref[i], h) for i in range(4)], axis=0)
 
 
 def turned(rows):
@@ -326,8 +347,8 @@
 
 
 def front_kernel(
-    x_ref, wq, wk, wv, v0, v1, v2, v3, v4, v5, v6, v7, v8, wi, wu, wo,
-    a_ref, qo_ref, kvo_ref, ot_ref, lse_ref, w_ref, w_i, w_u, w_o, vec_ref, bi_ref, xo_ref,
+    x_hbm, wq, wk, wv, v0, v1, v2, v3, v4, v5, v6, v7, v8, wi, wu, wo,
+    a_ref, qo_ref, kvo_ref, ot_ref, lse_ref, w_ref, w_i, w_u, w_o, vec_ref, bi_ref, xo_ref, x_ref,
     q_ref, kv_ref, small, small_o, o_ref, qt, top, total,
     own_sem, a_out, a_in, b_out, b_in, p_out, p_in, qs, qr, ks, kr, ms, mr, fs, fr, os, om, own, *rest,
 ):
@@ -362,6 +383,8 @@
     mine = [
         pltpu.make_async_copy(w, w_ref.at[i, pl.ds(rows, HALF)], own_sem.at[i]) for i, w in enumerate((wq, wk, wv))
     ]
+    x_copy = pltpu.make_async_copy(x_hbm, x_ref, own_sem.at[12])
+    x_copy.start()
     for copy in mine:
         copy.start()
     fetch.own_rows()
@@ -391,6 +414,7 @@
     for i in range(4):
         bi_ref[:, i * HALF : (i + 1) * HALF] = ahead[8 + i : 9 + i]
         bi_ref[:, 1536 + i * HALF : 1536 + (i + 1) * HALF] = behind[8 + i : 9 + i]
+    x_copy.wait()
     send(x_ref, xo_ref, a_out.at[4], a_in.at[4], sibling)
     x = x_ref[...]
     for i in (1, 2, 0):
@@ -420,10 +444,9 @@
             turn.mates(kv_ref, kvo_ref.at[y], ks, kr, own=xl)
     fetch.issue(2)
     fetch.issue(3)
-    pad = jnp.zeros((ROWS, 64), BF)
     query = (done[0] + vec_ref[0:1, :]).astype(BF) * BF(0.125)
     for g in range(4):
-        q_ref[g] = jnp.concatenate([query[:, g * GROUP : (g + 1) * GROUP], pad], axis=1)
+        q_ref[g] = packed_columns(query[:, g * GROUP : (g + 1) * GROUP])
     turn.mates(q_ref, qo_ref, qs, qr)
 
     def spot(t):
@@ -507,10 +530,8 @@
         normal = ot_ref[h] / total[h]
         ot_ref[h] = normal
         heads.append(normal.T.astype(BF))
-    heads.append(jnp.zeros((512, 64), BF))
-    out = jnp.concatenate(heads, axis=1)
     for i in range(4):
-        o_ref[i] = out[i * ROWS : (i + 1) * ROWS]
+        o_ref[i] = packed([v[i * ROWS : (i + 1) * ROWS] for v in heads])
     turn.mates(o_ref, a_ref, os, om)
     for c in range(6):
         fetch.step_y(c)
@@ -525,24 +546,24 @@
         name="front",
         cost_estimate=cost(70),
         out_shape=(
-            shape(4, ROWS, 256), shape(4, ROWS, 256), shape(4, 4, 2, ROWS, HALF),
+            shape(4, GROUP, ROWS), shape(4, GROUP, ROWS), shape(4, 4, 2, ROWS, HALF),
             shape(3, HD, 512, dtype=F32), shape(3, 1, 512, dtype=F32),
             shape(3, D, D), shape(D, FF), shape(FF, D), shape(D, D), shape(8, D, dtype=F32), shape(1, FF, dtype=F32),
-            shape(ROWS, D),
+            shape(ROWS, D), shape(ROWS, D),
         ),
-        in_specs=[VM, ANY, ANY, ANY] + [ANY] * 9 + [ANY] * 3,
-        out_specs=(VM,) * 12,
+        in_specs=[ANY, ANY, ANY, ANY] + [ANY] * 9 + [ANY] * 3,
+        out_specs=(VM,) * 13,
         scratch_shapes=[
-            pltpu.VMEM((4, ROWS, 256), BF), pltpu.VMEM((4, ROWS, HALF), BF),
+            pltpu.VMEM((4, GROUP, ROWS), BF), pltpu.VMEM((4, ROWS, HALF), BF),
             pltpu.VMEM((16, HALF), F32), pltpu.VMEM((16, HALF), F32),
-            pltpu.VMEM((4, ROWS, 256), BF),
+            pltpu.VMEM((4, GROUP, ROWS), BF),
             pltpu.VMEM((3, HD, 512), BF), pltpu.VMEM((3, 1, 512), F32), pltpu.VMEM((3, 1, 512), F32),
-            DMA((12,)), DMA((5,)), DMA((5,)), DMA((6,)), DMA((6,)), DMA((3,)), DMA((3,)),
+            DMA((13,)), DMA((5,)), DMA((5,)), DMA((6,)), DMA((6,)), DMA((3,)), DMA((3,)),
             DMA((4,)), DMA((4,)), DMA((4,)), DMA((4,)), DMA((16,)), DMA((16,)), DMA((16,)), DMA((16,)),
             DMA((4,)), DMA((4,)), DMA((3,)),
         ] + [DMA((7,))] * 8 + [pltpu.VMEM((HALF,), BF)] * 8 + [pltpu.VMEM((1536,), BF)],
         compiler_params=remote(1),
-    )(arrays[0], *map(hbm, arrays[1:]))
+    )(*map(hbm, arrays))
 
 
 def norm(hidden):
@@ -573,7 +594,7 @@
 
     b_output, first_gain, first_shift = vec_ref[2:3, :], vec_ref[3:4, :], vec_ref[4:5, :]
     b_outer, second_gain, second_shift = vec_ref[5:6, :], vec_ref[6:7, :], vec_ref[7:8, :]
-    mixed = jnp.concatenate([a_ref[g][:, :GROUP] for g in range(4)], axis=1)
+    mixed = jnp.concatenate([unpacked(a_ref[g]) for g in range(4)], axis=1)
     af_ref[...] = mixed
     hidden = x_ref[...].astype(F32) + nn(mixed, w_o[...]) + b_output
     normal1, inverse1 = norm(hidden)
@@ -630,9 +651,8 @@
     pass_on(5)
     note(2, column(dz.astype(F32)))
     da = nt(dz, w_o[...]).astype(BF)
-    pad = jnp.zeros((ROWS, 64), BF)
     for g in range(4):
-        da_out[g] = jnp.concatenate([da[:, g * GROUP : (g + 1) * GROUP], pad], axis=1)
+        da_out[g] = packed_columns(da[:, g * GROUP : (g + 1) * GROUP])
     turn.mates(da_out, da_ref, outs, ins)
     for n, (src, got) in enumerate(passed):
         finish(src, got, p_out.at[n], p_in.at[n], turn.sibling())
@@ -647,7 +667,7 @@
     dh1_ref, w_ref, vg_in,
     grad_ref, out, vo,
     rows_q, qt, rows_d, dt, delta, acc, dkv, other, dq, dqo, home, low, low_o, vg,
-    g0, g1, g2, r0, r1, r2, s0, s1, s2, t0, t1, t2, rv, sv, tv, uv,
+    g0, g1, g2, r0, r1, r2, s0, s1, s2, t0, t1, t2, rv, sv, sw, tv, uv,
     fs, fr, ks, kr, qs, qr, ls, lr, a_out, a_in, b_out, b_in, c_out, c_in, d_out, d_in, e_out, e_in,
 ):
     y, z, xl, core, half = turn.y, turn.z, turn.xl, turn.core, turn.half
@@ -814,10 +834,8 @@
         lax.fori_loop(3, 16, step, 0)
         lax.fori_loop(14, 16, finish_up, 0)
         heads = [(acc[h] * 0.125).T.astype(BF) for h in range(3)]
-        heads.append(jnp.zeros((512, 64), BF))
-        turned_back = jnp.concatenate(heads, axis=1)
         for i in range(4):
-            dq[i] = turned_back[i * ROWS : (i + 1) * ROWS]
+            dq[i] = packed([v[i * ROWS : (i + 1) * ROWS] for v in heads])
         turn.mates(dq, dqo, qs, qr)
 
         here = device(y, z, xl, core, half)
@@ -888,7 +906,7 @@
             return carry
 
         lax.fori_loop(1, 16, done, 0)
-        low[0] = jnp.concatenate([dqo[i][:, :GROUP] for i in range(4)], axis=1)
+        low[0] = jnp.concatenate([unpacked(dqo[i]) for i in range(4)], axis=1)
         sums = []
         for i in range(4):
             total = home[0, i].astype(F32)
@@ -981,7 +999,8 @@
                 send(mine, mine, d_out.at[late + 1, k], d_in.at[late + 1, k], at_yz(k * 4))
                 return carry
 
-            lax.fori_loop(1, 4, push1, 0)
+            for k in (1, 3) if part is EARLY else (1, 2, 3):
+                push1(k, 0)
 
             def got2(i, carry):
                 yy, xx = m + lax.div(i, 2), lax.rem(i, 2)
@@ -995,7 +1014,8 @@
                 send(mine, mine, d_out.at[late + 2, k], d_in.at[late + 2, k], at_yz(k))
                 return carry
 
-            lax.fori_loop(1, 4, push2, 0)
+            for k in (1, 3) if part is EARLY else (1, 2, 3):
+                push2(k, 0)
 
             def got0(i, carry):
                 yy, zz = m + lax.div(i, 4), lax.rem(i, 4)
@@ -1006,6 +1026,19 @@
             mine0 = out.at[core, 0, pl.ds(m, n), :, xl]
             send(mine0, mine0, d_out.at[late, 1], d_in.at[late, 1], device(y, z, 1 - xl, core, half))
 
+        def hand_on():
+            m, n = EARLY
+            for k, side in ((1, 0), (3, 1)):
+                y_from, z_from = wrap(y - k, 4), wrap(z - k, 4)
+                piece = out.at[core, 1, y_from, pl.ds(m, n)]
+                finish(piece, piece, d_out.at[1, k], d_in.at[1, k], here)
+                part1 = out.at[core, 1, y_from, pl.ds(m, n), side]
+                send(part1, part1, d_out.at[1, 2], d_in.at[1, 2], at_yz(k * 4))
+                piece = out.at[core, 2, pl.ds(m, n), z_from]
+                finish(piece, piece, d_out.at[2, k], d_in.at[2, k], here)
+                part2 = out.at[core, 2, pl.ds(m, n), z_from, side]
+                send(part2, part2, d_out.at[2, 2], d_in.at[2, 2], at_yz(k))
+
         def own_part(slab, who, part):
             m, n = part
             return out.at[who, 1, :, pl.ds(m, n)] if slab == 1 else out.at[who, slab, pl.ds(m, n)]
@@ -1028,9 +1061,11 @@
                 piece = own_part(slab, core, part)
                 send(piece, piece, e_out.at[late + slab], e_in.at[late + slab], sibling)
 
-            lax.fori_loop(1, 4, got1, 0)
+            for k in (2,) if part is EARLY else (1, 2, 3):
+                got1(k, 0)
             onward(1)
-            lax.fori_loop(1, 4, got2, 0)
+            for k in (2,) if part is EARLY else (1, 2, 3):
+                got2(k, 0)
             onward(2)
             piece0 = out.at[core, 0, pl.ds(m, n), :, 1 - xl]
             finish(piece0, piece0, d_out.at[late, 1], d_in.at[late, 1], here)
@@ -1042,41 +1077,44 @@
         part_sum = vg[half] + rv[0] + rv[1] + rv[2]
         sv[...] = part_sum.astype(BF)
 
-        def second3(k, carry):
-            send(sv, tv.at[k], b_out.at[3, k], b_in.at[3, k], at_yz(k))
-            return carry
-
-        lax.fori_loop(1, 16, second3, 0)
+        for k in range(1, 4):
+            send(sv, tv.at[k], b_out.at[3, k], b_in.at[3, k], at_yz(k * 4))
         second(LATE)
+        for k in range(1, 4):
+            finish(tv.at[k], tv.at[k], b_out.at[3, k], b_in.at[3, k], here)
+            part_sum = part_sum + tv[k].astype(F32)
+        sw[...] = part_sum.astype(BF)
+        for k in range(1, 4):
+            send(sw, tv.at[4 + k], b_out.at[3, 4 + k], b_in.at[3, 4 + k], at_yz(k))
         fourth(EARLY)
         third(LATE)
-
-        def done3(k, total):
+        hand_on()
+
+        for k in range(5, 8):
             finish(tv.at[k], tv.at[k], b_out.at[3, k], b_in.at[3, k], here)
-            return total + tv[k].astype(F32)
-
-        vo[...] = lax.fori_loop(1, 16, done3, part_sum)
+            part_sum = part_sum + tv[k].astype(F32)
+        vo[...] = part_sum
         send(vo, uv, e_out.at[6], e_in.at[6], sibling)
         fourth(LATE)
         last(EARLY)
+        for slab, count, own, got in ((1, 8, s1, t1), (2, 8, s2, t2), (0, 16, s0, t0)):
+            mine = out.at[core, slab, y, z, xl]
+
+            def gone2(k, carry):
+                left_here(got.at[k], b_out.at[slab, k], here)
+                return carry
+
+            def gone3(k, carry):
+                left_here(mine, c_out.at[slab, k], here)
+                return carry
+
+            lax.fori_loop(1, 16, gone2, 0)
+            lax.fori_loop(1, count, gone3, 0)
         last(LATE)
         for late, part in ((0, EARLY), (3, LATE)):
             for slab in range(3):
                 piece = own_part(slab, 1 - core, part)
                 finish(piece, piece, e_out.at[late + slab], e_in.at[late + slab], here)
-        for slab, count, own, got in ((1, 8, s1, t1), (2, 8, s2, t2), (0, 16, s0, t0)):
-            mine = out.at[core, slab, y, z, xl]
-
-            def gone2(k, carry):
-                left_here(got.at[k], b_out.at[slab, k], here)
-                return carry
-
-            def gone3(k, carry):
-                left_here(mine, c_out.at[slab, k], here)
-                return carry
-
-            lax.fori_loop(1, 16, gone2, 0)
-            lax.fori_loop(1, count, gone3, 0)
         finish(uv, uv, e_out.at[6], e_in.at[6], here)
         vo[...] = vo[...] + uv[...]
 
@@ -1108,19 +1146,19 @@
 def rest(*arrays):
     blk = (48, HALF)
     acts = [(v, BF) for v in BLOCK_ACTS]
-    first = [((ROWS, D), F32), ((4, ROWS, 256), BF), ((2, 16, HALF), F32)] + acts + acts + [
-        ((ROWS, FF), F32), ((4, ROWS, 256), BF),
+    first = [((ROWS, D), F32), ((4, GROUP, ROWS), BF), ((2, 16, HALF), F32)] + acts + acts + [
+        ((ROWS, FF), F32), ((4, GROUP, ROWS), BF),
     ]
     second = [
         ((3, 512, HD), BF), ((3, HD, 512), BF), ((3, 512, HD), BF), ((3, HD, 512), BF), ((3, 1, 512), F32),
         ((3, HD, 512), F32), ((4, 2, ROWS, HALF), BF), ((4, 4, ROWS, HALF), BF),
-        ((4, ROWS, 256), BF), ((4, ROWS, 256), BF), ((4, 4, ROWS, HALF), BF), ((3, ROWS, D), BF), ((3, ROWS, D), BF),
+        ((4, GROUP, ROWS), BF), ((4, GROUP, ROWS), BF), ((4, 4, ROWS, HALF), BF), ((3, ROWS, D), BF), ((3, ROWS, D), BF),
         ((2, 16, HALF), F32),
         ((2, 4, 4, 2, *blk), BF), ((2, 4, 4, 2, *blk), BF), ((2, 4, 4, 2, *blk), BF),
         ((3, 4, 4, *blk), BF), ((3, 2, 4, 2, *blk), BF), ((3, 2, 4, 2, *blk), BF),
         ((4, 4, *blk), BF), ((2, 4, 2, *blk), BF), ((2, 4, 2, *blk), BF),
         ((16, *blk), BF), ((16, *blk), BF), ((16, *blk), BF),
-        ((3, 16, HALF), F32), ((16, HALF), BF), ((16, 16, HALF), BF), ((16, HALF), F32),
+        ((3, 16, HALF), F32), ((16, HALF), BF), ((16, HALF), BF), ((8, 16, HALF), BF), ((16, HALF), F32),
     ]
     return pl.pallas_call(
         rest_kernel,
@@ -1156,24 +1194,24 @@
     lines[8][...] = jnp.concatenate([vo[8 + i : 9 + i, :] for i in range(4)], axis=1).reshape(1536)
 
     def copies(n):
-        slot = stage.at[n % 2]
+        slot = stage.at[n % 3]
         rows = slice(n * 48, (n + 1) * 48)
         made = [
-            pltpu.make_async_copy(slot.at[m], ref.at[rows], sems.at[n % 2, m])
+            pltpu.make_async_copy(slot.at[m], ref.at[rows], sems.at[n % 3, m])
             for m, ref in enumerate((q_ref, k_ref, v_ref, o_ref))
         ]
         for m in range(4):
             made.append(pltpu.make_async_copy(
-                slot.at[4 + m], i_ref.at[rows, m * D : (m + 1) * D], sems.at[n % 2, 4 + m]
+                slot.at[4 + m], i_ref.at[rows, m * D : (m + 1) * D], sems.at[n % 3, 4 + m]
             ))
             made.append(pltpu.make_async_copy(
-                slot.at[8 + m], u_ref.at[m * HALF + n * 48 : m * HALF + (n + 1) * 48], sems.at[n % 2, 8 + m]
+                slot.at[8 + m], u_ref.at[m * HALF + n * 48 : m * HALF + (n + 1) * 48], sems.at[n % 3, 8 + m]
             ))
         return made
 
     for n in range(8):
-        if n >= 2:
-            for copy in copies(n - 2):
+        if n >= 3:
+            for copy in copies(n - 3):
                 copy.wait()
         i, xl = n // 2, n % 2
         for c in range(2):
@@ -1181,10 +1219,10 @@
             units = [(2, 3), (1, 3), (0, 3), (0, 2), (2, 0), (2, 1), (2, 2), (0, 1), (1, 0), (1, 1), (1, 2), (0, 0)]
             for m, (slab, unit) in enumerate(units):
                 piece = full[c, 1, i, unit, xl] if slab == 1 else full[c, slab, unit, i, xl]
-                stage[n % 2, m, :, cols] = piece.astype(F32)
+                stage[n % 3, m, :, cols] = piece.astype(F32)
         for copy in copies(n):
             copy.start()
-    for n in (6, 7):
+    for n in (5, 6, 7):
         for copy in copies(n):
             copy.wait()
     for copy in straight:
@@ -1202,7 +1240,7 @@
         + (plain_shape(HALF, dtype=F32),) * 8 + (plain_shape(1536, dtype=F32),),
         in_specs=[VM] * 4,
         out_specs=(ANY,) * 8 + (VM,) * 9,
-        scratch_shapes=[pltpu.VMEM((2, 12, 48, D), F32), DMA((2, 12)), DMA((2,))],
+        scratch_shapes=[pltpu.VMEM((3, 12, 48, D), F32), DMA((3, 12)), DMA((2,))],
         compiler_params=plain(),
         cost_estimate=cost(6),
     )(*map(vm, arrays))
@@ -1213,12 +1251,12 @@
     first_gain, first_shift, w_inner, b_inner, w_outer, b_outer, second_gain, second_shift,
 ):
     x = tokens[0]
-    mixed, q_all, kv_all, mixed_t, lse, w_qkv, w_i, w_u, w_o, vec, bi, x_o = front(
+    mixed, q_all, kv_all, mixed_t, lse, w_qkv, w_i, w_u, w_o, vec, bi, x_o, x_in = front(
         x, w_query, w_key, w_value, b_query, b_value, b_output, first_gain, first_shift, b_outer, second_gain,
         second_shift, b_inner, w_inner, w_outer, w_output,
     )
     layer_out, tokens_grad, summed, vecs = rest(
-        x, cotangent[0], mixed, w_i, w_u, w_o, vec, bi, q_all, kv_all, mixed_t, lse, x_o, w_qkv
+        x_in, cotangent[0], mixed, w_i, w_u, w_o, vec, bi, q_all, kv_all, mixed_t, lse, x_o, w_qkv
     )
     gq, gk, gv, go, gi, gu, layer_out, tokens_grad, *vecs = spell(summed, vecs, layer_out, tokens_grad)
     return (

time: 200 us -> 192 us (0.960)
  Pallas kernels: 196 us -> 190 us
    pallas_call x1, Pallas kernels: 125 us -> 122 us  [rest(): pl.pallas_call(rest_kernel, name='rest', cost_estimate=cost(130), out_sha...]
where the time goes in v7:
time: 192 us; the launch traced here: 191 us
  Pallas kernels  190 us (99%)
    pallas_call x1, Pallas kernels, rest(): pl.pallas_call(rest_kernel, name='rest', cost_estimate=cost(130), out_sha...  122 us
    pallas_call x1, Pallas kernels, front(): pl.pallas_call(front_kernel, name='front', cost_estimate=cost(70), out_sh...  62 us
    pallas_call x1, Pallas kernels, spell(): pl.pallas_call(spell_kernel, name='spell', out_shape=tuple((plain_shape(*...  6.26 us

profile of v7, /device:TPU:1, one launch (start us, length us, event | category | flops | bytes accessed | tf_op | source)
XLA Modules:
  0.0 190.8 jit_solution(4609857770122941156)
XLA Ops:
  0.7 0.0 copy-start
  0.7 62.0 %front.1 = (bf16[4,192,128]{2,1,0:T(8,128)(2,1)S(1)}, bf16[4,192,128]{2,1,0:T(8,128)(2,1)S(1)}, bf16[4,4,2,128,384]{4,3,2,1,0:T(8,128)(2,1)S(1)}, f32[3,64,512]{...) custom-call(bf16[128,768]{1,0:T(8,128)(2,1)} %bitcast.5, ...), custom_call_target="tpu_custom_call" | custom-call | bytes 210000000 | tf_op jit(solution)/shard_map/front/pallas_call | solution.py:544
  62.7 0.0 copy-done
  62.7 121.7 %rest.1 = (bf16[128,768]{1,0:T(8,128)(2,1)S(1)}, f32[128,768]{1,0:T(8,128)S(1)}, bf16[2,3,4,4,2,48,384]{6,5,4,3,2,1,0:T(8,128)(2,1)S(1)}, f32[16,384]{1,0:T(8,128)S(1)}) custom-call(bf16[128,768]{1,0:T(8,128)(2,1)S(1)} %get-tuple-element.51.x, bf16[128,768]{1,0:T(8,128)(2,1)S(1)} %bitcast.4, bf16[4,192,128]{2,1,0:T(8,128)(2,1)S(1)} %get-tuple-element.52.mixed, ...), custom_call_target="tpu_custom_call" | custom-call | bytes 390000000 | tf_op jit(solution)/shard_map/rest/pallas_call | solution.py:1163
  184.4 6.3 %spell.1 = (f32[384,768]{1,0:T(8,128)}, f32[384,768]{1,0:T(8,128)}, f32[384,768]{1,0:T(8,128)}, f32[384,768]{1,0:T(8,128)}, f32[384,3072]{1,0:T(8,128)}, /*index...) custom-call(bf16[2,3,4,4,2,48,384]{6,5,4,3,2,1,0:T(8,128)(2,1)S(1)} , ...), custom_call_target="tpu_custom_call" | custom-call | bytes 18000000 | tf_op jit(solution)/shard_map/spell/pallas_call | solution.py:1233
Async XLA Ops:
  0.7 62.0 %copy-start = (bf16[1,128,768]{2,1,0:T(8,128)(2,1)S(1)}, bf16[1,128,768]{2,1,0:T(8,128)(2,1)}, u32[]{:S(2)}) copy-start(bf16[1,128,768]{2,1,0:T(8,128)(2,1)} %param.18) | copy-start | bytes 589828

commit v8 on v7

--- a/solution.py
+++ b/solution.py
@@ -1079,6 +1079,7 @@
 
         for k in range(1, 4):
             send(sv, tv.at[k], b_out.at[3, k], b_in.at[3, k], at_yz(k * 4))
+        fourth(EARLY)
         second(LATE)
         for k in range(1, 4):
             finish(tv.at[k], tv.at[k], b_out.at[3, k], b_in.at[3, k], here)
@@ -1086,7 +1087,6 @@
         sw[...] = part_sum.astype(BF)
         for k in range(1, 4):
             send(sw, tv.at[4 + k], b_out.at[3, 4 + k], b_in.at[3, 4 + k], at_yz(k))
-        fourth(EARLY)
         third(LATE)
         hand_on()
 

time: 192 us -> 196 us (1.021)
  Pallas kernels: 190 us -> 195 us
    pallas_call x1, Pallas kernels: 122 us -> 127 us  [rest(): pl.pallas_call(rest_kernel, name='rest', cost_estimate=cost(130), out_sha...]
where the time goes in v8:
time: 196 us
  Pallas kernels  195 us (99%)
    pallas_call x1, Pallas kernels, rest(): pl.pallas_call(rest_kernel, name='rest', cost_estimate=cost(130), out_sha...  127 us
    pallas_call x1, Pallas kernels, front(): pl.pallas_call(front_kernel, name='front', cost_estimate=cost(70), out_sh...  62 us
    pallas_call x1, Pallas kernels, spell(): pl.pallas_call(spell_kernel, name='spell', out_shape=tuple((plain_shape(*...  6.26 us

profile of v8, /device:TPU:1, one launch (start us, length us, event | category | flops | bytes accessed | tf_op | source)
XLA Modules:
  0.0 195.8 jit_solution(4619363385096249238)
XLA Ops:
  0.7 0.0 copy-start
  0.7 62.0 %front.1 = (bf16[4,192,128]{2,1,0:T(8,128)(2,1)S(1)}, bf16[4,192,128]{2,1,0:T(8,128)(2,1)S(1)}, bf16[4,4,2,128,384]{4,3,2,1,0:T(8,128)(2,1)S(1)}, f32[3,64,512]{...) custom-call(bf16[128,768]{1,0:T(8,128)(2,1)} %bitcast.5, ...), custom_call_target="tpu_custom_call" | custom-call | bytes 210000000 | tf_op jit(solution)/shard_map/front/pallas_call | solution.py:544
  62.7 0.0 copy-done
  62.7 126.6 %rest.1 = (bf16[128,768]{1,0:T(8,128)(2,1)S(1)}, f32[128,768]{1,0:T(8,128)S(1)}, bf16[2,3,4,4,2,48,384]{6,5,4,3,2,1,0:T(8,128)(2,1)S(1)}, f32[16,384]{1,0:T(8,128)S(1)}) custom-call(bf16[128,768]{1,0:T(8,128)(2,1)S(1)} %get-tuple-element.51.x, bf16[128,768]{1,0:T(8,128)(2,1)S(1)} %bitcast.4, bf16[4,192,128]{2,1,0:T(8,128)(2,1)S(1)} %get-tuple-element.52.mixed, ...), custom_call_target="tpu_custom_call" | custom-call | bytes 390000000 | tf_op jit(solution)/shard_map/rest/pallas_call | solution.py:1163
  189.3 6.3 %spell.1 = (f32[384,768]{1,0:T(8,128)}, f32[384,768]{1,0:T(8,128)}, f32[384,768]{1,0:T(8,128)}, f32[384,768]{1,0:T(8,128)}, f32[384,3072]{1,0:T(8,128)}, /*index...) custom-call(bf16[2,3,4,4,2,48,384]{6,5,4,3,2,1,0:T(8,128)(2,1)S(1)} , ...), custom_call_target="tpu_custom_call" | custom-call | bytes 18000000 | tf_op jit(solution)/shard_map/spell/pallas_call | solution.py:1233
Async XLA Ops:
  0.7 62.0 %copy-start = (bf16[1,128,768]{2,1,0:T(8,128)(2,1)S(1)}, bf16[1,128,768]{2,1,0:T(8,128)(2,1)}, u32[]{:S(2)}) copy-start(bf16[1,128,768]{2,1,0:T(8,128)(2,1)} %param.18) | copy-start | bytes 589828
